TPU v7x, 32 devices: a whole 2x2x4 slice. The times are simulated.
32 devices in a mesh: dp: 2 (over core), shard: 16 (over z, y, x).
Axes of the slice: x: 2, y: 2, z: 4, core: 2. Of those that a mesh axis runs over, the one named last changes fastest.
Arguments:
- hidden_in: bfloat16 [4096, 1024], P(('dp', 'shard')), may hold values from -6 to 6
- doc_ids: int32 [32, 128], P(('dp', 'shard')), may hold values from 0 to 3, never falling along the last dimension, each value on 1 to 64 neighbouring positions
- expert_ids: int32 [4096], P(('dp', 'shard')), may hold values from 0 to 1, as said below
- slot_ids: int32 [4096], P(('dp', 'shard')), may hold values from 0 to 73, as said below
- out_grad: bfloat16 [4096, 1024], P(('dp', 'shard')), may hold values from -6 to 6
- ln1_gain: bfloat16 [1024], P(('dp', 'shard')), may hold values from 0.5 to 1.5
- ln1_bias: bfloat16 [1024], P(('dp', 'shard')), may hold values from -1 to 1
- w_query: bfloat16 [1024, 1024], P(('dp', 'shard')), may hold values from -0.1875 to 0.1875
- w_key: bfloat16 [1024, 1024], P(('dp', 'shard')), may hold values from -0.1875 to 0.1875
- w_value: bfloat16 [1024, 1024], P(('dp', 'shard')), may hold values from -0.1875 to 0.1875
- w_out: bfloat16 [1024, 1024], P(('dp', 'shard')), may hold values from -0.5 to 0.5
- ln2_gain: bfloat16 [1024], P(('dp', 'shard')), may hold values from 0.5 to 1.5
- ln2_bias: bfloat16 [1024], P(('dp', 'shard')), may hold values from -1 to 1
- w_up: bfloat16 [1024, 4096], P(('dp', 'shard')), may hold values from -0.1875 to 0.1875
- w_down: bfloat16 [4096, 1024], P(('dp', 'shard')), may hold values from -0.09375 to 0.09375
- w_router: bfloat16 [1024, 2], P(('dp', 'shard')), may hold values from -0.125 to 0.125
- w_mix: bfloat16 [1024, 2], P(('dp', 'shard')), may hold values from -0.1875 to 0.1875
- expert_up: bfloat16 [2, 1024, 4096], P(None, ('dp', 'shard')), may hold values from -0.1875 to 0.1875
- expert_down: bfloat16 [2, 4096, 1024], P(None, ('dp', 'shard')), may hold values from -0.09375 to 0.09375
- load_avg: float32 [2], replicated, may hold values from 0.05 to 0.3
Outputs:
- layer_out: bfloat16 [4096, 1024], P(('dp', 'shard'))
- input_grad: bfloat16 [4096, 1024], P(('dp', 'shard'))
- grad_ln1_gain: float32 [1024], P(('dp', 'shard'))
- grad_ln1_bias: float32 [1024], P(('dp', 'shard'))
- grad_w_query: float32 [1024, 1024], P(('dp', 'shard'))
- grad_w_key: float32 [1024, 1024], P(('dp', 'shard'))
- grad_w_value: float32 [1024, 1024], P(('dp', 'shard'))
- grad_w_out: float32 [1024, 1024], P(('dp', 'shard'))
- grad_ln2_gain: float32 [1024], P(('dp', 'shard'))
- grad_ln2_bias: float32 [1024], P(('dp', 'shard'))
- grad_w_up: float32 [1024, 4096], P(('dp', 'shard'))
- grad_w_down: float32 [4096, 1024], P(('dp', 'shard'))
- grad_w_router: float32 [1024, 2], P(('dp', 'shard'))
- grad_w_mix: float32 [1024, 2], P(('dp', 'shard'))
- grad_expert_up: float32 [2, 1024, 4096], P(None, ('dp', 'shard'))
- grad_expert_down: float32 [2, 4096, 1024], P(None, ('dp', 'shard'))
- expert_counts: int32 [2], replicated
- load_avg_new: float32 [2], replicated
Inputs may be any that keep to these rules, and one draw needn't show every extreme that they name: `expert_ids`: of the 128 tokens of one sequence at most 74 go to one expert, and in some sequence exactly 74 do. `slot_ids`: A token's slot is the number of earlier tokens of the same sequence routed to the same expert.
All inputs are finite; a program needn't handle non-finite values.
Results may differ from a plain program's by a relative error of at most 0.012.
The roundings to bfloat16 on the way count: a program that leaves them out, or rounds other values in their place, can miss the bound.
Values may be sent and summed in bfloat16 or wider, within the bound.
A program may use at most 384 MiB of HBM per device.

v0:
```python
import jax
import jax.numpy as jnp
from jax import lax
from jax.sharding import PartitionSpec as P

HEADS = 16
CAP = 74


def layer_norm(values, gain, bias):
    centre = values - jnp.mean(values, axis=-1, keepdims=True)
    scale_inv = lax.rsqrt(jnp.mean(centre * centre, axis=-1, keepdims=True) + 1e-05)
    normed = centre * scale_inv
    return (normed * gain + bias, normed, scale_inv)


def norm_back(grad_out, normed, scale_inv, gain):
    grad_normed = grad_out * gain
    inner = grad_normed - jnp.mean(grad_normed, axis=-1, keepdims=True)
    inner = inner - normed * jnp.mean(grad_normed * normed, axis=-1, keepdims=True)
    return (scale_inv * inner, jnp.sum(grad_out * normed, axis=0), jnp.sum(grad_out, axis=0))


def gelu_fn(values):
    return jax.nn.gelu(values, approximate=True)


def gelu_back(values, grad_out):
    return jax.vjp(gelu_fn, values)[1](grad_out)[0]


def masked_scores(query, keys, allowed):
    scores = jnp.einsum("ihd,jhd->hij", query, keys, preferred_element_type=jnp.float32)
    return jnp.where(allowed[None], scores, -1e30)


def body(
    hidden_in,
    doc_ids,
    expert_ids,
    slot_ids,
    out_grad,
    ln1_gain,
    ln1_bias,
    w_query,
    w_key,
    w_value,
    w_out,
    ln2_gain,
    ln2_bias,
    w_up,
    w_down,
    w_router,
    w_mix,
    expert_up,
    expert_down,
    load_avg,
):
    row_count, model_width = hidden_in.shape
    head_count = HEADS
    head_size = model_width // head_count
    expert_count = expert_up.shape[0]
    highest = lax.Precision.HIGHEST
    attn_first = (
        lax.all_gather(ln1_gain, ("dp", "shard"), axis=0, tiled=True),
        lax.all_gather(ln1_bias, ("dp", "shard"), axis=0, tiled=True),
        lax.all_gather(w_query, ("dp", "shard"), axis=0, tiled=True),
        lax.all_gather(w_key, ("dp", "shard"), axis=0, tiled=True),
        lax.all_gather(w_value, ("dp", "shard"), axis=0, tiled=True),
        lax.all_gather(w_out, ("dp", "shard"), axis=0, tiled=True),
    )
    gain_one = attn_first[0].astype(jnp.float32)
    bias_one = attn_first[1].astype(jnp.float32)
    wq_full, wk_full, wv_full, wo_full = (
        attn_first[2],
        attn_first[3],
        attn_first[4],
        attn_first[5],
    )
    base_in = hidden_in.astype(jnp.float32)
    normed_in, unit_one, inv_one = layer_norm(base_in, gain_one, bias_one)
    low_one = normed_in.astype(jnp.bfloat16)
    query = (jnp.dot(low_one, wq_full, preferred_element_type=jnp.float32) * 0.125).astype(
        jnp.bfloat16
    )
    keys = jnp.dot(low_one, wk_full, preferred_element_type=jnp.float32).astype(jnp.bfloat16)
    values = jnp.dot(low_one, wv_full, preferred_element_type=jnp.float32).astype(jnp.bfloat16)
    query = query.reshape(row_count, head_count, head_size)
    keys = keys.reshape(row_count, head_count, head_size)
    values = values.reshape(row_count, head_count, head_size)
    places = lax.iota(jnp.int32, row_count)
    doc_row = doc_ids[0]
    allowed = (places[None, :] <= places[:, None]) & (doc_row[:, None] == doc_row[None, :])
    scores = masked_scores(query, keys, allowed)
    row_max = jnp.max(scores, axis=-1, keepdims=True)
    expo = jnp.exp(scores - row_max)
    row_total = jnp.sum(expo, axis=-1, keepdims=True)
    log_total = row_max + jnp.log(row_total)
    probs_low = (expo / row_total).astype(jnp.bfloat16)
    attended = jnp.einsum("hij,jhd->ihd", probs_low, values, preferred_element_type=jnp.float32)
    attended = attended.reshape(row_count, model_width).astype(jnp.bfloat16)
    branch = jnp.dot(attended, wo_full, preferred_element_type=jnp.float32)
    resid = base_in + branch
    local_counts = jnp.sum(
        (expert_ids[:, None] == lax.iota(jnp.int32, expert_count)[None, :]).astype(jnp.int32),
        axis=0,
    )
    counts_total = lax.psum(local_counts, ("dp", "shard"))
    ffn_first = (
        lax.all_gather(ln2_gain, ("dp", "shard"), axis=0, tiled=True),
        lax.all_gather(ln2_bias, ("dp", "shard"), axis=0, tiled=True),
        lax.all_gather(w_up, ("dp", "shard"), axis=0, tiled=True),
        lax.all_gather(w_down, ("dp", "shard"), axis=0, tiled=True),
        lax.all_gather(w_router, ("dp", "shard"), axis=0, tiled=True),
        lax.all_gather(w_mix, ("dp", "shard"), axis=0, tiled=True),
        lax.all_gather(expert_up, ("dp", "shard"), axis=1, tiled=True),
        lax.all_gather(expert_down, ("dp", "shard"), axis=1, tiled=True),
    )
    gain_two = ffn_first[0].astype(jnp.float32)
    bias_two = ffn_first[1].astype(jnp.float32)
    wu_full, wd_full = (ffn_first[2], ffn_first[3])
    wr_full = ffn_first[4].astype(jnp.float32)
    wm_full = ffn_first[5].astype(jnp.float32)
    eu_full, ed_full = (ffn_first[6], ffn_first[7])
    normed_two, unit_two, inv_two = layer_norm(resid, gain_two, bias_two)
    low_two = normed_two.astype(jnp.bfloat16)
    up_pre = jnp.dot(low_two, wu_full, preferred_element_type=jnp.float32)
    up_low = gelu_fn(up_pre).astype(jnp.bfloat16)
    dense_out = jnp.dot(up_low, wd_full, preferred_element_type=jnp.float32)
    router_probs = jax.nn.softmax(jnp.dot(normed_two, wr_full, precision=highest), axis=-1)
    onehot = (expert_ids[:, None] == lax.iota(jnp.int32, expert_count)[None, :]).astype(jnp.float32)
    gate_prob = jnp.sum(router_probs * onehot, axis=-1)
    mix_coef = jax.nn.softmax(jnp.dot(normed_two, wm_full, precision=highest), axis=-1)
    flat_slot = expert_ids * CAP + slot_ids
    token_of = jnp.zeros((expert_count * CAP,), jnp.int32).at[flat_slot].set(places)
    filled = jnp.zeros((expert_count * CAP,), jnp.bfloat16).at[flat_slot].set(1.0)
    packed = (low_two[token_of] * filled[:, None]).reshape(expert_count, CAP, model_width)
    expert_pre = jnp.einsum("ecd,edf->ecf", packed, eu_full, preferred_element_type=jnp.float32)
    expert_low = gelu_fn(expert_pre).astype(jnp.bfloat16)
    expert_res = jnp.einsum("ecf,efd->ecd", expert_low, ed_full, preferred_element_type=jnp.float32)
    expert_res = expert_res.reshape(expert_count * CAP, model_width)
    token_res = expert_res[flat_slot]
    routed = token_res * gate_prob[:, None]
    layer_out = (resid + mix_coef[:, 0:1] * routed + mix_coef[:, 1:2] * dense_out).astype(
        jnp.bfloat16
    )
    grad_top = out_grad.astype(jnp.float32)
    ffn_late = (
        lax.all_gather(ln2_gain, ("dp", "shard"), axis=0, tiled=True),
        lax.all_gather(ln2_bias, ("dp", "shard"), axis=0, tiled=True),
        lax.all_gather(w_up, ("dp", "shard"), axis=0, tiled=True),
        lax.all_gather(w_down, ("dp", "shard"), axis=0, tiled=True),
        lax.all_gather(w_router, ("dp", "shard"), axis=0, tiled=True),
        lax.all_gather(w_mix, ("dp", "shard"), axis=0, tiled=True),
        lax.all_gather(expert_up, ("dp", "shard"), axis=1, tiled=True),
        lax.all_gather(expert_down, ("dp", "shard"), axis=1, tiled=True),
    )
    gain_two_b = ffn_late[0].astype(jnp.float32)
    wu_back, wd_back = (ffn_late[2], ffn_late[3])
    wr_back = ffn_late[4].astype(jnp.float32)
    wm_back = ffn_late[5].astype(jnp.float32)
    eu_back, ed_back = (ffn_late[6], ffn_late[7])
    grad_routed = grad_top * mix_coef[:, 0:1]
    grad_dense = grad_top * mix_coef[:, 1:2]
    grad_coef = jnp.stack(
        [jnp.sum(grad_top * routed, axis=-1), jnp.sum(grad_top * dense_out, axis=-1)], axis=-1
    )
    grad_mixl = mix_coef * (grad_coef - jnp.sum(mix_coef * grad_coef, axis=-1, keepdims=True))
    grad_gate = jnp.sum(grad_routed * token_res, axis=-1)
    grad_token_res = grad_routed * gate_prob[:, None]
    grad_probs = onehot * grad_gate[:, None]
    grad_logits = router_probs * (
        grad_probs - jnp.sum(router_probs * grad_probs, axis=-1, keepdims=True)
    )
    grad_eres = (grad_token_res[token_of] * filled.astype(jnp.float32)[:, None]).astype(
        jnp.bfloat16
    )
    grad_eres = grad_eres.reshape(expert_count, CAP, model_width)
    grad_ed_lead = jnp.einsum(
        "ecf,ecd->fed", expert_low, grad_eres, preferred_element_type=jnp.float32
    )
    grad_elow = jnp.einsum("ecd,efd->ecf", grad_eres, ed_back, preferred_element_type=jnp.float32)
    grad_epre = gelu_back(expert_pre, grad_elow).astype(jnp.bfloat16)
    grad_eu_lead = jnp.einsum("ecd,ecf->def", packed, grad_epre, preferred_element_type=jnp.float32)
    grad_packed = jnp.einsum("ecf,edf->ecd", grad_epre, eu_back, preferred_element_type=jnp.float32)
    grad_packed = grad_packed.reshape(expert_count * CAP, model_width)
    grad_dense_low = grad_dense.astype(jnp.bfloat16)
    grad_wd = jnp.dot(up_low.T, grad_dense_low, preferred_element_type=jnp.float32)
    grad_uplow = jnp.dot(grad_dense_low, wd_back.T, preferred_element_type=jnp.float32)
    grad_uppre = gelu_back(up_pre, grad_uplow).astype(jnp.bfloat16)
    grad_wu = jnp.dot(low_two.T, grad_uppre, preferred_element_type=jnp.float32)
    grad_norm_two = jnp.dot(grad_uppre, wu_back.T, preferred_element_type=jnp.float32)
    grad_norm_two = grad_norm_two + grad_packed[flat_slot]
    grad_norm_two = grad_norm_two + jnp.dot(grad_logits, wr_back.T, precision=highest)
    grad_norm_two = grad_norm_two + jnp.dot(grad_mixl, wm_back.T, precision=highest)
    grad_wr = jnp.dot(normed_two.T, grad_logits, precision=highest)
    grad_wm = jnp.dot(normed_two.T, grad_mixl, precision=highest)
    grad_resid_norm, grad_gain_two, grad_bias_two = norm_back(
        grad_norm_two, unit_two, inv_two, gain_two_b
    )
    grad_resid = grad_top + grad_resid_norm
    attn_late = (
        lax.all_gather(ln1_gain, ("dp", "shard"), axis=0, tiled=True),
        lax.all_gather(ln1_bias, ("dp", "shard"), axis=0, tiled=True),
        lax.all_gather(w_query, ("dp", "shard"), axis=0, tiled=True),
        lax.all_gather(w_key, ("dp", "shard"), axis=0, tiled=True),
        lax.all_gather(w_value, ("dp", "shard"), axis=0, tiled=True),
        lax.all_gather(w_out, ("dp", "shard"), axis=0, tiled=True),
    )
    gain_one_b = attn_late[0].astype(jnp.float32)
    wq_back, wk_back, wv_back, wo_back = (attn_late[2], attn_late[3], attn_late[4], attn_late[5])
    grad_branch = grad_resid.astype(jnp.bfloat16)
    grad_wo = jnp.dot(attended.T, grad_branch, preferred_element_type=jnp.float32)
    grad_att = jnp.dot(grad_branch, wo_back.T, preferred_element_type=jnp.float32).astype(
        jnp.bfloat16
    )
    grad_att = grad_att.reshape(row_count, head_count, head_size)
    scores_again = masked_scores(query, keys, allowed)
    probs_again = jnp.exp(scores_again - log_total)
    probs_again_low = probs_again.astype(jnp.bfloat16)
    grad_probs_att = jnp.einsum(
        "ihd,jhd->hij", grad_att, values, preferred_element_type=jnp.float32
    )
    row_inner = jnp.sum(probs_again * grad_probs_att, axis=-1, keepdims=True)
    grad_scores = (probs_again * (grad_probs_att - row_inner)).astype(jnp.bfloat16)
    grad_query = jnp.einsum(
        "hij,jhd->ihd", grad_scores, keys, preferred_element_type=jnp.float32
    ).astype(jnp.bfloat16)
    grad_query = (grad_query * jnp.bfloat16(0.125)).reshape(row_count, model_width)
    grad_keys = jnp.einsum("hij,ihd->jhd", grad_scores, query, preferred_element_type=jnp.float32)
    grad_keys = grad_keys.astype(jnp.bfloat16).reshape(row_count, model_width)
    grad_values = jnp.einsum(
        "hij,ihd->jhd", probs_again_low, grad_att, preferred_element_type=jnp.float32
    )
    grad_values = grad_values.astype(jnp.bfloat16).reshape(row_count, model_width)
    grad_wq = jnp.dot(low_one.T, grad_query, preferred_element_type=jnp.float32)
    grad_wk = jnp.dot(low_one.T, grad_keys, preferred_element_type=jnp.float32)
    grad_wv = jnp.dot(low_one.T, grad_values, preferred_element_type=jnp.float32)
    grad_norm_one = jnp.dot(grad_query, wq_back.T, preferred_element_type=jnp.float32)
    grad_norm_one = grad_norm_one + jnp.dot(
        grad_keys, wk_back.T, preferred_element_type=jnp.float32
    )
    grad_norm_one = grad_norm_one + jnp.dot(
        grad_values, wv_back.T, preferred_element_type=jnp.float32
    )
    grad_in_norm, grad_gain_one, grad_bias_one = norm_back(
        grad_norm_one, unit_one, inv_one, gain_one_b
    )
    input_grad = (grad_resid + grad_in_norm).astype(jnp.bfloat16)
    owned_all = (
        lax.psum_scatter(grad_gain_one, ("dp", "shard"), scatter_dimension=0, tiled=True),
        lax.psum_scatter(grad_bias_one, ("dp", "shard"), scatter_dimension=0, tiled=True),
        lax.psum_scatter(grad_wq, ("dp", "shard"), scatter_dimension=0, tiled=True),
        lax.psum_scatter(grad_wk, ("dp", "shard"), scatter_dimension=0, tiled=True),
        lax.psum_scatter(grad_wv, ("dp", "shard"), scatter_dimension=0, tiled=True),
        lax.psum_scatter(grad_wo, ("dp", "shard"), scatter_dimension=0, tiled=True),
        lax.psum_scatter(grad_gain_two, ("dp", "shard"), scatter_dimension=0, tiled=True),
        lax.psum_scatter(grad_bias_two, ("dp", "shard"), scatter_dimension=0, tiled=True),
        lax.psum_scatter(grad_wu, ("dp", "shard"), scatter_dimension=0, tiled=True),
        lax.psum_scatter(grad_wd, ("dp", "shard"), scatter_dimension=0, tiled=True),
        lax.psum_scatter(grad_wr, ("dp", "shard"), scatter_dimension=0, tiled=True),
        lax.psum_scatter(grad_wm, ("dp", "shard"), scatter_dimension=0, tiled=True),
        lax.psum_scatter(grad_eu_lead, ("dp", "shard"), scatter_dimension=0, tiled=True),
        lax.psum_scatter(grad_ed_lead, ("dp", "shard"), scatter_dimension=0, tiled=True),
    )
    attn_owned = owned_all[0:6]
    ffn_owned = owned_all[6:14]
    owned_eu = jnp.transpose(ffn_owned[6], (1, 0, 2))
    owned_ed = jnp.transpose(ffn_owned[7], (1, 0, 2))
    total_tokens = row_count * lax.axis_size(("dp", "shard"))
    load_new = 0.9 * load_avg + 0.1 * counts_total.astype(jnp.float32) * expert_count / total_tokens
    return (
        layer_out,
        input_grad,
        attn_owned[0],
        attn_owned[1],
        attn_owned[2],
        attn_owned[3],
        attn_owned[4],
        attn_owned[5],
        ffn_owned[0],
        ffn_owned[1],
        ffn_owned[2],
        ffn_owned[3],
        ffn_owned[4],
        ffn_owned[5],
        owned_eu,
        owned_ed,
        counts_total,
        load_new,
    )


def solution(mesh):
    placed = (
        P(("dp", "shard"), None),
        P(("dp", "shard"), None),
        P(("dp", "shard")),
        P(("dp", "shard")),
        P(("dp", "shard"), None),
        P(("dp", "shard")),
        P(("dp", "shard")),
        P(("dp", "shard"), None),
        P(("dp", "shard"), None),
        P(("dp", "shard"), None),
        P(("dp", "shard"), None),
        P(("dp", "shard")),
        P(("dp", "shard")),
        P(("dp", "shard"), None),
        P(("dp", "shard"), None),
        P(("dp", "shard"), None),
        P(("dp", "shard"), None),
        P(None, ("dp", "shard"), None),
        P(None, ("dp", "shard"), None),
        P(),
    )
    return jax.shard_map(
        body,
        mesh=mesh,
        in_specs=placed,
        out_specs=(
            P(("dp", "shard"), None),
            P(("dp", "shard"), None),
            P(("dp", "shard")),
            P(("dp", "shard")),
            P(("dp", "shard"), None),
            P(("dp", "shard"), None),
            P(("dp", "shard"), None),
            P(("dp", "shard"), None),
            P(("dp", "shard")),
            P(("dp", "shard")),
            P(("dp", "shard"), None),
            P(("dp", "shard"), None),
            P(("dp", "shard"), None),
            P(("dp", "shard"), None),
            P(None, ("dp", "shard"), None),
            P(None, ("dp", "shard"), None),
            P(),
            P(),
        ),
        check_vma=False,
    )
```

profile of v0, /device:TPU:0, one launch (start us, length us, event | category | flops | bytes accessed | tf_op | source)
XLA Modules:
  0.0 3450.7 jit_solution(6429598345189964262)
XLA Ops:
  18.2 42.3 %all-reduce.10 = (bf16[1024]{0:T(1024)(128)(2,1)S(1)}, bf16[1024]{0:T(1024)(128)(2,1)S(1)}, bf16[1024]{0:T(1024)(128)(2,1)S(1)}, bf16[1024]{0:T(1024)(128)(2,1)S(1)}) all-reduce(bf16[1024]{0:T(1024)(128)(2,1)S(1)} %dynamic-update-slice.3, bf16[1024]{0:T(1024)(128)(2,1)S(1)} %dynamic-update-slice.2, ...), channel_id=1, replica_groups=mesh['dp'=2,'shard'=16] {'dp','shard'}, use_global_device_ids=true, to_apply=%add.3 | all-reduce | flops 4096 | bytes 16384
  60.5 65.7 %all-gather.1 = bf16[32,32,2]{1,2,0:T(2,128)(2,1)S(1)} all-gather(bf16[1,32,2]{1,2,0:T(2,128)(2,1)} %bitcast.108), channel_id=1, replica_groups=mesh['dp'=2,'shard'=16] {'dp','shard'}, dimensions={0}, use_global_device_ids=true | all-gather | bytes 4224 | tf_op jit(solution)/shard_map/all_gather | solution.py:114
  126.4 63.2 %all-gather = bf16[32,32,2]{1,2,0:T(2,128)(2,1)S(1)} all-gather(bf16[1,32,2]{1,2,0:T(2,128)(2,1)} %bitcast.109), channel_id=1, replica_groups=mesh['dp'=2,'shard'=16] {'dp','shard'}, dimensions={0}, use_global_device_ids=true | all-gather | bytes 4224 | tf_op jit(solution)/shard_map/all_gather | solution.py:115
  202.3 42.5 %all-gather.17.cloned.1.call-done = bf16[1024,1024]{1,0:T(8,128)(2,1)} async-done(((bf16[32,1024]{1,0:T(8,128)(2,1)}), bf16[1024,1024]{1,0:T(8,128)(2,1)}) %all-gather.17.cloned.1.call-update) | async-done | bytes 2097168 | tf_op jit(solution)/shard_map/all_gather | solution.py:70
  249.5 74.5 %all-gather.23.cloned.1.call-done = bf16[1024,4096]{1,0:T(8,128)(2,1)} async-done(((bf16[32,4096]{1,0:T(8,128)(2,1)}), bf16[1024,4096]{1,0:T(8,128)(2,1)}) %all-gather.23.cloned.1.call-update) | async-done | bytes 8388624 | tf_op jit(solution)/shard_map/all_gather | solution.py:112
  330.0 110.2 %all-gather.19.cloned.1.call-done = bf16[2,1024,4096]{2,1,0:T(8,128)(2,1)} async-done(((bf16[2,32,4096]{2,1,0:T(8,128)(2,1)}), bf16[2,1024,4096]{2,1,0:T(8,128)(2,1)}) %all-gather.19.cloned.1.call-update) | async-done | bytes 16777232 | tf_op jit(solution)/shard_map/all_gather | solution.py:116
  450.5 105.5 %all-gather.21.cloned.1.call-done = bf16[2,4096,1024]{2,1,0:T(8,128)(2,1)} async-done(((bf16[2,128,1024]{2,1,0:T(8,128)(2,1)}), bf16[2,4096,1024]{2,1,0:T(8,128)(2,1)}) %all-gather.21.cloned.1.call-update) | async-done | bytes 16777232 | tf_op jit(solution)/shard_map/all_gather | solution.py:117
  569.6 65.0 %all-gather.25.cloned.1.call-done = bf16[4096,1024]{1,0:T(8,128)(2,1)} async-done(((bf16[128,1024]{1,0:T(8,128)(2,1)}), bf16[4096,1024]{1,0:T(8,128)(2,1)}) %all-gather.25.cloned.1.call-update) | async-done | bytes 8388624 | tf_op jit(solution)/shard_map/all_gather | solution.py:113
  649.0 13.5 fusion.6
  662.5 14.6 convolution_bitcast_fusion.1
  677.1 49.4 %copy.74 = f32[1024,2,4096]{2,1,0:T(2,128)} copy(f32[1024,2,4096]{0,2,1:T(8,128)} %convolution_bitcast_fusion.1) | data formatting | bytes 67108864 | tf_op jit(solution)/shard_map/ecd,ecf->def/transpose | solution.py:184
  727.6 15.0 convolution_bitcast_fusion
  752.1 11.4 fusion.91
  811.0 39.2 %psum.7 = s32[2]{0:T(128)S(1)} all-reduce(s32[2]{0:T(128)S(1)} %convert_reduce_fusion.1), channel_id=1, replica_groups=mesh['dp'=2,'shard'=16] {'dp','shard'}, use_global_device_ids=true, to_apply=%region_42.43 | all-reduce | flops 2 | bytes 16 | tf_op jit(solution)/shard_map/psum | solution.py:108
  855.3 40.3 %all-reduce.9 = (f32[1024]{0:T(1024)S(1)}, f32[1024]{0:T(1024)S(1)}, f32[1024]{0:T(1024)S(1)}, f32[1024]{0:T(1024)S(1)}) all-reduce(f32[1024]{0:T(1024)S(1)} %get-tuple-element.74, f32[1024]{0:T(1024)S(1)} %get-tuple-element.81, f32[1024]{0:T(1024)S(1)} %get-tuple-element.72, ...), channel_id=2, replica_groups=mesh['dp'=2,'shard'=16] {'dp','shard'}, use_global_device_ids=true, to_apply=%region_24.25.clone | all-reduce | flops 4096 | bytes 32768
  900.3 16.0 reduce-scatter.30.cloned.1.call-done
  917.7 500.6 %all-reduce.13.cloned.1.call-done = f32[1024,2,4096]{2,1,0:T(2,128)} async-done(((f32[1024,2,4096]{2,1,0:T(2,128)}), f32[1024,2,4096]{2,1,0:T(2,128)}) %all-reduce.13.cloned.1.call-update) | async-done | bytes 33554448
  1421.1 704.9 %reduce-scatter.26.cloned.1.call-done = f32[128,2,1024]{0,2,1:T(8,128)} async-done(((f32[4096,2,1024]{0,2,1:T(8,128)}), f32[128,2,1024]{0,2,1:T(8,128)}) %reduce-scatter.26.cloned.1.call-update) | async-done | bytes 1048592 | tf_op jit(solution)/shard_map/reduce_scatter | solution.py:264
  2128.6 151.0 %reduce-scatter.20.cloned.1.call-done = f32[32,1024]{1,0:T(8,128)} async-done(((f32[1024,1024]{1,0:T(8,128)}), f32[32,1024]{1,0:T(8,128)}) %reduce-scatter.20.cloned.1.call-update) | async-done | bytes 131088 | tf_op jit(solution)/shard_map/reduce_scatter | solution.py:256
  2279.6 147.1 %reduce-scatter.18.cloned.1.call-done = f32[32,1024]{1,0:T(8,128)} async-done(((f32[1024,1024]{1,0:T(8,128)}), f32[32,1024]{1,0:T(8,128)}) %reduce-scatter.18.cloned.1.call-update) | async-done | bytes 131088 | tf_op jit(solution)/shard_map/reduce_scatter | solution.py:255
  2426.7 147.7 %reduce-scatter.16.cloned.1.call-done = f32[32,1024]{1,0:T(8,128)} async-done(((f32[1024,1024]{1,0:T(8,128)}), f32[32,1024]{1,0:T(8,128)}) %reduce-scatter.16.cloned.1.call-update) | async-done | bytes 131088 | tf_op jit(solution)/shard_map/reduce_scatter | solution.py:254
  2574.5 147.7 %reduce-scatter.14.cloned.1.call-done = f32[32,1024]{1,0:T(8,128)} async-done(((f32[1024,1024]{1,0:T(8,128)}), f32[32,1024]{1,0:T(8,128)}) %reduce-scatter.14.cloned.1.call-update) | async-done | bytes 131088 | tf_op jit(solution)/shard_map/reduce_scatter | solution.py:253
  2722.2 358.6 %reduce-scatter.24.cloned.1.call-done = f32[128,1024]{1,0:T(8,128)} async-done(((f32[4096,1024]{1,0:T(8,128)}), f32[128,1024]{1,0:T(8,128)}) %reduce-scatter.24.cloned.1.call-update) | async-done | bytes 524304 | tf_op jit(solution)/shard_map/reduce_scatter | solution.py:260
  3080.8 362.9 %reduce-scatter.22.cloned.1.call-done = f32[32,4096]{1,0:T(8,128)} async-done(((f32[1024,4096]{1,0:T(8,128)}), f32[32,4096]{1,0:T(8,128)}) %reduce-scatter.22.cloned.1.call-update) | async-done | bytes 524304 | tf_op jit(solution)/shard_map/reduce_scatter | solution.py:259
  (193 shorter events, 146.4 us)
Async XLA Ops:
  7.2 187.0 %copy-start = (bf16[128,1024]{1,0:T(8,128)(2,1)S(1)}, bf16[128,1024]{1,0:T(8,128)(2,1)}, u32[]{:S(2)}) copy-start(bf16[128,1024]{1,0:T(8,128)(2,1)} %param.20) | copy-start | bytes 786436
  7.2 187.0 %all-gather.13.cloned.1.call-start = ((), (), s32[]{:S(2)}) async-start(), calls=%async_computation.10 | async-start | bytes 2162688 | tf_op jit(solution)/shard_map/all_gather | solution.py:67
  7.9 188.6 %all-gather.15.cloned.1.call-start = ((), (), s32[]{:S(2)}) async-start(), calls=%async_computation.11 | async-start | bytes 2162688 | tf_op jit(solution)/shard_map/all_gather | solution.py:68
  8.7 190.3 %all-gather.11.cloned.1.call-start = ((), (), s32[]{:S(2)}) async-start(), calls=%async_computation.9 | async-start | bytes 2162688 | tf_op jit(solution)/shard_map/all_gather | solution.py:69
  9.4 235.4 %all-gather.17.cloned.1.call-start = ((), (), s32[]{:S(2)}) async-start(), calls=%async_computation.12 | async-start | bytes 2162688 | tf_op jit(solution)/shard_map/all_gather | solution.py:70
  10.0 314.0 %all-gather.23.cloned.1.call-start = ((), (), s32[]{:S(2)}) async-start(), calls=%async_computation.15 | async-start | bytes 8650752 | tf_op jit(solution)/shard_map/all_gather | solution.py:112
  10.6 429.6 %all-gather.19.cloned.1.call-start = ((), (), s32[]{:S(2)}) async-start(), calls=%async_computation.13 | async-start | bytes 17301504 | tf_op jit(solution)/shard_map/all_gather | solution.py:116
  11.2 544.9 %all-gather.21.cloned.1.call-start = ((), (), s32[]{:S(2)}) async-start(), calls=%async_computation.14 | async-start | bytes 17301504 | tf_op jit(solution)/shard_map/all_gather | solution.py:117
  11.9 622.8 %all-gather.25.cloned.1.call-start = ((), (), s32[]{:S(2)}) async-start(), calls=%async_computation.16 | async-start | bytes 8650752 | tf_op jit(solution)/shard_map/all_gather | solution.py:113
  12.7 886.3 %reduce-scatter.28.cloned.1.call-start = ((), (), s32[]{:S(2)}) async-start(), calls=%async_computation.24 | async-start | bytes 540672
  202.3 44.9 %copy-start.19 = (bf16[16,64,128]{2,1,0:T(8,128)(2,1)}, bf16[16,64,128]{2,1,0:T(8,128)(2,1)S(1)}, u32[]{:S(2)}) copy-start(bf16[16,64,128]{2,1,0:T(8,128)(2,1)S(1)} %convolution_convert_fusion.4) | copy-start | bytes 786436
  568.0 66.6 %copy-start.14 = (bf16[128,1024]{1,0:T(8,128)(2,1)S(1)}, bf16[128,1024]{1,0:T(8,128)(2,1)}, u32[]{:S(2)}) copy-start(bf16[128,1024]{1,0:T(8,128)(2,1)} %param.24) | copy-start | bytes 786436
  643.3 273.0 %reduce-scatter.30.cloned.1.call-start = ((), (), s32[]{:S(2)}) async-start(), calls=%async_computation.25 | async-start | bytes 540672
  648.9 769.3 %all-reduce.13.cloned.1.call-start = ((), (), s32[]{:S(2)}) async-start(), calls=%async_computation.26 | async-start | bytes 67108864
  726.5 1399.5 %reduce-scatter.26.cloned.1.call-start = ((), (), s32[]{:S(2)}) async-start(), calls=%async_computation.23 | async-start | bytes 34603008 | tf_op jit(solution)/shard_map/reduce_scatter | solution.py:264
  742.7 1536.9 %reduce-scatter.20.cloned.1.call-start = ((), (), s32[]{:S(2)}) async-start(), calls=%async_computation.20 | async-start | bytes 4325376 | tf_op jit(solution)/shard_map/reduce_scatter | solution.py:256
  775.2 1651.6 %reduce-scatter.18.cloned.1.call-start = ((), (), s32[]{:S(2)}) async-start(), calls=%async_computation.19 | async-start | bytes 4325376 | tf_op jit(solution)/shard_map/reduce_scatter | solution.py:255
  781.3 1793.1 %reduce-scatter.16.cloned.1.call-start = ((), (), s32[]{:S(2)}) async-start(), calls=%async_computation.18 | async-start | bytes 4325376 | tf_op jit(solution)/shard_map/reduce_scatter | solution.py:254
  786.2 1936.0 %reduce-scatter.14.cloned.1.call-start = ((), (), s32[]{:S(2)}) async-start(), calls=%async_computation.17 | async-start | bytes 4325376 | tf_op jit(solution)/shard_map/reduce_scatter | solution.py:253
  790.9 2289.9 %reduce-scatter.24.cloned.1.call-start = ((), (), s32[]{:S(2)}) async-start(), calls=%async_computation.22 | async-start | bytes 17301504 | tf_op jit(solution)/shard_map/reduce_scatter | solution.py:260
  801.6 2642.1 %reduce-scatter.22.cloned.1.call-start = ((), (), s32[]{:S(2)}) async-start(), calls=%async_computation.21 | async-start | bytes 17301504 | tf_op jit(solution)/shard_map/reduce_scatter | solution.py:259
  810.9 39.4 %copy-start.22 = (f32[2]{0:T(128)S(1)}, f32[2]{0:T(128)}, u32[]{:S(2)}) copy-start(f32[2]{0:T(128)} %param.39) | copy-start | bytes 28
  810.9 39.9 %copy-start.11 = (bf16[16,64,128]{2,1,0:T(8,128)(2,1)S(1)}, bf16[16,64,128]{2,1,0:T(8,128)(2,1)}, u32[]{:S(2)}) copy-start(bf16[16,64,128]{2,1,0:T(8,128)(2,1)} %copy-done.10) | copy-start | bytes 786436
  810.9 42.5 %copy-start.9 = (bf16[16,64,128]{2,1,0:T(8,128)(2,1)S(1)}, bf16[16,64,128]{2,1,0:T(8,128)(2,1)}, u32[]{:S(2)}) copy-start(bf16[16,64,128]{2,1,0:T(8,128)(2,1)} %copy-done.8) | copy-start | bytes 786436
  (18 other events, 36.0 us)
Sparse Core Ops, SparseCore 0:
  10.9 59.4 all-gather.12
  73.2 55.2 all-gather.14
  131.4 55.2 all-gather.10
  189.5 55.2 all-gather.16
  247.5 76.3 all-gather.22
  326.7 113.3 all-gather.18
  443.1 112.9 all-gather.20
  558.9 75.7 all-gather.24
  643.4 136.2 reduce-scatter.27
  781.9 134.3 reduce-scatter.29
  922.7 495.5 all-reduce.12
  1420.5 705.5 reduce-scatter.25
  2129.0 150.5 reduce-scatter.19
  2282.4 144.2 reduce-scatter.17
  2429.5 144.8 reduce-scatter.15
  2577.3 144.8 reduce-scatter.13
  2725.0 355.6 reduce-scatter.23
  3083.6 359.9 reduce-scatter.21
where the time goes:
time: 3460 us; the launch traced here: 3450 us
  waiting for transfers between devices  2940 us (85%)
  blocking collectives  251 us (7%)
  matrix products  155 us (4%)
  local copies, waits for them, and re-layouts  81.9 us (2%)
    reduce_scatter x1, waiting for transfers between devices, body(): lax.psum_scatter(grad_ed_lead, ('dp', 'shard'), scatter_dimension=0, tile...  705 us
    unnamed x21, waiting for transfers between devices  522 us
    reduce_scatter x1, waiting for transfers between devices, body(): lax.psum_scatter(grad_wu, ('dp', 'shard'), scatter_dimension=0, tiled=True)  363 us
    reduce_scatter x1, waiting for transfers between devices, body(): lax.psum_scatter(grad_wd, ('dp', 'shard'), scatter_dimension=0, tiled=True)  359 us
    reduce_scatter x1, waiting for transfers between devices, body(): lax.psum_scatter(grad_wo, ('dp', 'shard'), scatter_dimension=0, tiled=True)  151 us
    reduce_scatter x1, waiting for transfers between devices, body(): lax.psum_scatter(grad_wk, ('dp', 'shard'), scatter_dimension=0, tiled=True)  148 us
    reduce_scatter x1, waiting for transfers between devices, body(): lax.psum_scatter(grad_wq, ('dp', 'shard'), scatter_dimension=0, tiled=True)  148 us
    reduce_scatter x1, waiting for transfers between devices, body(): lax.psum_scatter(grad_wv, ('dp', 'shard'), scatter_dimension=0, tiled=True)  147 us
  transfers between devices with their start and end apart: 18, of which 14 were waited for; matrix products, arithmetic and copies ran while one was open for 7% of the time, Pallas kernels for 0%

commit v1 on v0

v1 whole, which is shorter than its diff:
```python
import jax
import jax.numpy as jnp
from jax import lax
from jax.sharding import PartitionSpec as P

HEADS = 16
CAP = 74
BF = jnp.bfloat16
F32 = jnp.float32
BOTH = ("dp", "shard")


def mm(a, b, dims=((1,), (0,))):
    return lax.dot_general(a, b, (dims, ((), ())), preferred_element_type=F32)


def layer_norm(values, gain, bias):
    centre = values - jnp.mean(values, axis=-1, keepdims=True)
    scale_inv = lax.rsqrt(jnp.mean(centre * centre, axis=-1, keepdims=True) + 1e-05)
    normed = centre * scale_inv
    return (normed * gain + bias, normed, scale_inv)


def norm_back(grad_out, normed, scale_inv, gain):
    grad_normed = grad_out * gain
    inner = grad_normed - jnp.mean(grad_normed, axis=-1, keepdims=True)
    inner = inner - normed * jnp.mean(grad_normed * normed, axis=-1, keepdims=True)
    return (scale_inv * inner, jnp.sum(grad_out * normed, axis=0), jnp.sum(grad_out, axis=0))


def gelu_pair(t):
    inner = 0.7978845608 * (t + 0.044715 * t * t * t)
    th = jnp.tanh(inner)
    val = 0.5 * t * (1.0 + th)
    der = 0.5 * (1.0 + th) + 0.5 * t * (1.0 - th * th) * 0.7978845608 * (1.0 + 3.0 * 0.044715 * t * t)
    return val, der


def ag(block):
    return lax.all_gather(block, "shard", axis=0, tiled=False)


def rs(parts):
    return lax.psum_scatter(parts.astype(BF), "shard", scatter_dimension=0, tiled=False).astype(F32)


def body(
    hidden_in, doc_ids, expert_ids, slot_ids, out_grad, ln1_gain, ln1_bias, w_query, w_key, w_value,
    w_out, ln2_gain, ln2_bias, w_up, w_down, w_router, w_mix, expert_up, expert_down, load_avg,
):
    T, D = hidden_in.shape
    H, HD = HEADS, D // HEADS
    S = lax.axis_size("shard")
    C = lax.axis_size("dp")
    WR = w_query.shape[0]
    FF = w_up.shape[1]
    FR = w_down.shape[0]
    F = FR * C
    E = expert_up.shape[0]
    LO, HI = 80, T - 80

    pos = jnp.where(expert_ids == 0, slot_ids, jnp.sum((expert_ids == 0).astype(jnp.int32)) + slot_ids)
    n0 = jnp.sum((expert_ids == 0).astype(jnp.int32))
    place = lax.iota(jnp.int32, T)
    perm = (pos[None, :] == place[:, None]).astype(BF)
    xs = mm(perm, hidden_in)
    dys = mm(perm, out_grad).astype(BF)
    doc = doc_ids[0]
    allowed = (place[None, :] <= place[:, None]) & (doc[:, None] == doc[None, :])
    allowed = mm(mm(perm, allowed.astype(BF)).astype(BF), perm, ((1,), (1,))) > 0.5
    is0 = (place < n0)[:, None]

    small = jnp.stack(
        [ln1_gain, ln1_bias, ln2_gain, ln2_bias, w_router[:, 0], w_router[:, 1], w_mix[:, 0], w_mix[:, 1]]
    ).astype(F32)
    small = lax.all_gather(small, BOTH, axis=1, tiled=True)
    g1, b1, g2, b2 = small[0], small[1], small[2], small[3]
    wr, wm = small[4:6], small[6:8]

    wa = jnp.stack([w_query, w_key, w_value, w_out])
    wa = lax.all_gather(wa, BOTH, axis=1, tiled=True)
    wq, wk, wv, wo = wa[0], wa[1], wa[2], wa[3]

    ups = jnp.stack([w_up, expert_up[0], expert_up[1]])
    ups = ups.reshape(3, WR, C, S, FR).transpose(3, 0, 1, 2, 4).reshape(S, 3, WR, F)
    ups = lax.all_to_all(ups, "shard", 0, 0)
    ups = lax.all_gather(ups, "dp", axis=0)
    ups = ups.transpose(2, 0, 1, 3, 4).reshape(3, D, F)
    downs = jnp.stack([w_down, expert_down[0], expert_down[1]])
    downs = lax.all_gather(downs, "dp", axis=1, tiled=True)

    dy_all = ag(dys)

    n1, u1, i1 = layer_norm(xs, g1, b1)
    h1b = n1.astype(BF)
    q = (mm(h1b, wq) * 0.125).astype(BF).reshape(T, H, HD)
    k = mm(h1b, wk).astype(BF).reshape(T, H, HD)
    v = mm(h1b, wv).astype(BF).reshape(T, H, HD)
    s = jnp.einsum("ihd,jhd->hij", q, k, preferred_element_type=F32)
    s = jnp.where(allowed[None], s, -1e30)
    ex = jnp.exp(s - jnp.max(s, axis=-1, keepdims=True))
    p = ex / jnp.sum(ex, axis=-1, keepdims=True)
    pb = p.astype(BF)
    o = jnp.einsum("hij,jhd->ihd", pb, v, preferred_element_type=F32).reshape(T, D).astype(BF)
    x1 = xs + mm(o, wo)
    h2, u2, i2 = layer_norm(x1, g2, b2)
    h2b = h2.astype(BF)

    def two(w):
        return jnp.stack([jnp.sum(h2 * w[0], axis=-1), jnp.sum(h2 * w[1], axis=-1)], axis=-1)

    r = jax.nn.softmax(two(wr), axis=-1)
    c = jax.nn.softmax(two(wm), axis=-1)
    gate = jnp.where(is0, r[:, 0:1], r[:, 1:2])
    c0, c1 = c[:, 0:1], c[:, 1:2]
    we = c0 * gate
    scal = jnp.concatenate([c1, jnp.where(is0, we, 0.0), jnp.where(is0, 0.0, we)], axis=1)

    h_all = ag(h2b)
    scal_all = ag(scal)

    def cut(a, e):
        return (a[:, :LO] if e == 1 else a[:, HI:]) if e else a

    partial_y = jnp.zeros((S, T, D), F32)
    partial_dh = jnp.zeros((S, T, D), F32)
    score = []
    gup, gdown = [], []
    for e in range(3):
        he = cut(h_all, e)
        dye = cut(dy_all, e).astype(F32)
        se = cut(scal_all, e)[:, :, e : e + 1]
        n = he.shape[1]
        hf = he.reshape(S * n, D)
        pre = mm(hf, ups[e])
        val, der = gelu_pair(pre)
        ub = val.astype(BF)
        m = mm(ub, downs[e]).reshape(S, n, D)
        dm = (dye * se).astype(BF).reshape(S * n, D)
        dg = (mm(dm, downs[e], ((1,), (1,))) * der).astype(BF)
        gdown.append(mm(ub, dm, ((0,), (0,))))
        gup.append(mm(hf, dg, ((0,), (0,))))
        dx = mm(dg, ups[e], ((1,), (1,))).reshape(S, n, D)
        y = m * se
        sc = jnp.sum(dye * m, axis=-1)
        pad = [(0, 0), (0, T - n) if e < 2 else (T - n, 0)]
        live = is0[None, :, 0]
        partial_y += jnp.pad(y, pad + [(0, 0)])
        partial_dh += jnp.pad(dx, pad + [(0, 0)])
        score.append(jnp.pad(sc, pad))
    yfull = rs(partial_y)
    dh2 = rs(partial_dh)
    sc = lax.psum_scatter(jnp.stack(score, axis=1), "shard", scatter_dimension=0, tiled=False)
    sm = sc[0][:, None]
    se = jnp.where(is0, sc[1][:, None], sc[2][:, None])

    dc0, dc1 = gate * se, sm
    tot = c0 * dc0 + c1 * dc1
    dcl0, dcl1 = c0 * (dc0 - tot), c1 * (dc1 - tot)
    dgate = c0 * se
    dr0, dr1 = jnp.where(is0, dgate, 0.0), jnp.where(is0, 0.0, dgate)
    tot = r[:, 0:1] * dr0 + r[:, 1:2] * dr1
    drl0, drl1 = r[:, 0:1] * (dr0 - tot), r[:, 1:2] * (dr1 - tot)
    layer_out = (x1 + yfull).astype(BF)
    dh2 = dh2 + drl0 * wr[0] + drl1 * wr[1] + dcl0 * wm[0] + dcl1 * wm[1]
    gw = [jnp.sum(h2 * t, axis=0) for t in (drl0, drl1, dcl0, dcl1)]
    dx1, gg2, gb2 = norm_back(dh2, u2, i2, g2)
    dx1 = dx1 + dys.astype(F32)
    dab = dx1.astype(BF)
    gwo = mm(o, dab, ((0,), (0,)))
    do = mm(dab, wo, ((1,), (1,))).astype(BF).reshape(T, H, HD)
    dp = jnp.einsum("ihd,jhd->hij", do, v, preferred_element_type=F32)
    ds = (p * (dp - jnp.sum(p * dp, axis=-1, keepdims=True))).astype(BF)
    dq = jnp.einsum("hij,jhd->ihd", ds, k, preferred_element_type=F32).astype(BF)
    dq = (dq * BF(0.125)).reshape(T, D)
    dk = jnp.einsum("hij,ihd->jhd", ds, q, preferred_element_type=F32).astype(BF).reshape(T, D)
    dv = jnp.einsum("hij,ihd->jhd", pb, do, preferred_element_type=F32).astype(BF).reshape(T, D)
    dh1 = mm(dq, wq, ((1,), (1,))) + mm(dk, wk, ((1,), (1,))) + mm(dv, wv, ((1,), (1,)))
    ga = jnp.stack([mm(h1b, dq, ((0,), (0,))), mm(h1b, dk, ((0,), (0,))), mm(h1b, dv, ((0,), (0,))), gwo])
    dxn, gg1, gb1 = norm_back(dh1, u1, i1, g1)
    input_grad = (dx1 + dxn).astype(BF)

    layer_out = mm(perm, layer_out, ((0,), (0,))).astype(BF)
    input_grad = mm(perm, input_grad, ((0,), (0,))).astype(BF)

    smalls = lax.psum(jnp.stack([gg1, gb1, gg2, gb2] + gw), BOTH)
    mine = lax.dynamic_slice_in_dim(smalls, lax.axis_index(BOTH) * WR, WR, 1)
    ga = ga.reshape(4, C, S, WR, D).transpose(1, 2, 0, 3, 4)
    ga = lax.psum_scatter(ga.astype(BF), "dp", scatter_dimension=0, tiled=False)
    ga = lax.psum_scatter(ga, "shard", scatter_dimension=0, tiled=False).astype(F32)
    gdown = lax.psum_scatter(jnp.stack(gdown), "dp", scatter_dimension=1, tiled=True)
    gup = jnp.stack(gup).reshape(3, C, S, WR, F).transpose(1, 2, 0, 3, 4)
    gup = lax.psum_scatter(gup, "dp", scatter_dimension=0, tiled=False).astype(BF)
    gup = lax.all_to_all(gup, "shard", 0, 0).astype(F32)
    gup = gup.reshape(S, 3, WR, C, FR).transpose(1, 2, 3, 0, 4).reshape(3, WR, FF)

    counts = lax.psum(jnp.stack([n0, T - n0]), BOTH)
    load_new = 0.9 * load_avg + 0.1 * counts.astype(F32) * E / (T * C * S)
    return (
        layer_out, input_grad, mine[0], mine[1], ga[0], ga[1], ga[2], ga[3], mine[2], mine[3],
        gup[0], gdown[0], jnp.stack([mine[4], mine[5]], axis=1), jnp.stack([mine[6], mine[7]], axis=1),
        gup[1:], gdown[1:], counts, load_new,
    )


def solution(mesh):
    row, vec = P(BOTH, None), P(BOTH)
    mid = P(None, BOTH, None)
    return jax.shard_map(
        body,
        mesh=mesh,
        in_specs=(row, row, vec, vec, row, vec, vec, row, row, row, row, vec, vec, row, row, row, row, mid, mid, P()),
        out_specs=(row, row, vec, vec, row, row, row, row, vec, vec, row, row, row, row, mid, mid, P(), P()),
        check_vma=False,
    )
```

time: 3460 us -> 914 us (0.26)
  waiting for transfers between devices: 2940 us -> 397 us
  matrix products: 155 us -> 86.8 us
  blocking collectives: 251 us -> 296 us
    reduce_scatter x7 -> x3, waiting for transfers between devices: 2020 us -> 92.2 us  [the longest x2 92.2 us: rs(): lax.psum_scatter(parts.astype(BF), 'shard', scatter_dimension=0, tiled=Fa...]
    unnamed x21 -> x12, waiting for transfers between devices: 522 us -> 157 us
    all_gather x8 -> x5, waiting for transfers between devices: 398 us -> 148 us  [the longest x2 146 us: ag(): return lax.all_gather(block, 'shard', axis=0, tiled=False)]
    dot_general x34 -> x40, matrix products: 152 us -> 85.4 us  [the longest x35 80.9 us: mm(): return lax.dot_general(a, b, (dims, ((), ())), preferred_element_type=F32)]
    psum x1 -> x2, blocking collectives: 39.2 us -> 92 us  [the longest x1 48.4 us: body(): counts = lax.psum(jnp.stack([n0, T - n0]), BOTH)]
    transpose x2 -> x1, local copies, waits for them, and re-layouts: 50.7 us -> 2.01 us  [body(): gup.reshape(S, 3, WR, C, FR).transpose(1, 2, 3, 0, 4).reshape(3, WR, FF)]
  transfers between devices with their start and end apart: 18 -> 12, of which waited for: 14 -> 5; matrix products, arithmetic and copies ran while one was open for 7% -> 11% of each run, Pallas kernels for 0% -> 0%
where the time goes in v1:
time: 914 us; the launch traced here: 907 us
  waiting for transfers between devices  397 us (43%)
  blocking collectives  296 us (32%)
  matrix products  86.8 us (9%)
  local copies, waits for them, and re-layouts  55.5 us (6%)
  other arithmetic  40 us (4%)
  between operations  16.2 us (2%)
  starting transfers between devices  15.4 us (2%)
    unnamed x12, waiting for transfers between devices  157 us
    all_gather x2, waiting for transfers between devices, ag(): return lax.all_gather(block, 'shard', axis=0, tiled=False)  146 us
    reduce_scatter x2, waiting for transfers between devices, rs(): lax.psum_scatter(parts.astype(BF), 'shard', scatter_dimension=0, tiled=Fa...  92.2 us
    unnamed x2, blocking collectives  86.7 us
    all_gather x1, blocking collectives, body(): small = lax.all_gather(small, BOTH, axis=1, tiled=True)  81.6 us
    dot_general x35, matrix products, mm(): return lax.dot_general(a, b, (dims, ((), ())), preferred_element_type=F32)  80.9 us
    psum x1, blocking collectives, body(): counts = lax.psum(jnp.stack([n0, T - n0]), BOTH)  48.4 us
    psum x1, blocking collectives, body(): smalls = lax.psum(jnp.stack([gg1, gb1, gg2, gb2] + gw), BOTH)  43.6 us
  transfers between devices with their start and end apart: 12, of which 5 were waited for; matrix products, arithmetic and copies ran while one was open for 11% of the time, Pallas kernels for 0%

profile of v1, /device:TPU:0, one launch (start us, length us, event | category | flops | bytes accessed | tf_op | source)
XLA Modules:
  0.0 906.6 jit_solution(14686394213423674145)
XLA Ops:
  13.6 8.3 all-to-all-start
  22.1 81.6 %all-gather.4 = f32[32,32,8]{1,2,0:T(8,128)S(1)} all-gather(f32[1,32,8]{1,2,0:T(8,128)S(1)} %convert_bitcast_fusion.4), channel_id=1, replica_groups=mesh['dp'=2,'shard'=16] {'dp','shard'}, dimensions={0}, use_global_device_ids=true | all-gather | bytes 33792 | tf_op jit(solution)/shard_map/all_gather | solution.py:76
  125.7 70.3 %all-gather.15.cloned.1.call-done = bf16[2048,1024]{1,0:T(8,128)(2,1)} async-done(((bf16[128,1024]{1,0:T(8,128)(2,1)}), bf16[2048,1024]{1,0:T(8,128)(2,1)}) %all-gather.15.cloned.1.call-update) | async-done | bytes 4194320 | tf_op jit(solution)/shard_map/all_gather | solution.py:40
  205.8 4.4 fusion.52
  210.2 76.1 %all-gather.19.cloned.1.call-done = bf16[2048,1024]{1,0:T(8,128)(2,1)} async-done(((bf16[128,1024]{1,0:T(8,128)(2,1)}), bf16[2048,1024]{1,0:T(8,128)(2,1)}) %all-gather.19.cloned.1.call-update) | async-done | bytes 4194320 | tf_op jit(solution)/shard_map/all_gather | solution.py:40
  286.3 8.0 fusion.4
  297.4 6.0 fusion.2
  303.4 74.4 %all-reduce.6 = f32[16,3,128]{2,1,0:T(4,128)S(1)} all-reduce(f32[16,3,128]{2,1,0:T(4,128)S(1)} %pad_maximum_fusion.3), channel_id=8, replica_groups=mesh['dp'=2,'shard'=16] {'shard'}, use_global_device_ids=true, to_apply=%region_18.19.clone | all-reduce | flops 6144 | bytes 49152
  380.5 35.9 %all-gather.2 = f32[2048,3]{0,1:T(4,128)S(1)} all-gather(f32[128,3]{0,1:T(4,128)S(1)} %pad_maximum_fusion.4), channel_id=4, replica_groups=mesh['dp'=2,'shard'=16] {'shard'}, dimensions={0}, use_global_device_ids=true | all-gather | bytes 26112 | tf_op jit(solution)/shard_map/all_gather | solution.py:40
  416.5 10.2 %fusion.3 = (bf16[16,80,1024]{2,1,0:T(8,128)(2,1)S(1)}, bf16[16,80,1024]{2,1,0:T(8,128)(2,1)S(1)}, f32[16,80,1024]{2,1,0:T(8,128)}, f32[16,80,1024]{2,1,0:T(8,128)}) fusion(f32[16,80]{1,0:T(8,128)S(1)} %get-tuple-element.62, bf16[16,128,1024]{2,1,0:T(8,128)(2,1)} %bitcast.390, f32[16,80]{1,0:T(8,128)S(1)} %get-tuple-element.63, f32[16,80,1024]{2,1,0:T(8,128)} %fusion.52, ...), kind=kLoop, calls=%fused_computation.12 | loop fusion | flops 10485760 | bytes 31467520 | tf_op jit(solution)/shard_map/convert_element_type | solution.py:139
  432.8 3.5 fusion.120
  438.2 7.0 fusion.1
  445.2 5.2 fusion.7
  455.3 92.2 %reduce-scatter.15.cloned.1.call-done = bf16[1,128,1024]{2,1,0:T(8,128)(2,1)} async-done(((bf16[16,128,1024]{2,1,0:T(8,128)(2,1)}), bf16[1,128,1024]{2,1,0:T(8,128)(2,1)}) %reduce-scatter.15.cloned.1.call-update) | async-done | bytes 262160 | tf_op jit(solution)/shard_map/reduce_scatter | solution.py:44
  560.1 3.8 maximum_bitcast_fusion
  574.0 4.7 copy.102
  578.7 4.4 copy.103
  583.1 6.6 copy.101
  599.3 12.2 %all-reduce.17 = bf16[2,16,3,32,256]{4,3,1,0,2:T(8,128)(2,1)S(1)} all-reduce(f32[2,16,3,32,256]{4,3,1,0,2:T(8,128)} %maximum_bitcast_fusion.1), channel_id=11, replica_groups=mesh['dp'=2,'shard'=16] {'dp'}, use_global_device_ids=true, to_apply=%region_35.36.clone | all-reduce | flops 786432 | bytes 4718592
  613.2 5.8 all-to-all-start.1
  619.0 5.6 dynamic-slice_bitcast_fusion
  626.1 48.4 %psum.15 = s32[2]{0:T(128)S(1)} all-reduce(s32[2]{0:T(128)S(1)} %pad_add_fusion), channel_id=1, replica_groups=mesh['dp'=2,'shard'=16] {'dp','shard'}, use_global_device_ids=true, to_apply=%region_37.38 | all-reduce | flops 2 | bytes 16 | tf_op jit(solution)/shard_map/psum | solution.py:197
  692.8 43.6 %psum.14 = f32[8,1024]{1,0:T(8,128)S(1)} all-reduce(f32[8,1024]{1,0:T(8,128)S(1)} %stack.176), channel_id=1, replica_groups=mesh['dp'=2,'shard'=16] {'dp','shard'}, use_global_device_ids=true, to_apply=%region_32.33 | all-reduce | flops 8192 | bytes 65536 | tf_op jit(solution)/shard_map/psum | solution.py:186
  741.2 155.9 %all-reduce.16.cloned.1.call-done = bf16[16,4,32,1024]{3,2,0,1:T(8,128)(2,1)} async-done(((bf16[16,4,32,1024]{3,2,0,1:T(8,128)(2,1)}), bf16[16,4,32,1024]{3,2,0,1:T(8,128)(2,1)}) %all-reduce.16.cloned.1.call-update) | async-done | bytes 4194320
  (279 shorter events, 116.3 us)
Async XLA Ops:
  7.2 98.4 %copy-start = (bf16[128,1024]{1,0:T(8,128)(2,1)S(1)}, bf16[128,1024]{1,0:T(8,128)(2,1)}, u32[]{:S(2)}) copy-start(bf16[128,1024]{1,0:T(8,128)(2,1)} %param.20) | copy-start | bytes 786436
  7.2 100.0 %all-gather.11.cloned.1.call-start = ((), (), s32[]{:S(2)}) async-start(), calls=%async_computation.5 | async-start | bytes 8650752 | tf_op jit(solution)/shard_map/all_gather | solution.py:81
  11.1 10.9 %copy-start.45 = (bf16[32,2]{0,1:T(2,128)(2,1)S(1)}, bf16[32,2]{0,1:T(2,128)(2,1)}, u32[]{:S(2)}) copy-start(bf16[32,2]{0,1:T(2,128)(2,1)} %param.35) | copy-start | bytes 388
  11.1 10.9 %copy-start.46 = (bf16[32]{0:T(256)(128)(2,1)S(1)}, bf16[32]{0:T(256)(128)(2,1)}, u32[]{:S(2)}) copy-start(bf16[32]{0:T(256)(128)(2,1)} %param.25) | copy-start | bytes 196
  11.1 10.9 %copy-start.47 = (bf16[32]{0:T(256)(128)(2,1)S(1)}, bf16[32]{0:T(256)(128)(2,1)}, u32[]{:S(2)}) copy-start(bf16[32]{0:T(256)(128)(2,1)} %param.26) | copy-start | bytes 196
  11.1 10.9 %copy-start.48 = (bf16[32]{0:T(256)(128)(2,1)S(1)}, bf16[32]{0:T(256)(128)(2,1)}, u32[]{:S(2)}) copy-start(bf16[32]{0:T(256)(128)(2,1)} %param.31) | copy-start | bytes 196
  11.1 10.9 %copy-start.49 = (bf16[32]{0:T(256)(128)(2,1)S(1)}, bf16[32]{0:T(256)(128)(2,1)}, u32[]{:S(2)}) copy-start(bf16[32]{0:T(256)(128)(2,1)} %param.32) | copy-start | bytes 196
  12.1 91.7 %copy-start.51 = (s32[128]{0:T(128)S(1)}, s32[128]{0:T(128)}, u32[]{:S(2)}) copy-start(s32[128]{0:T(128)} %param.22) | copy-start | bytes 1540
  12.2 92.3 %copy-start.50 = (s32[128]{0:T(128)S(1)}, s32[128]{0:T(128)}, u32[]{:S(2)}) copy-start(s32[128]{0:T(128)} %param.23) | copy-start | bytes 1540
  12.2 93.0 %copy-start.52 = (s32[1,128]{1,0:T(1,128)S(1)}, s32[1,128]{1,0:T(1,128)}, u32[]{:S(2)}) copy-start(s32[1,128]{1,0:T(1,128)} %param.21) | copy-start | bytes 1540
  13.6 92.6 %all-to-all-start = ((bf16[16,3,32,256]{3,2,1,0:T(8,128)(2,1)}), bf16[16,3,32,256]{3,2,1,0:T(8,128)(2,1)S(1)}, u32[]{:S(2)}, u32[]{:S(2)}) async-start(bf16[16,3,32,256]{3,2,1,0:T(8,128)(2,1)} %reshape.288), calls=%async_computation | async-start | bytes 1572864 | tf_op jit(solution)/shard_map/all_to_all | solution.py:86
  21.9 101.2 %all-gather.17.cloned.1.call-start = ((), (), s32[]{:S(2)}) async-start(), calls=%async_computation.11 | async-start | bytes 2359296 | tf_op jit(solution)/shard_map/all_gather | solution.py:87
  107.1 88.9 %all-gather.15.cloned.1.call-start = ((), (), s32[]{:S(2)}) async-start(), calls=%async_computation.10 | async-start | bytes 4456448 | tf_op jit(solution)/shard_map/all_gather | solution.py:40
  120.1 85.8 %all-gather.13.cloned.1.call-start = ((), (), s32[]{:S(2)}) async-start(), calls=%async_computation.6 | async-start | bytes 2359296 | tf_op jit(solution)/shard_map/all_gather | solution.py:90
  121.2 165.1 %all-gather.19.cloned.1.call-start = ((), (), s32[]{:S(2)}) async-start(), calls=%async_computation.12 | async-start | bytes 4456448 | tf_op jit(solution)/shard_map/all_gather | solution.py:40
  122.2 425.3 %reduce-scatter.15.cloned.1.call-start = ((), (), s32[]{:S(2)}) async-start(), calls=%async_computation.8 | async-start | bytes 4456448 | tf_op jit(solution)/shard_map/reduce_scatter | solution.py:44
  454.4 94.8 %copy-start.14 = (bf16[128,1024]{1,0:T(8,128)(2,1)S(1)}, bf16[128,1024]{1,0:T(8,128)(2,1)}, u32[]{:S(2)}) copy-start(bf16[128,1024]{1,0:T(8,128)(2,1)} %convolution_convert_fusion.4) | copy-start | bytes 786436
  454.4 164.6 %all-reduce.14.cloned.1.call-start = ((), (), s32[]{:S(2)}) async-start(), calls=%async_computation.13 | async-start | bytes 16777216
  563.9 117.0 %reduce-scatter.17.cloned.1.call-start = ((), (), s32[]{:S(2)}) async-start(), calls=%async_computation.9 | async-start | bytes 4718592 | tf_op jit(solution)/shard_map/reduce_scatter | solution.py:191
  572.6 165.6 %reduce-scatter.13.cloned.1.call-start = ((), (), s32[]{:S(2)}) async-start(), calls=%async_computation.7 | async-start | bytes 4456448 | tf_op jit(solution)/shard_map/reduce_scatter | solution.py:44
  613.2 61.8 %all-to-all-start.1 = ((bf16[16,3,32,256]{3,2,1,0:T(8,128)(2,1)}), bf16[16,3,32,256]{3,2,1,0:T(8,128)(2,1)}, u32[]{:S(2)}, u32[]{:S(2)}) async-start(bf16[16,3,32,256]{3,2,1,0:T(8,128)(2,1)} %copy.104), calls=%async_computation.3 | async-start | bytes 1572864 | tf_op jit(solution)/shard_map/all_to_all | solution.py:194
  619.0 278.1 %all-reduce.16.cloned.1.call-start = ((), (), s32[]{:S(2)}) async-start(), calls=%async_computation.14 | async-start | bytes 8388608
  624.7 49.8 %copy-start.53 = (f32[2]{0:T(128)S(1)}, f32[2]{0:T(128)}, u32[]{:S(2)}) copy-start(f32[2]{0:T(128)} %param.39) | copy-start | bytes 28
  738.1 161.4 %copy-start.1 = (bf16[128,1024]{1,0:T(8,128)(2,1)S(1)}, bf16[128,1024]{1,0:T(8,128)(2,1)}, u32[]{:S(2)}) copy-start(bf16[128,1024]{1,0:T(8,128)(2,1)} %param.20) | copy-start | bytes 786436
  (53 other events, 196.0 us)
Sparse Core Ops, SparseCore 0:
  11.5 86.9 all-gather.10
  107.2 8.0 all-gather.16
  120.2 75.7 all-gather.14
  197.4 8.3 all-gather.12
  209.0 77.2 all-gather.18
  454.5 92.9 reduce-scatter.14
  564.1 38.4 all-reduce.13
  604.8 12.2 reduce-scatter.16
  619.5 101.9 reduce-scatter.12
  727.9 169.1 all-reduce.15

commit v2 on v1

--- a/solution.py
+++ b/solution.py
@@ -1,6 +1,8 @@
 import jax
 import jax.numpy as jnp
 from jax import lax
+from jax.experimental import pallas as pl
+from jax.experimental.pallas import tpu as pltpu
 from jax.sharding import PartitionSpec as P
 
 HEADS = 16
@@ -8,6 +10,7 @@
 BF = jnp.bfloat16
 F32 = jnp.float32
 BOTH = ("dp", "shard")
+MESH = pl.DeviceIdType.MESH
 
 
 def mm(a, b, dims=((1,), (0,))):
@@ -42,6 +45,354 @@
 
 def rs(parts):
     return lax.psum_scatter(parts.astype(BF), "shard", scatter_dimension=0, tiled=False).astype(F32)
+
+
+def place_of():
+    me = lax.axis_index("shard")
+    core = lax.axis_index("dp")
+    z, p = me // 4, me % 4
+    xq = p + 1 - 2 * (p % 2)
+    yq = p + 2 - 4 * (p // 2)
+    return me, core, z, p, xq, yq, 3 - p
+
+
+def greet(shards, core):
+    bar = pltpu.get_barrier_semaphore()
+    me = lax.axis_index("shard")
+
+    @pl.loop(1, shards)
+    def _(i):
+        pl.semaphore_signal(bar, inc=1, device_id=(core, (me + i) % shards), device_id_type=MESH)
+
+    pl.semaphore_signal(bar, inc=1, device_id=(1 - core, me), device_id_type=MESH)
+    pl.semaphore_wait(bar, shards)
+
+
+def remote(src, dst, send, recv, dev):
+    return pltpu.make_async_remote_copy(
+        src_ref=src, dst_ref=dst, send_sem=send, recv_sem=recv, device_id=dev, device_id_type=MESH
+    )
+
+
+def rows_loop(count, step, fn):
+    @pl.loop(0, count // step)
+    def _(i):
+        fn(pl.multiple_of(i * step, step))
+
+
+def ffn_kernel(
+    h_ref, scal_ref, dy_ref, up_ref, dn_ref,
+    y_out, dh_out, sc_out, gup_out, gdn0_out, gdn12_out,
+    hall, scall, psc, screcv, wcol, scol, part, ra, rbx, rby, rd, final,
+    pre, der, ub, dg, dm, m, yacc, dxacc, gdn, gup, sib_dn, sib_up, gsend, grecv,
+    ag_s, ag_r, rs_s, rs_r, one_s, one_r, sm_s, sm_r,
+):
+    S, T, D = hall.shape
+    F = up_ref.shape[2]
+    L = S // 4
+    LO = 80
+    HI = T - LO
+    me, core, z, p, xq, yq, dq = place_of()
+    xn, yn = z * 4 + xq, z * 4 + yq
+    sgn = 1 - 2 * (z // (L // 2))
+    greet(S, core)
+
+    def lev_of(k):
+        return (z + k * sgn + L) % L
+
+    def h_copy(kind, slot, src, idx, dev):
+        return remote(src, hall.at[idx], ag_s.at[kind, slot], ag_r.at[kind, slot], (core, dev))
+
+    @pl.loop(1, L)
+    def _(k):
+        lev = lev_of(k)
+        remote(h_ref, hall.at[me], ag_s.at[0, lev], ag_r.at[0, z], (core, lev * 4 + p)).start()
+
+    h_copy(1, z, h_ref, me, xn).start()
+    h_copy(2, z, h_ref, me, yn).start()
+
+    @pl.loop(1, S)
+    def _(i):
+        remote(scal_ref, scall.at[me], sm_s.at[0, i], sm_r.at[0], (core, (me + i) % S)).start()
+
+    hall[me] = h_ref[...]
+    scall[me] = scal_ref[...]
+    gdn[...] = jnp.zeros_like(gdn)
+    gup[...] = jnp.zeros_like(gup)
+    remote(scall.at[pl.ds(0, S - 1)], scall.at[pl.ds(0, S - 1)], sm_s.at[0, 0], sm_r.at[0], (core, xn)).wait_recv()
+
+    def stage_a(k):
+        lev = lev_of(k)
+        idx = lev * 4 + p
+        h_copy(0, lev, hall.at[idx], idx, xn).wait_recv()
+        h_copy(1, lev, hall.at[idx], idx, xn).start()
+        h_copy(2, lev, hall.at[idx], idx, yn).start()
+
+    def stage_b(k):
+        lev = lev_of(k)
+        odd = k % 2
+        h_copy(1, lev, h_ref, lev * 4 + xq, xn).wait_recv()
+        h_copy(2, lev, h_ref, lev * 4 + yq, yn).wait_recv()
+        idx = lev * 4 + xq + odd * (yq - xq)
+        h_copy(3, lev, hall.at[idx], idx, yn + odd * (xn - yn)).start()
+        h_copy(3, lev, h_ref, lev * 4 + dq, xn).wait_recv()
+
+    lane = lax.broadcasted_iota(jnp.int32, (16, 128), 1)
+
+    def compute(lev):
+        base = lev * 4
+        for q in range(4):
+            full = jnp.concatenate([scall[base + q], jnp.zeros((120, 128), F32)], axis=0)
+            wcol[q] = full.T
+        for e in range(3):
+            n = LO if e else T
+            off = HI if e == 2 else 0
+            rows = 4 * n
+            hm = hall[pl.ds(base, 4), off : off + n, :].reshape(rows, D)
+            pre[0:rows, :] = mm(hm, up_ref[e])
+
+            def act(r):
+                val, d = gelu_pair(pre[pl.ds(r, 32), :])
+                ub[pl.ds(r, 32), :] = val.astype(BF)
+                der[pl.ds(r, 32), :] = d
+
+            rows_loop(rows, 32, act)
+            m[0:rows, :] = mm(ub[0:rows, :], dn_ref[e])
+            for q in range(4):
+
+                def elem(r):
+                    at = pl.multiple_of(r + off, 16)
+                    mine = pl.ds(pl.multiple_of(q * n + r, 16), 16)
+                    t = pl.ds(pl.multiple_of(q * T + off + r, 16), 16)
+                    w = wcol[q, pl.ds(at, 16), :][:, e : e + 1]
+                    dyv = dy_ref[base + q, pl.ds(at, 16), :].astype(F32)
+                    mv = m[mine, :]
+                    s = jnp.sum(dyv * mv, axis=1, keepdims=True)
+                    s = jnp.where(lane == e, s, 0.0)
+                    dm[mine, :] = (dyv * w).astype(BF)
+                    if e:
+                        yacc[t, :] = yacc[t, :] + mv * w
+                        scol[q, pl.ds(at, 16), :] = scol[q, pl.ds(at, 16), :] + s
+                    else:
+                        yacc[t, :] = mv * w
+                        scol[q, pl.ds(at, 16), :] = s
+
+                rows_loop(n, 16, elem)
+            pre[0:rows, :] = mm(dm[0:rows, :], dn_ref[e], ((1,), (1,)))
+
+            def back(r):
+                dg[pl.ds(r, 32), :] = (pre[pl.ds(r, 32), :] * der[pl.ds(r, 32), :]).astype(BF)
+
+            rows_loop(rows, 32, back)
+            gdn[e] = gdn[e] + mm(ub[0:rows, :], dm[0:rows, :], ((0,), (0,)))
+            gup[e] = gup[e] + mm(dg[0:rows, :], hm, ((0,), (0,)))
+            if e:
+                m[0:rows, :] = mm(dg[0:rows, :], up_ref[e], ((1,), (1,)))
+                for q in range(4):
+
+                    def addx(r):
+                        t = pl.ds(pl.multiple_of(q * T + off + r, 16), 16)
+                        dxacc[t, :] = dxacc[t, :] + m[pl.ds(pl.multiple_of(q * n + r, 16), 16), :]
+
+                    rows_loop(n, 16, addx)
+            else:
+                dxacc[...] = mm(dg[...], up_ref[0], ((1,), (1,)))
+        for q in range(4):
+            psc[base + q] = scol[q].T[0:8, :]
+
+            def out(r):
+                t = pl.ds(pl.multiple_of(q * T + r, 16), 16)
+                part[0, base + q, pl.ds(r, 16), :] = dxacc[t, :].astype(BF)
+                part[1, base + q, pl.ds(r, 16), :] = yacc[t, :].astype(BF)
+
+            rows_loop(T, 16, out)
+
+    def r_copy(kind, a, lev, src, dst, dev):
+        return remote(src, dst, rs_s.at[kind, a, lev], rs_r.at[kind, a, lev], (core, dev))
+
+    def rs_a(k):
+        lev = lev_of(k)
+        odd = k % 2
+        for a in range(2):
+            r_copy(0, a, lev, part.at[a, lev * 4 + dq], ra.at[a, lev], yn + odd * (xn - yn)).start()
+
+    def rs_b(k):
+        lev = lev_of(k)
+        odd = k % 2
+        via = lev * 4 + xq + odd * (yq - xq)
+        for a in range(2):
+            r_copy(0, a, lev, ra.at[a, lev], ra.at[a, lev], xn).wait_recv()
+
+            def add(r):
+                t = pl.ds(r, 16)
+                part[a, via, t, :] = (part[a, via, t, :].astype(F32) + ra[a, lev, t, :].astype(F32)).astype(BF)
+
+            rows_loop(T, 16, add)
+            r_copy(1, a, lev, part.at[a, lev * 4 + xq], rbx.at[a, lev], xn).start()
+            r_copy(2, a, lev, part.at[a, lev * 4 + yq], rby.at[a, lev], yn).start()
+
+    def rs_c(k):
+        lev = lev_of(k)
+        own = lev * 4 + p
+        for a in range(2):
+            r_copy(1, a, lev, rbx.at[a, lev], rbx.at[a, lev], xn).wait_recv()
+            r_copy(2, a, lev, rby.at[a, lev], rby.at[a, lev], yn).wait_recv()
+
+            def add(r):
+                t = pl.ds(r, 16)
+                tot = part[a, own, t, :].astype(F32) + rbx[a, lev, t, :].astype(F32) + rby[a, lev, t, :].astype(F32)
+
+                @pl.when(k == 0)
+                def _():
+                    final[a, t, :] = tot
+
+                @pl.when(k > 0)
+                def _():
+                    part[a, own, t, :] = tot.astype(BF)
+
+            rows_loop(T, 16, add)
+
+            @pl.when(k > 0)
+            def _():
+                remote(
+                    part.at[a, own], rd.at[a, z], rs_s.at[3, a, lev], rs_r.at[3, a, z], (core, lev * 4 + p)
+                ).start()
+
+    stage_a(1)
+
+    @pl.loop(0, L)
+    def _(k):
+        stage_b(k)
+
+        @pl.when(k < L - 2)
+        def _():
+            stage_a(k + 2)
+
+        compute(lev_of(k))
+        rs_a(k)
+
+        @pl.when(k > 0)
+        def _():
+            rs_c(k - 1)
+
+        rs_b(k)
+
+    half = D // 2
+    other = pl.multiple_of((1 - core) * half, half)
+    mine_d = pl.multiple_of(core * half, half)
+    FR = F // 2
+    other_f = pl.multiple_of((1 - core) * FR, FR)
+    mine_f = pl.multiple_of(core * FR, FR)
+    sib = (1 - core, me)
+    c_up = remote(gup.at[:, :, pl.ds(other, half)], sib_up, one_s.at[0], one_r.at[0], sib)
+    c_dn = remote(gdn.at[:, pl.ds(other_f, FR), :], sib_dn, one_s.at[1], one_r.at[1], sib)
+    c_up.start()
+    c_dn.start()
+
+    @pl.loop(1, S)
+    def _(i):
+        to = (me + i) % S
+        remote(psc.at[to], screcv.at[i], sm_s.at[1, i], sm_r.at[1], (core, to)).start()
+
+    rs_c(L - 1)
+    c_up.wait_recv()
+    for e in range(3):
+        tot = gup[e, :, pl.ds(mine_d, half)] + sib_up[e]
+        gsend[e] = tot.T.astype(BF)
+    WR = half // S
+    screcv[0] = psc[me]
+
+    def g_copy(i, to):
+        return remote(
+            gsend.at[:, pl.ds(pl.multiple_of(to * WR, WR), WR), :], grecv.at[me], sm_s.at[2, i], sm_r.at[2], (core, to)
+        )
+
+    @pl.loop(1, S)
+    def _(i):
+        g_copy(i, (me + i) % S).start()
+
+    grecv[me] = gsend[:, pl.ds(pl.multiple_of(me * WR, WR), WR), :]
+    c_dn.wait_recv()
+    gdn0_out[...] = gdn[0, pl.ds(mine_f, FR), :] + sib_dn[0]
+    for e in range(1, 3):
+        gdn12_out[e - 1] = gdn[e, pl.ds(mine_f, FR), :] + sib_dn[e]
+
+    @pl.loop(1, L)
+    def _(k):
+        lev = lev_of(k)
+        for a in range(2):
+            r_copy(3, a, lev, rd.at[a, lev], rd.at[a, lev], xn).wait_recv()
+
+            def add(r):
+                t = pl.ds(r, 16)
+                final[a, t, :] = final[a, t, :] + rd[a, lev, t, :].astype(F32)
+
+            rows_loop(T, 16, add)
+
+    dh_out[...] = final[0]
+    y_out[...] = final[1]
+    remote(screcv.at[pl.ds(1, S - 1)], screcv.at[pl.ds(1, S - 1)], sm_s.at[1, 0], sm_r.at[1], (core, xn)).wait_recv()
+    sc_out[...] = jnp.sum(screcv[...], axis=0)
+    remote(grecv.at[pl.ds(0, S - 1)], grecv.at[pl.ds(0, S - 1)], sm_s.at[2, 0], sm_r.at[2], (core, xn)).wait_recv()
+    gup_out[...] = grecv[...]
+
+    c_up.wait_send()
+    c_dn.wait_send()
+
+    @pl.loop(1, S)
+    def _(i):
+        remote(scal_ref, scall.at[0], sm_s.at[0, i], sm_r.at[0], (core, xn)).wait_send()
+        remote(psc.at[0], screcv.at[0], sm_s.at[1, i], sm_r.at[1], (core, xn)).wait_send()
+        g_copy(i, (me + i) % S).wait_send()
+
+    @pl.loop(0, L)
+    def _(k):
+        lev = lev_of(k)
+        for kind in range(1, 4):
+            h_copy(kind, lev, hall.at[0], 0, xn).wait_send()
+        for a in range(2):
+            for kind in range(3):
+                r_copy(kind, a, lev, ra.at[a, 0], ra.at[a, 0], xn).wait_send()
+
+        @pl.when(k > 0)
+        def _():
+            h_copy(0, lev, hall.at[0], 0, xn).wait_send()
+            for a in range(2):
+                r_copy(3, a, lev, ra.at[a, 0], ra.at[a, 0], xn).wait_send()
+
+
+def ffn_call(h2b, scal, dy_all, ups, downs):
+    S, T, D = dy_all.shape
+    F = ups.shape[2]
+    L = S // 4
+    WR = D // 2 // S
+    vm = pl.BlockSpec(memory_space=pltpu.VMEM)
+    V = pltpu.VMEM
+    dma = pltpu.SemaphoreType.DMA
+    sds = jax.ShapeDtypeStruct
+    return pl.pallas_call(
+        ffn_kernel,
+        out_shape=(
+            sds((T, D), F32), sds((T, D), F32), sds((8, 128), F32), sds((S, 3, WR, F), BF),
+            sds((F // 2, D), F32), sds((2, F // 2, D), F32),
+        ),
+        in_specs=[vm] * 5,
+        out_specs=(vm,) * 6,
+        scratch_shapes=[
+            V((S, T, D), BF), V((S, 8, 128), F32), V((S, 8, 128), F32), V((S, 8, 128), F32),
+            V((4, T, 128), F32), V((4, T, 128), F32),
+            V((2, S, T, D), BF), V((2, L, T, D), BF), V((2, L, T, D), BF), V((2, L, T, D), BF), V((2, L, T, D), BF),
+            V((2, T, D), F32),
+            V((4 * T, F), F32), V((4 * T, F), F32), V((4 * T, F), BF), V((4 * T, F), BF), V((4 * T, D), BF),
+            V((4 * T, D), F32), V((4 * T, D), F32), V((4 * T, D), F32),
+            V((3, F, D), F32), V((3, F, D), F32), V((3, F // 2, D), F32), V((3, F, D // 2), F32),
+            V((3, D // 2, F), BF), V((S, 3, WR, F), BF),
+            dma((4, L)), dma((4, L)), dma((4, 2, L)), dma((4, 2, L)), dma((2,)), dma((2,)), dma((3, S)), dma((3,)),
+        ],
+        compiler_params=pltpu.CompilerParams(collective_id=2, has_side_effects=True, vmem_limit_bytes=64000000),
+        cost_estimate=pl.CostEstimate(flops=15 * 10**9, bytes_accessed=20 * 2**20, transcendentals=2**20),
+        name="ffn",
+    )(h2b, scal, dy_all, ups, downs)
 
 
 def body(
@@ -116,44 +467,49 @@
     we = c0 * gate
     scal = jnp.concatenate([c1, jnp.where(is0, we, 0.0), jnp.where(is0, 0.0, we)], axis=1)
 
-    h_all = ag(h2b)
-    scal_all = ag(scal)
-
-    def cut(a, e):
-        return (a[:, :LO] if e == 1 else a[:, HI:]) if e else a
-
-    partial_y = jnp.zeros((S, T, D), F32)
-    partial_dh = jnp.zeros((S, T, D), F32)
-    score = []
-    gup, gdown = [], []
-    for e in range(3):
-        he = cut(h_all, e)
-        dye = cut(dy_all, e).astype(F32)
-        se = cut(scal_all, e)[:, :, e : e + 1]
-        n = he.shape[1]
-        hf = he.reshape(S * n, D)
-        pre = mm(hf, ups[e])
-        val, der = gelu_pair(pre)
-        ub = val.astype(BF)
-        m = mm(ub, downs[e]).reshape(S, n, D)
-        dm = (dye * se).astype(BF).reshape(S * n, D)
-        dg = (mm(dm, downs[e], ((1,), (1,))) * der).astype(BF)
-        gdown.append(mm(ub, dm, ((0,), (0,))))
-        gup.append(mm(hf, dg, ((0,), (0,))))
-        dx = mm(dg, ups[e], ((1,), (1,))).reshape(S, n, D)
-        y = m * se
-        sc = jnp.sum(dye * m, axis=-1)
-        pad = [(0, 0), (0, T - n) if e < 2 else (T - n, 0)]
-        live = is0[None, :, 0]
-        partial_y += jnp.pad(y, pad + [(0, 0)])
-        partial_dh += jnp.pad(dx, pad + [(0, 0)])
-        score.append(jnp.pad(sc, pad))
-    yfull = rs(partial_y)
-    dh2 = rs(partial_dh)
-    sc = lax.psum_scatter(jnp.stack(score, axis=1), "shard", scatter_dimension=0, tiled=False)
+    fast = C == 2 and S % 4 == 0 and S >= 8 and FR % 128 == 0 and WR % 16 == 0
+    if fast:
+        scal8 = jnp.pad(scal.T, ((0, 5), (0, 0)))
+        yfull, dh2, sc, gup, gdn0, gdn12 = ffn_call(h2b, scal8, dy_all, ups, downs)
+    else:
+        h_all = ag(h2b)
+        scal_all = ag(scal)
+
+        def cut(a, e):
+            return (a[:, :LO] if e == 1 else a[:, HI:]) if e else a
+
+        partial_y = jnp.zeros((S, T, D), F32)
+        partial_dh = jnp.zeros((S, T, D), F32)
+        score = []
+        gup, gdown = [], []
+        for e in range(3):
+            he = cut(h_all, e)
+            dye = cut(dy_all, e).astype(F32)
+            se = cut(scal_all, e)[:, :, e : e + 1]
+            n = he.shape[1]
+            hf = he.reshape(S * n, D)
+            pre = mm(hf, ups[e])
+            val, der = gelu_pair(pre)
+            ub = val.astype(BF)
+            m = mm(ub, downs[e]).reshape(S, n, D)
+            dm = (dye * se).astype(BF).reshape(S * n, D)
+            dg = (mm(dm, downs[e], ((1,), (1,))) * der).astype(BF)
+            gdown.append(mm(ub, dm, ((0,), (0,))))
+            gup.append(mm(hf, dg, ((0,), (0,))))
+            dx = mm(dg, ups[e], ((1,), (1,))).reshape(S, n, D)
+            y = m * se
+            sc = jnp.sum(dye * m, axis=-1)
+            pad = [(0, 0), (0, T - n) if e < 2 else (T - n, 0)]
+            live = is0[None, :, 0]
+            partial_y += jnp.pad(y, pad + [(0, 0)])
+            partial_dh += jnp.pad(dx, pad + [(0, 0)])
+            score.append(jnp.pad(sc, pad))
+        yfull = rs(partial_y)
+        dh2 = rs(partial_dh)
+        sc = lax.psum_scatter(jnp.stack(score, axis=1), "shard", scatter_dimension=0, tiled=False)
+
     sm = sc[0][:, None]
     se = jnp.where(is0, sc[1][:, None], sc[2][:, None])
-
     dc0, dc1 = gate * se, sm
     tot = c0 * dc0 + c1 * dc1
     dcl0, dcl1 = c0 * (dc0 - tot), c1 * (dc1 - tot)
@@ -188,18 +544,22 @@
     ga = ga.reshape(4, C, S, WR, D).transpose(1, 2, 0, 3, 4)
     ga = lax.psum_scatter(ga.astype(BF), "dp", scatter_dimension=0, tiled=False)
     ga = lax.psum_scatter(ga, "shard", scatter_dimension=0, tiled=False).astype(F32)
-    gdown = lax.psum_scatter(jnp.stack(gdown), "dp", scatter_dimension=1, tiled=True)
-    gup = jnp.stack(gup).reshape(3, C, S, WR, F).transpose(1, 2, 0, 3, 4)
-    gup = lax.psum_scatter(gup, "dp", scatter_dimension=0, tiled=False).astype(BF)
-    gup = lax.all_to_all(gup, "shard", 0, 0).astype(F32)
+    if not fast:
+        gdown = lax.psum_scatter(jnp.stack(gdown), "dp", scatter_dimension=1, tiled=True)
+        gdn0, gdn12 = gdown[0], gdown[1:]
+        gup = jnp.stack(gup).reshape(3, C, S, WR, F)
+        gup = gup.transpose(1, 2, 0, 3, 4)
+        gup = lax.psum_scatter(gup, "dp", scatter_dimension=0, tiled=False).astype(BF)
+        gup = lax.all_to_all(gup, "shard", 0, 0)
+    gup = gup.astype(F32)
     gup = gup.reshape(S, 3, WR, C, FR).transpose(1, 2, 3, 0, 4).reshape(3, WR, FF)
 
     counts = lax.psum(jnp.stack([n0, T - n0]), BOTH)
     load_new = 0.9 * load_avg + 0.1 * counts.astype(F32) * E / (T * C * S)
     return (
         layer_out, input_grad, mine[0], mine[1], ga[0], ga[1], ga[2], ga[3], mine[2], mine[3],
-        gup[0], gdown[0], jnp.stack([mine[4], mine[5]], axis=1), jnp.stack([mine[6], mine[7]], axis=1),
-        gup[1:], gdown[1:], counts, load_new,
+        gup[0], gdn0, jnp.stack([mine[4], mine[5]], axis=1), jnp.stack([mine[6], mine[7]], axis=1),
+        gup[1:], gdn12, counts, load_new,
     )
 
 

time: 914 us -> 692 us (0.76)
  Pallas kernels: 0 us -> 218 us
  waiting for transfers between devices: 397 us -> 194 us
  blocking collectives: 296 us -> 180 us
  matrix products: 86.8 us -> 32 us
  local copies, waits for them, and re-layouts: 55.5 us -> 29.5 us
  other arithmetic: 40 us -> 20.7 us
  starting transfers between devices: 15.4 us -> 0.25 us
    pallas_call x0 -> x1, Pallas kernels: none -> 218 us  [ffn_call(): pl.pallas_call(ffn_kernel, out_shape=(sds((T, D), F32), sds((T, D), F32),...]
    reduce_scatter x3 -> x0, waiting for transfers between devices: 92.2 us -> none  [the longest x2 92.2 us: rs(): lax.psum_scatter(parts.astype(BF), 'shard', scatter_dimension=0, tiled=Fa...]
    unnamed x2 -> x0, blocking collectives: 86.7 us -> none
    all_gather x2 -> x1, waiting for transfers between devices: 146 us -> 76.5 us  [ag(): return lax.all_gather(block, 'shard', axis=0, tiled=False)]
    dot_general x35 -> x17, matrix products: 80.9 us -> 26 us  [mm(): return lax.dot_general(a, b, (dims, ((), ())), preferred_element_type=F32)]
    unnamed x12 -> x8, waiting for transfers between devices: 157 us -> 102 us
    all_gather x1 -> x0, blocking collectives: 35.9 us -> none  [ag(): return lax.all_gather(block, 'shard', axis=0, tiled=False)]
    all_to_all x0 -> x1, blocking collectives: none -> 29.5 us  [body(): ups = lax.all_to_all(ups, 'shard', 0, 0)]
  transfers between devices with their start and end apart: 12 -> 6, of which waited for: 5 -> 4; matrix products, arithmetic and copies ran while one was open for 11% -> 6% of each run, Pallas kernels for 0% -> 0%
where the time goes in v2:
time: 692 us; the launch traced here: 691 us
  Pallas kernels  218 us (32%)
  waiting for transfers between devices  194 us (28%)
  blocking collectives  180 us (26%)
  matrix products  32 us (5%)
  local copies, waits for them, and re-layouts  29.5 us (4%)
  other arithmetic  20.7 us (3%)
  between operations  15.5 us (2%)
    pallas_call x1, Pallas kernels, ffn_call(): pl.pallas_call(ffn_kernel, out_shape=(sds((T, D), F32), sds((T, D), F32),...  218 us
    unnamed x8, waiting for transfers between devices  102 us
    all_gather x1, waiting for transfers between devices, ag(): return lax.all_gather(block, 'shard', axis=0, tiled=False)  76.5 us
    all_gather x1, blocking collectives, body(): small = lax.all_gather(small, BOTH, axis=1, tiled=True)  65.7 us
    psum x1, blocking collectives, body(): counts = lax.psum(jnp.stack([n0, T - n0]), BOTH)  44 us
    psum x1, blocking collectives, body(): smalls = lax.psum(jnp.stack([gg1, gb1, gg2, gb2] + gw), BOTH)  41.1 us
    all_to_all x1, blocking collectives, body(): ups = lax.all_to_all(ups, 'shard', 0, 0)  29.5 us
    dot_general x17, matrix products, mm(): return lax.dot_general(a, b, (dims, ((), ())), preferred_element_type=F32)  26 us
  transfers between devices with their start and end apart: 6, of which 4 were waited for; matrix products, arithmetic and copies ran while one was open for 6% of the time, Pallas kernels for 0%

profile of v2, /device:TPU:0, one launch (start us, length us, event | category | flops | bytes accessed | tf_op | source)
XLA Modules:
  0.0 690.8 jit_solution(14058538774132330860)
XLA Ops:
  12.0 29.5 %all_to_all.5 = bf16[16,3,32,256]{3,2,1,0:T(8,128)(2,1)} all-to-all(bf16[16,3,32,256]{3,2,1,0:T(8,128)(2,1)S(1)} %reshape.217), channel_id=1, replica_groups=mesh['dp'=2,'shard'=16] {'shard'}, dimensions={0} | all-to-all | bytes 1572864 | tf_op jit(solution)/shard_map/all_to_all | solution.py:437
  45.9 65.7 %all-gather.2 = f32[32,32,8]{1,2,0:T(8,128)S(1)} all-gather(f32[1,32,8]{1,2,0:T(8,128)S(1)} %convert_bitcast_fusion.4), channel_id=1, replica_groups=mesh['dp'=2,'shard'=16] {'dp','shard'}, dimensions={0}, use_global_device_ids=true | all-gather | bytes 33792 | tf_op jit(solution)/shard_map/all_gather | solution.py:427
  113.2 2.7 copy.86
  115.9 16.0 %all-gather.8.cloned.1.call-done = bf16[4,1024,1024]{2,1,0:T(8,128)(2,1)} async-done(((bf16[4,32,1024]{2,1,0:T(8,128)(2,1)}), bf16[4,1024,1024]{2,1,0:T(8,128)(2,1)}) %all-gather.8.cloned.1.call-update) | async-done | bytes 8388624 | tf_op jit(solution)/shard_map/all_gather | solution.py:432
  131.9 2.1 fusion.17
  134.2 2.2 fusion.18
  136.6 2.1 fusion.16
  141.0 2.2 fusion.67
  146.5 76.5 %all-gather.12.cloned.1.call-done = bf16[2048,1024]{1,0:T(8,128)(2,1)} async-done(((bf16[128,1024]{1,0:T(8,128)(2,1)}), bf16[2048,1024]{1,0:T(8,128)(2,1)}) %all-gather.12.cloned.1.call-update) | async-done | bytes 4194320 | tf_op jit(solution)/shard_map/all_gather | solution.py:43
  223.0 218.3 %ffn.1 = (f32[128,1024]{1,0:T(8,128)}, f32[128,1024]{1,0:T(8,128)}, f32[8,128]{1,0:T(8,128)}, bf16[16,3,32,256]{3,2,1,0:T(8,128)(2,1)}, f32[128,1024]{1,0:T(8,128)}, /*index=5*/f32[2,128,1024]{2,1,0:T(8,128)}) custom-call(bf16[128,1024]{1,0:T(8,128)(2,1)} %convert_element_type.110.h_ref, f32[8,128]{1,0:T(8,128)} %pad.4.scal_ref, ...), custom_call_target="tpu_custom_call" | custom-call | flops 15000000512 | bytes 20971520 | tf_op jit(solution)/shard_map/ffn/pallas_call | solution.py:373
  446.8 3.3 fusion.15
  458.3 3.8 maximum_bitcast_fusion
  463.4 37.6 %all-reduce.6.cloned.1.call-done = bf16[2,16,4,32,1024]{4,3,1,0,2:T(8,128)(2,1)} async-done(((bf16[2,16,4,32,1024]{4,3,1,0,2:T(8,128)(2,1)}), bf16[2,16,4,32,1024]{4,3,1,0,2:T(8,128)(2,1)}) %all-reduce.6.cloned.1.call-update) | async-done | bytes 8388624
  501.0 5.6 dynamic-slice_bitcast_fusion
  508.0 44.0 %psum.15 = s32[2]{0:T(128)S(1)} all-reduce(s32[2]{0:T(128)S(1)} %pad_add_fusion), channel_id=1, replica_groups=mesh['dp'=2,'shard'=16] {'dp','shard'}, use_global_device_ids=true, to_apply=%region_29.30 | all-reduce | flops 2 | bytes 16 | tf_op jit(solution)/shard_map/psum | solution.py:557
  553.1 2.0 reshape.226
  557.4 1.8 copy.96
  560.5 2.4 fusion.1
  562.9 2.5 fusion.3
  565.4 2.7 multiply_reduce_fusion.6
  568.2 41.1 %psum.14 = f32[8,1024]{1,0:T(8,128)S(1)} all-reduce(f32[8,1024]{1,0:T(8,128)S(1)} %stack.142), channel_id=1, replica_groups=mesh['dp'=2,'shard'=16] {'dp','shard'}, use_global_device_ids=true, to_apply=%region_26.27 | all-reduce | flops 8192 | bytes 65536 | tf_op jit(solution)/shard_map/psum | solution.py:542
  613.2 64.2 %all-reduce.8.cloned.1.call-done = bf16[16,4,32,1024]{3,2,0,1:T(8,128)(2,1)} async-done(((bf16[16,4,32,1024]{3,2,0,1:T(8,128)(2,1)}), bf16[16,4,32,1024]{3,2,0,1:T(8,128)(2,1)}) %all-reduce.8.cloned.1.call-update) | async-done | bytes 4194320
  679.8 1.9 copy.118
  681.7 2.3 copy.119
  (162 shorter events, 42.8 us)
Async XLA Ops:
  7.2 105.0 %copy-start = (bf16[128,1024]{1,0:T(8,128)(2,1)S(1)}, bf16[128,1024]{1,0:T(8,128)(2,1)}, u32[]{:S(2)}) copy-start(bf16[128,1024]{1,0:T(8,128)(2,1)} %param.20) | copy-start | bytes 786436
  7.2 106.0 %all-gather.14.cloned.1.call-start = ((), (), s32[]{:S(2)}) async-start(), calls=%async_computation.4 | async-start | bytes 2359296 | tf_op jit(solution)/shard_map/all_gather | solution.py:438
  7.3 34.3 %copy-start.16 = (bf16[32,1024]{1,0:T(8,128)(2,1)S(1)}, bf16[32,1024]{1,0:T(8,128)(2,1)}, u32[]{:S(2)}) copy-start(bf16[32,1024]{1,0:T(8,128)(2,1)} %param.30) | copy-start | bytes 196612
  7.3 34.3 %copy-start.17 = (bf16[32,1024]{1,0:T(8,128)(2,1)S(1)}, bf16[32,1024]{1,0:T(8,128)(2,1)}, u32[]{:S(2)}) copy-start(bf16[32,1024]{1,0:T(8,128)(2,1)} %param.29) | copy-start | bytes 196612
  7.3 34.3 %copy-start.18 = (bf16[32,1024]{1,0:T(8,128)(2,1)S(1)}, bf16[32,1024]{1,0:T(8,128)(2,1)}, u32[]{:S(2)}) copy-start(bf16[32,1024]{1,0:T(8,128)(2,1)} %param.28) | copy-start | bytes 196612
  10.4 34.4 %copy-start.10 = (bf16[128,1024]{1,0:T(8,128)(2,1)S(1)}, bf16[128,1024]{1,0:T(8,128)(2,1)}, u32[]{:S(2)}) copy-start(bf16[128,1024]{1,0:T(8,128)(2,1)} %param.24) | copy-start | bytes 786436
  11.4 34.4 %copy-start.20 = (bf16[32,2]{0,1:T(2,128)(2,1)S(1)}, bf16[32,2]{0,1:T(2,128)(2,1)}, u32[]{:S(2)}) copy-start(bf16[32,2]{0,1:T(2,128)(2,1)} %param.35) | copy-start | bytes 388
  11.4 34.4 %copy-start.21 = (bf16[32,2]{0,1:T(2,128)(2,1)S(1)}, bf16[32,2]{0,1:T(2,128)(2,1)}, u32[]{:S(2)}) copy-start(bf16[32,2]{0,1:T(2,128)(2,1)} %param.36) | copy-start | bytes 388
  11.4 34.4 %copy-start.22 = (bf16[32]{0:T(256)(128)(2,1)S(1)}, bf16[32]{0:T(256)(128)(2,1)}, u32[]{:S(2)}) copy-start(bf16[32]{0:T(256)(128)(2,1)} %param.25) | copy-start | bytes 196
  11.5 34.4 %copy-start.23 = (bf16[32]{0:T(256)(128)(2,1)S(1)}, bf16[32]{0:T(256)(128)(2,1)}, u32[]{:S(2)}) copy-start(bf16[32]{0:T(256)(128)(2,1)} %param.26) | copy-start | bytes 196
  11.5 34.4 %copy-start.24 = (bf16[32]{0:T(256)(128)(2,1)S(1)}, bf16[32]{0:T(256)(128)(2,1)}, u32[]{:S(2)}) copy-start(bf16[32]{0:T(256)(128)(2,1)} %param.31) | copy-start | bytes 196
  11.5 34.4 %copy-start.25 = (bf16[32]{0:T(256)(128)(2,1)S(1)}, bf16[32]{0:T(256)(128)(2,1)}, u32[]{:S(2)}) copy-start(bf16[32]{0:T(256)(128)(2,1)} %param.32) | copy-start | bytes 196
  11.5 100.3 %copy-start.28 = (s32[1,128]{1,0:T(1,128)S(1)}, s32[1,128]{1,0:T(1,128)}, u32[]{:S(2)}) copy-start(s32[1,128]{1,0:T(1,128)} %param.21) | copy-start | bytes 1540
  41.5 90.3 %all-gather.8.cloned.1.call-start = ((), (), s32[]{:S(2)}) async-start(), calls=%async_computation.1 | async-start | bytes 8650752 | tf_op jit(solution)/shard_map/all_gather | solution.py:432
  42.4 104.1 %all-gather.10.cloned.1.call-start = ((), (), s32[]{:S(2)}) async-start(), calls=%async_computation.2 | async-start | bytes 2359296 | tf_op jit(solution)/shard_map/all_gather | solution.py:441
  43.4 179.6 %all-gather.12.cloned.1.call-start = ((), (), s32[]{:S(2)}) async-start(), calls=%async_computation.3 | async-start | bytes 4456448 | tf_op jit(solution)/shard_map/all_gather | solution.py:43
  45.8 455.3 %all-reduce.6.cloned.1.call-start = ((), (), s32[]{:S(2)}) async-start(), calls=%async_computation.5 | async-start | bytes 16777216
  223.0 223.5 %copy-start.4 = (bf16[128,1024]{1,0:T(8,128)(2,1)S(1)}, bf16[128,1024]{1,0:T(8,128)(2,1)}, u32[]{:S(2)}) copy-start(bf16[128,1024]{1,0:T(8,128)(2,1)} %convolution_convert_fusion.5) | copy-start | bytes 786436
  462.2 215.2 %all-reduce.8.cloned.1.call-start = ((), (), s32[]{:S(2)}) async-start(), calls=%async_computation.6 | async-start | bytes 8388608
  506.6 45.4 %copy-start.30 = (u32[32]{0:T(128)S(1)}, u32[32]{0:T(128)}, u32[]{:S(2)}) copy-start(u32[32]{0:T(128)} %constant.64) | copy-start | bytes 388
  506.6 46.0 %copy-start.29 = (f32[2]{0:T(128)S(1)}, f32[2]{0:T(128)}, u32[]{:S(2)}) copy-start(f32[2]{0:T(128)} %param.39) | copy-start | bytes 28
  562.9 48.2 %copy-start.9 = (f32[128,1024]{1,0:T(8,128)S(1)}, f32[128,1024]{1,0:T(8,128)}, u32[]{:S(2)}) copy-start(f32[128,1024]{1,0:T(8,128)} %get-tuple-element.24) | copy-start | bytes 1572868
  562.9 49.2 %copy-start.3 = (f32[128,1024]{1,0:T(8,128)S(1)}, f32[128,1024]{1,0:T(8,128)}, u32[]{:S(2)}) copy-start(f32[128,1024]{1,0:T(8,128)} %copy-done.2) | copy-start | bytes 1572868
  565.4 118.5 %copy-start.1 = (bf16[128,1024]{1,0:T(8,128)(2,1)S(1)}, bf16[128,1024]{1,0:T(8,128)(2,1)}, u32[]{:S(2)}) copy-start(bf16[128,1024]{1,0:T(8,128)(2,1)} %param.20) | copy-start | bytes 786436
  (15 other events, 214.4 us)
Sparse Core Ops, SparseCore 0:
  41.7 7.5 all-gather.13
  52.7 79.0 all-gather.7
  134.0 8.4 all-gather.9
  145.7 77.2 all-gather.11
  462.3 38.6 all-reduce.5
  506.7 170.5 all-reduce.7

commit v3 on v2

--- a/solution.py
+++ b/solution.py
@@ -395,7 +395,405 @@
     )(h2b, scal, dy_all, ups, downs)
 
 
-def body(
+def tree_gather(at, own, ss, rs, dev, levels):
+    core, z, p, xq, yq, dq = dev
+    xn, yn = z * 4 + xq, z * 4 + yq
+    me = z * 4 + p
+    lev_of, L = levels
+
+    def copy(kind, slot, src, idx, to):
+        return remote(src, at(idx), ss.at[kind, slot], rs.at[kind, slot], (core, to))
+
+    class Stages:
+        @staticmethod
+        def start():
+            @pl.loop(1, L)
+            def _(k):
+                lev = lev_of(k)
+                remote(own, at(me), ss.at[0, lev], rs.at[0, z], (core, lev * 4 + p)).start()
+
+            copy(1, z, own, me, xn).start()
+            copy(2, z, own, me, yn).start()
+
+        @staticmethod
+        def a(k):
+            lev = lev_of(k)
+            idx = lev * 4 + p
+            copy(0, lev, own, idx, xn).wait_recv()
+            copy(1, lev, at(idx), idx, xn).start()
+            copy(2, lev, at(idx), idx, yn).start()
+
+        @staticmethod
+        def b(k):
+            lev = lev_of(k)
+            odd = k % 2
+            copy(1, lev, own, lev * 4 + xq, xn).wait_recv()
+            copy(2, lev, own, lev * 4 + yq, yn).wait_recv()
+            idx = lev * 4 + xq + odd * (yq - xq)
+            copy(3, lev, at(idx), idx, yn + odd * (xn - yn)).start()
+
+        @staticmethod
+        def c(k):
+            lev = lev_of(k)
+            copy(3, lev, own, lev * 4 + dq, xn).wait_recv()
+
+        @staticmethod
+        def finish():
+            @pl.loop(0, L)
+            def _(k):
+                lev = lev_of(k)
+                for kind in range(1, 4):
+                    copy(kind, lev, own, me, xn).wait_send()
+
+                @pl.when(k > 0)
+                def _():
+                    copy(0, lev, own, me, xn).wait_send()
+
+    return Stages
+
+
+def sort_matrix(ids_e, ids_s, T):
+    zero = ids_e == 0
+    n0 = jnp.sum(jnp.where(zero, 1.0, 0.0), axis=1, keepdims=True)
+    slot = ids_s.astype(F32)
+    pos = jnp.where(zero, slot, slot + n0)
+    sub = lax.broadcasted_iota(jnp.int32, (T, T), 0).astype(F32)
+    return jnp.where(sub == pos, 1.0, 0.0), n0
+
+
+def attn_kernel(
+    x_ref, dy_ref, doc_ref, e_ref, s_ref, small_ref, wq_ref, wk_ref, wv_ref, wo_ref,
+    wu_ref, eu_ref, wd_ref, ed_ref,
+    h2b_out, stat_out, scal_out, u1_out, u2_out, x1_out, dys_out, q_out, k_out, v_out, p_out, o_out,
+    small_out, count_out, w_out, dyall_out, up_out, dn_out,
+    wbuf, smallbuf, h1b, bias, xs, tmp,
+    ag_s, ag_r, sib_s, sib_r, sm_s, sm_r, loc,
+):
+    T, D = x_ref.shape
+    WR = wq_ref.shape[0]
+    FR = wd_ref.shape[0]
+    N = wbuf.shape[1]
+    S = N // 2
+    L = S // 4
+    me, core, z, p, xq, yq, dq = place_of()
+    xn = z * 4 + xq
+    sgn = 1 - 2 * (z // (L // 2))
+    my = core * S + me
+    sib = (1 - core, me)
+    greet(S, core)
+
+    def lev_of(k):
+        return (z + k * sgn + L) % L
+
+    dev, levels = (core, z, p, xq, yq, dq), (lev_of, L)
+
+    def w1_at(i):
+        return wbuf.at[pl.ds(0, 3), core * S + i]
+
+    def w2_at(i):
+        return wbuf.at[3, core * S + i]
+
+    w1 = tree_gather(w1_at, w1_at(me), ag_s.at[0], ag_r.at[0], dev, levels)
+    w2 = tree_gather(w2_at, w2_at(me), ag_s.at[1], ag_r.at[1], dev, levels)
+    dyg = tree_gather(lambda i: dyall_out.at[i], dys_out, ag_s.at[2], ag_r.at[2], dev, levels)
+
+    for i, w in enumerate((wq_ref, wk_ref, wv_ref, wo_ref)):
+        wbuf[i, my] = w[...]
+    w1.start()
+
+    perm, n0 = sort_matrix(e_ref[...], s_ref[...], T)
+    smallbuf[my, 0:8, :] = small_ref[...]
+    lane8 = lax.broadcasted_iota(jnp.int32, (8, 128), 1)
+    smallbuf[my, 8:16, :] = jnp.where(lane8 == 0, jnp.broadcast_to(n0, (8, 128)), 0.0)
+
+    @pl.loop(1, S)
+    def _(i):
+        remote(smallbuf.at[my], smallbuf.at[my], sm_s.at[0, i], sm_r.at[0], (core, (me + i) % S)).start()
+
+    def dn_own(e0, n, src):
+        dst = dn_out.at[pl.ds(e0, n), pl.ds(pl.multiple_of(core * FR, FR), FR), :]
+        return src, dst
+
+    d0 = dn_own(0, 1, wd_ref)
+    d0 = (wd_ref, dn_out.at[0, pl.ds(pl.multiple_of(core * FR, FR), FR), :])
+    d1 = dn_own(1, 2, ed_ref)
+    dn_copies = []
+    for j, (src, dst) in enumerate((d0, d1)):
+        r = remote(src, dst, sib_s.at[2, j], sib_r.at[2, j], sib)
+        lc = pltpu.make_async_copy(src, dst, loc.at[j])
+        r.start()
+        lc.start()
+        dn_copies.append((r, lc))
+
+    permb = perm.astype(BF)
+    xs[...] = mm(permb, x_ref[...])
+    dys_out[...] = mm(permb, dy_ref[...]).astype(BF)
+    dy_local = pltpu.make_async_copy(dys_out, dyall_out.at[me], loc.at[2])
+    dy_local.start()
+
+    docs = (doc_ref[...] == lax.broadcasted_iota(jnp.int32, (16, T), 0)).astype(F32).astype(BF)
+    docs = mm(docs, permb, ((1,), (1,))).astype(BF)
+    same = mm(docs, docs, ((0,), (0,)))
+    place = lax.broadcasted_iota(jnp.int32, (T, T), 1).astype(F32)
+    ord_col = jnp.sum(perm * place, axis=1, keepdims=True)
+    ord_row = mm(place[0:16, :].astype(BF), permb, ((1,), (1,)))[0:1, :]
+    bias[...] = jnp.where((same > 0.5) & (ord_row <= ord_col), 0.0, -1e30)
+
+    lane = lax.broadcasted_iota(jnp.int32, (16, 128), 1)
+
+    def norm1(r):
+        t = pl.ds(r, 16)
+        v = xs[t, :]
+        cen = v - jnp.mean(v, axis=1, keepdims=True)
+        inv = lax.rsqrt(jnp.mean(cen * cen, axis=1, keepdims=True) + 1e-05)
+        u1_out[t, :] = cen * inv
+        stat_out[t, :] = jnp.where(lane == 8, inv, 0.0)
+
+    rows_loop(T, 16, norm1)
+
+    w1.a(1)
+    w1.b(0)
+    w1.a(2)
+    w1.b(1)
+
+    group = 128 // WR
+    remote(smallbuf.at[pl.ds(0, S - 1)], smallbuf.at[pl.ds(0, S - 1)], sm_s.at[0, 0], sm_r.at[0], (core, xn)).wait_recv()
+    mine_small = smallbuf.at[pl.ds(core * S, S)]
+    c_small = remote(mine_small, mine_small, sib_s.at[2, 2], sib_r.at[2, 2], sib)
+    c_small.start()
+
+    def w1_sib(lev, who):
+        b = wbuf.at[pl.ds(0, 3), pl.ds(who * S + lev * 4, 4)]
+        return remote(b, b, sib_s.at[0, lev], sib_r.at[0, lev], sib)
+
+    def w2_sib(lev, who):
+        b = wbuf.at[3, pl.ds(who * S + lev * 4, 4)]
+        return remote(b, b, sib_s.at[1, lev], sib_r.at[1, lev], sib)
+
+    def c1(k):
+        w1.c(k)
+        w1_sib(lev_of(k), core).start()
+
+    def c2(k):
+        w2.c(k)
+        w2_sib(lev_of(k), core).start()
+
+    for k in range(3, L):
+        w1.a(k)
+    c1(0)
+    w2.start()
+    for k in range(2, L):
+        w1.b(k)
+        c1(k - 1)
+
+    def up_copy(e, h, i):
+        to = (me + i) % S
+        src = wu_ref if e == 0 else eu_ref.at[e - 1]
+        return remote(
+            src.at[:, pl.ds(pl.multiple_of((h * S + to) * FR, FR), FR)],
+            up_out.at[e, pl.ds(pl.multiple_of(my * WR, WR), WR), pl.ds(h * FR, FR)],
+            sm_s.at[1, i], sm_r.at[1], (core, to),
+        )
+
+    def up_local(e, h):
+        src = wu_ref if e == 0 else eu_ref.at[e - 1]
+        return pltpu.make_async_copy(
+            src.at[:, pl.ds(pl.multiple_of((h * S + me) * FR, FR), FR)],
+            up_out.at[e, pl.ds(pl.multiple_of(my * WR, WR), WR), pl.ds(h * FR, FR)],
+            loc.at[4 + 2 * e + h],
+        )
+
+    @pl.loop(1, S)
+    def _(i):
+        for e in range(3):
+            for h in range(2):
+                up_copy(e, h, i).start()
+
+    for e in range(3):
+        for h in range(2):
+            up_local(e, h).start()
+
+    c_small.wait_recv()
+    for g in range(D // 128):
+        part = smallbuf[g * group, 0:8, :]
+        for j in range(1, group):
+            part = part + smallbuf[g * group + j, 0:8, :]
+        small_out[:, g * 128 : (g + 1) * 128] = part
+    cnt = smallbuf[0, 8:16, :]
+    for i in range(1, N):
+        cnt = cnt + smallbuf[i, 8:16, :]
+    count_out[...] = cnt
+
+    def norm1b(r):
+        t = pl.ds(r, 16)
+        h1b[t, :] = (u1_out[t, :] * small_out[0:1, :] + small_out[1:2, :]).astype(BF)
+
+    rows_loop(T, 16, norm1b)
+    c1(L - 1)
+    w2.a(1)
+    w2.b(0)
+    for k in range(L):
+        w1_sib(lev_of(k), 1 - core).wait_recv()
+
+    def full(i):
+        return wbuf[i].reshape(D, D)
+
+    tmp[...] = mm(h1b[...], full(0))
+    q_out[...] = (tmp[...] * 0.125).astype(BF)
+    for k in range(2, L):
+        w2.a(k)
+    w2.b(1)
+    tmp[...] = mm(h1b[...], full(1))
+    k_out[...] = tmp[...].astype(BF)
+    c2(0)
+    dyg.start()
+    for k in range(2, L):
+        w2.b(k)
+        c2(k - 1)
+    tmp[...] = mm(h1b[...], full(2))
+    v_out[...] = tmp[...].astype(BF)
+    c2(L - 1)
+    dyg.a(1)
+    dyg.b(0)
+
+    low = lax.broadcasted_iota(jnp.int32, (T, 128), 1) < 64
+    lowb = low.astype(F32).astype(BF)
+    highb = (1.0 - low.astype(F32)).astype(BF)
+
+    def heads(j):
+        ln = pl.ds(pl.multiple_of(j * 128, 128), 128)
+        qp = q_out[:, ln]
+        q2 = jnp.concatenate([qp * lowb, qp * highb], axis=0)
+        s = mm(q2, k_out[:, ln], ((1,), (1,)))
+        s = s + jnp.concatenate([bias[...], bias[...]], axis=0)
+        ex = jnp.exp(s - jnp.max(s, axis=1, keepdims=True))
+        pr = ex / jnp.sum(ex, axis=1, keepdims=True)
+        p_out[j] = pr
+        o2 = mm(pr.astype(BF), v_out[:, ln])
+        o_out[:, ln] = jnp.where(low, o2[0:T], o2[T:]).astype(BF)
+
+    half = D // 256
+
+    @pl.loop(0, half)
+    def _(j):
+        heads(j)
+
+    dyg.a(2)
+    dyg.b(1)
+
+    @pl.loop(half, 2 * half)
+    def _(j):
+        heads(j)
+
+    for k in range(3, L):
+        dyg.a(k)
+    for k in range(L):
+        w2_sib(lev_of(k), 1 - core).wait_recv()
+    w_save = pltpu.make_async_copy(wbuf, w_out, loc.at[3])
+    w_save.start()
+    tmp[...] = mm(o_out[...], full(3))
+
+    def norm2(r):
+        t = pl.ds(r, 16)
+        v = xs[t, :] + tmp[t, :]
+        x1_out[t, :] = v
+        cen = v - jnp.mean(v, axis=1, keepdims=True)
+        inv = lax.rsqrt(jnp.mean(cen * cen, axis=1, keepdims=True) + 1e-05)
+        u = cen * inv
+        u2_out[t, :] = u
+        h2 = u * small_out[2:3, :] + small_out[3:4, :]
+        h2b_out[t, :] = h2.astype(BF)
+        lg = [jnp.sum(h2 * small_out[i : i + 1, :], axis=1, keepdims=True) for i in range(4, 8)]
+
+        def soft(a, b):
+            mx = jnp.maximum(a, b)
+            ea, eb = jnp.exp(a - mx), jnp.exp(b - mx)
+            return ea / (ea + eb), eb / (ea + eb)
+
+        r0, r1 = soft(lg[0], lg[1])
+        k0, k1 = soft(lg[2], lg[3])
+        row = (lax.broadcasted_iota(jnp.int32, (16, 1), 0) + r).astype(F32)
+        is0 = row < n0
+        gate = jnp.where(is0, r0, r1)
+        we = k0 * gate
+        cols = (k1, jnp.where(is0, we, 0.0), jnp.where(is0, 0.0, we), k0, gate, r0, r1)
+        st = stat_out[t, :] + jnp.where(lane == 9, inv, 0.0)
+        for i, col in enumerate(cols):
+            st = st + jnp.where(lane == i, col, 0.0)
+        stat_out[t, :] = st
+
+    rows_loop(T, 16, norm2)
+    scal_out[...] = stat_out[...].T[0:8, :]
+
+    for k in range(2, L):
+        dyg.b(k)
+    for k in range(L):
+        dyg.c(k)
+
+    got = up_out.at[:, pl.ds(0, (S - 1) * WR), :]
+    remote(got, got, sm_s.at[1, 0], sm_r.at[1], (core, xn)).wait_recv()
+    for e in range(3):
+        for h in range(2):
+            up_local(e, h).wait()
+    mine_up = up_out.at[:, pl.ds(pl.multiple_of(core * S * WR, S * WR), S * WR), :]
+    c_up = remote(mine_up, mine_up, sib_s.at[2, 3], sib_r.at[2, 3], sib)
+    c_up.start()
+    c_up.wait()
+    w_save.wait()
+    dy_local.wait()
+    for r, lc in dn_copies:
+        r.wait()
+        lc.wait()
+    c_small.wait_send()
+    w1.finish()
+    w2.finish()
+    dyg.finish()
+
+    @pl.loop(0, L)
+    def _(k):
+        w1_sib(k, core).wait_send()
+        w2_sib(k, core).wait_send()
+
+    @pl.loop(1, S)
+    def _(i):
+        remote(smallbuf.at[my], smallbuf.at[my], sm_s.at[0, i], sm_r.at[0], (core, xn)).wait_send()
+        for e in range(3):
+            for h in range(2):
+                up_copy(e, h, i).wait_send()
+
+
+def attn_call(x, dy, docs, es, ss, small, ws, wu, eu, wd, ed, S):
+    T, D = x.shape
+    WR, FR = ws[0].shape[0], wd.shape[0]
+    L = S // 4
+    N = 2 * S
+    vm = pl.BlockSpec(memory_space=pltpu.VMEM)
+    hb = pl.BlockSpec(memory_space=pl.ANY)
+    V = pltpu.VMEM
+    dma = pltpu.SemaphoreType.DMA
+    sds = jax.ShapeDtypeStruct
+    row = sds((T, D), BF)
+    rowf = sds((T, D), F32)
+    return pl.pallas_call(
+        attn_kernel,
+        out_shape=(
+            row, sds((T, 128), F32), sds((8, T), F32), rowf, rowf, rowf, row, row, row, row,
+            sds((D // 128, 2 * T, T), F32), row, sds((8, D), F32), sds((8, 128), F32),
+            sds((4, N, WR, D), BF), sds((S, T, D), BF), sds((3, D, 2 * FR), BF), sds((3, 2 * FR, D), BF),
+        ),
+        in_specs=[vm] * 10 + [hb] * 4,
+        out_specs=(vm,) * 14 + (hb,) * 4,
+        scratch_shapes=[
+            V((4, N, WR, D), BF), V((N, 16, 128), F32), V((T, D), BF), V((T, T), F32), V((T, D), F32), V((T, D), F32),
+            dma((3, 4, L)), dma((3, 4, L)), dma((3, max(L, 4))), dma((3, max(L, 4))), dma((2, S)), dma((2,)), dma((10,)),
+        ],
+        compiler_params=pltpu.CompilerParams(collective_id=1, has_side_effects=True, vmem_limit_bytes=60000000),
+        cost_estimate=pl.CostEstimate(flops=2 * 10**9, bytes_accessed=40 * 2**20, transcendentals=2**20),
+        name="attn",
+    )(x, dy, docs, es, ss, small, *ws, wu, eu, wd, ed)
+
+
+def body_plain(
     hidden_in, doc_ids, expert_ids, slot_ids, out_grad, ln1_gain, ln1_bias, w_query, w_key, w_value,
     w_out, ln2_gain, ln2_bias, w_up, w_down, w_router, w_mix, expert_up, expert_down, load_avg,
 ):
@@ -467,47 +865,135 @@
     we = c0 * gate
     scal = jnp.concatenate([c1, jnp.where(is0, we, 0.0), jnp.where(is0, 0.0, we)], axis=1)
 
-    fast = C == 2 and S % 4 == 0 and S >= 8 and FR % 128 == 0 and WR % 16 == 0
-    if fast:
-        scal8 = jnp.pad(scal.T, ((0, 5), (0, 0)))
-        yfull, dh2, sc, gup, gdn0, gdn12 = ffn_call(h2b, scal8, dy_all, ups, downs)
-    else:
-        h_all = ag(h2b)
-        scal_all = ag(scal)
-
-        def cut(a, e):
-            return (a[:, :LO] if e == 1 else a[:, HI:]) if e else a
-
-        partial_y = jnp.zeros((S, T, D), F32)
-        partial_dh = jnp.zeros((S, T, D), F32)
-        score = []
-        gup, gdown = [], []
-        for e in range(3):
-            he = cut(h_all, e)
-            dye = cut(dy_all, e).astype(F32)
-            se = cut(scal_all, e)[:, :, e : e + 1]
-            n = he.shape[1]
-            hf = he.reshape(S * n, D)
-            pre = mm(hf, ups[e])
-            val, der = gelu_pair(pre)
-            ub = val.astype(BF)
-            m = mm(ub, downs[e]).reshape(S, n, D)
-            dm = (dye * se).astype(BF).reshape(S * n, D)
-            dg = (mm(dm, downs[e], ((1,), (1,))) * der).astype(BF)
-            gdown.append(mm(ub, dm, ((0,), (0,))))
-            gup.append(mm(hf, dg, ((0,), (0,))))
-            dx = mm(dg, ups[e], ((1,), (1,))).reshape(S, n, D)
-            y = m * se
-            sc = jnp.sum(dye * m, axis=-1)
-            pad = [(0, 0), (0, T - n) if e < 2 else (T - n, 0)]
-            live = is0[None, :, 0]
-            partial_y += jnp.pad(y, pad + [(0, 0)])
-            partial_dh += jnp.pad(dx, pad + [(0, 0)])
-            score.append(jnp.pad(sc, pad))
-        yfull = rs(partial_y)
-        dh2 = rs(partial_dh)
-        sc = lax.psum_scatter(jnp.stack(score, axis=1), "shard", scatter_dimension=0, tiled=False)
-
+    h_all = ag(h2b)
+    scal_all = ag(scal)
+
+    def cut(a, e):
+        return (a[:, :LO] if e == 1 else a[:, HI:]) if e else a
+
+    partial_y = jnp.zeros((S, T, D), F32)
+    partial_dh = jnp.zeros((S, T, D), F32)
+    score = []
+    gup, gdown = [], []
+    for e in range(3):
+        he = cut(h_all, e)
+        dye = cut(dy_all, e).astype(F32)
+        se = cut(scal_all, e)[:, :, e : e + 1]
+        n = he.shape[1]
+        hf = he.reshape(S * n, D)
+        pre = mm(hf, ups[e])
+        val, der = gelu_pair(pre)
+        ub = val.astype(BF)
+        m = mm(ub, downs[e]).reshape(S, n, D)
+        dm = (dye * se).astype(BF).reshape(S * n, D)
+        dg = (mm(dm, downs[e], ((1,), (1,))) * der).astype(BF)
+        gdown.append(mm(ub, dm, ((0,), (0,))))
+        gup.append(mm(hf, dg, ((0,), (0,))))
+        dx = mm(dg, ups[e], ((1,), (1,))).reshape(S, n, D)
+        y = m * se
+        sc = jnp.sum(dye * m, axis=-1)
+        pad = [(0, 0), (0, T - n) if e < 2 else (T - n, 0)]
+        live = is0[None, :, 0]
+        partial_y += jnp.pad(y, pad + [(0, 0)])
+        partial_dh += jnp.pad(dx, pad + [(0, 0)])
+        score.append(jnp.pad(sc, pad))
+    yfull = rs(partial_y)
+    dh2 = rs(partial_dh)
+    sc = lax.psum_scatter(jnp.stack(score, axis=1), "shard", scatter_dimension=0, tiled=False)
+    sm = sc[0][:, None]
+    se = jnp.where(is0, sc[1][:, None], sc[2][:, None])
+
+    dc0, dc1 = gate * se, sm
+    tot = c0 * dc0 + c1 * dc1
+    dcl0, dcl1 = c0 * (dc0 - tot), c1 * (dc1 - tot)
+    dgate = c0 * se
+    dr0, dr1 = jnp.where(is0, dgate, 0.0), jnp.where(is0, 0.0, dgate)
+    tot = r[:, 0:1] * dr0 + r[:, 1:2] * dr1
+    drl0, drl1 = r[:, 0:1] * (dr0 - tot), r[:, 1:2] * (dr1 - tot)
+    layer_out = (x1 + yfull).astype(BF)
+    dh2 = dh2 + drl0 * wr[0] + drl1 * wr[1] + dcl0 * wm[0] + dcl1 * wm[1]
+    gw = [jnp.sum(h2 * t, axis=0) for t in (drl0, drl1, dcl0, dcl1)]
+    dx1, gg2, gb2 = norm_back(dh2, u2, i2, g2)
+    dx1 = dx1 + dys.astype(F32)
+    dab = dx1.astype(BF)
+    gwo = mm(o, dab, ((0,), (0,)))
+    do = mm(dab, wo, ((1,), (1,))).astype(BF).reshape(T, H, HD)
+    dp = jnp.einsum("ihd,jhd->hij", do, v, preferred_element_type=F32)
+    ds = (p * (dp - jnp.sum(p * dp, axis=-1, keepdims=True))).astype(BF)
+    dq = jnp.einsum("hij,jhd->ihd", ds, k, preferred_element_type=F32).astype(BF)
+    dq = (dq * BF(0.125)).reshape(T, D)
+    dk = jnp.einsum("hij,ihd->jhd", ds, q, preferred_element_type=F32).astype(BF).reshape(T, D)
+    dv = jnp.einsum("hij,ihd->jhd", pb, do, preferred_element_type=F32).astype(BF).reshape(T, D)
+    dh1 = mm(dq, wq, ((1,), (1,))) + mm(dk, wk, ((1,), (1,))) + mm(dv, wv, ((1,), (1,)))
+    ga = jnp.stack([mm(h1b, dq, ((0,), (0,))), mm(h1b, dk, ((0,), (0,))), mm(h1b, dv, ((0,), (0,))), gwo])
+    dxn, gg1, gb1 = norm_back(dh1, u1, i1, g1)
+    input_grad = (dx1 + dxn).astype(BF)
+
+    layer_out = mm(perm, layer_out, ((0,), (0,))).astype(BF)
+    input_grad = mm(perm, input_grad, ((0,), (0,))).astype(BF)
+
+    smalls = lax.psum(jnp.stack([gg1, gb1, gg2, gb2] + gw), BOTH)
+    mine = lax.dynamic_slice_in_dim(smalls, lax.axis_index(BOTH) * WR, WR, 1)
+    ga = ga.reshape(4, C, S, WR, D).transpose(1, 2, 0, 3, 4)
+    ga = lax.psum_scatter(ga.astype(BF), "dp", scatter_dimension=0, tiled=False)
+    ga = lax.psum_scatter(ga, "shard", scatter_dimension=0, tiled=False).astype(F32)
+    gdown = lax.psum_scatter(jnp.stack(gdown), "dp", scatter_dimension=1, tiled=True)
+    gup = jnp.stack(gup).reshape(3, C, S, WR, F).transpose(1, 2, 0, 3, 4)
+    gup = lax.psum_scatter(gup, "dp", scatter_dimension=0, tiled=False).astype(BF)
+    gup = lax.all_to_all(gup, "shard", 0, 0).astype(F32)
+    gup = gup.reshape(S, 3, WR, C, FR).transpose(1, 2, 3, 0, 4).reshape(3, WR, FF)
+
+    counts = lax.psum(jnp.stack([n0, T - n0]), BOTH)
+    load_new = 0.9 * load_avg + 0.1 * counts.astype(F32) * E / (T * C * S)
+    return (
+        layer_out, input_grad, mine[0], mine[1], ga[0], ga[1], ga[2], ga[3], mine[2], mine[3],
+        gup[0], gdown[0], jnp.stack([mine[4], mine[5]], axis=1), jnp.stack([mine[6], mine[7]], axis=1),
+        gup[1:], gdown[1:], counts, load_new,
+    )
+
+
+def body(
+    hidden_in, doc_ids, expert_ids, slot_ids, out_grad, ln1_gain, ln1_bias, w_query, w_key, w_value,
+    w_out, ln2_gain, ln2_bias, w_up, w_down, w_router, w_mix, expert_up, expert_down, load_avg,
+):
+    T, D = hidden_in.shape
+    H, HD = HEADS, D // HEADS
+    S = lax.axis_size("shard")
+    C = lax.axis_size("dp")
+    WR = w_query.shape[0]
+    FF = w_up.shape[1]
+    FR = w_down.shape[0]
+    F = FR * C
+    E = expert_up.shape[0]
+    ndev = C * S
+    dev = lax.axis_index(BOTH)
+    small = jnp.stack(
+        [ln1_gain, ln1_bias, ln2_gain, ln2_bias, w_router[:, 0], w_router[:, 1], w_mix[:, 0], w_mix[:, 1]]
+    ).astype(F32)
+    group = 128 // WR
+    slot_of = lax.broadcasted_iota(jnp.int32, (8, 128), 1) // WR
+    small = jnp.where(slot_of == dev % group, jnp.tile(small, (1, group)), 0.0)
+    (h2b, stat, scal8, u1, u2, x1, dys, q, k, v, p, o, small, count, wa, dy_all, ups, downs) = attn_call(
+        hidden_in, out_grad, doc_ids, expert_ids.reshape(1, T), slot_ids.reshape(1, T), small,
+        (w_query, w_key, w_value, w_out), w_up, expert_up, w_down, expert_down, S,
+    )
+    wa = wa.reshape(4, D, D)
+    wq, wk, wv, wo = wa[0], wa[1], wa[2], wa[3]
+    g1, b1, g2, b2 = small[0], small[1], small[2], small[3]
+    wr, wm = small[4:6], small[6:8]
+    place = lax.iota(jnp.int32, T)
+    n0 = jnp.sum((expert_ids == 0).astype(jnp.int32))
+    pos = jnp.where(expert_ids == 0, slot_ids, n0 + slot_ids)
+    perm = (pos[None, :] == place[:, None]).astype(BF)
+    is0 = (place < n0)[:, None]
+    i1, i2 = stat[:, 8:9], stat[:, 9:10]
+    c0, c1, gate, r = stat[:, 3:4], stat[:, 0:1], stat[:, 4:5], stat[:, 5:7]
+    h1b = (u1 * g1 + b1).astype(BF)
+    h2 = u2 * g2 + b2
+    p = p.reshape(H, T, T)
+    pb = p.astype(BF)
+    q, k, v = q.reshape(T, H, HD), k.reshape(T, H, HD), v.reshape(T, H, HD)
+    yfull, dh2, sc, gup, gdn0, gdn12 = ffn_call(h2b, scal8, dy_all, ups, downs)
     sm = sc[0][:, None]
     se = jnp.where(is0, sc[1][:, None], sc[2][:, None])
     dc0, dc1 = gate * se, sm
@@ -544,17 +1030,11 @@
     ga = ga.reshape(4, C, S, WR, D).transpose(1, 2, 0, 3, 4)
     ga = lax.psum_scatter(ga.astype(BF), "dp", scatter_dimension=0, tiled=False)
     ga = lax.psum_scatter(ga, "shard", scatter_dimension=0, tiled=False).astype(F32)
-    if not fast:
-        gdown = lax.psum_scatter(jnp.stack(gdown), "dp", scatter_dimension=1, tiled=True)
-        gdn0, gdn12 = gdown[0], gdown[1:]
-        gup = jnp.stack(gup).reshape(3, C, S, WR, F)
-        gup = gup.transpose(1, 2, 0, 3, 4)
-        gup = lax.psum_scatter(gup, "dp", scatter_dimension=0, tiled=False).astype(BF)
-        gup = lax.all_to_all(gup, "shard", 0, 0)
     gup = gup.astype(F32)
     gup = gup.reshape(S, 3, WR, C, FR).transpose(1, 2, 3, 0, 4).reshape(3, WR, FF)
 
-    counts = lax.psum(jnp.stack([n0, T - n0]), BOTH)
+    tokens0 = count[0, 0].astype(jnp.int32)
+    counts = jnp.stack([tokens0, T * ndev - tokens0])
     load_new = 0.9 * load_avg + 0.1 * counts.astype(F32) * E / (T * C * S)
     return (
         layer_out, input_grad, mine[0], mine[1], ga[0], ga[1], ga[2], ga[3], mine[2], mine[3],
@@ -563,11 +1043,17 @@
     )
 
 
+def pick(*args):
+    S, C, WR, FR = lax.axis_size("shard"), lax.axis_size("dp"), args[7].shape[0], args[14].shape[0]
+    fast = C == 2 and S % 4 == 0 and S >= 8 and WR % 16 == 0 and 128 % WR == 0 and FR % 128 == 0
+    return (body if fast else body_plain)(*args)
+
+
 def solution(mesh):
     row, vec = P(BOTH, None), P(BOTH)
     mid = P(None, BOTH, None)
     return jax.shard_map(
-        body,
+        pick,
         mesh=mesh,
         in_specs=(row, row, vec, vec, row, vec, vec, row, row, row, row, vec, vec, row, row, row, row, mid, mid, P()),
         out_specs=(row, row, vec, vec, row, row, row, row, vec, vec, row, row, row, row, mid, mid, P(), P()),

time: 692 us -> 606 us (0.88)
  blocking collectives: 180 us -> 43.3 us
  Pallas kernels: 218 us -> 340 us
  waiting for transfers between devices: 194 us -> 149 us
  matrix products: 32 us -> 10.7 us
  other arithmetic: 20.7 us -> 13.1 us
    pallas_call x0 -> x1, Pallas kernels: none -> 112 us  [attn_call(): pl.pallas_call(attn_kernel, out_shape=(row, sds((T, 128), F32), sds((8, T...]
    all_gather x4 -> x0, waiting for transfers between devices: 92.5 us -> none  [the longest x1 76.5 us: ag(): return lax.all_gather(block, 'shard', axis=0, tiled=False)]
    all_gather x1 -> x0, blocking collectives: 65.7 us -> none  [body(): small = lax.all_gather(small, BOTH, axis=1, tiled=True)]
    unnamed x8 -> x4, waiting for transfers between devices: 102 us -> 149 us
    psum x1 -> x0, blocking collectives: 44 us -> none  [body(): counts = lax.psum(jnp.stack([n0, T - n0]), BOTH)]
    all_to_all x1 -> x0, blocking collectives: 29.5 us -> none  [body(): ups = lax.all_to_all(ups, 'shard', 0, 0)]
    dot_general x17 -> x10, matrix products: 26 us -> 9.31 us  [mm(): return lax.dot_general(a, b, (dims, ((), ())), preferred_element_type=F32)]
    pallas_call x1, Pallas kernels: 218 us -> 228 us  [ffn_call(): pl.pallas_call(ffn_kernel, out_shape=(sds((T, D), F32), sds((T, D), F32),...]
  transfers between devices with their start and end apart: 6 -> 2, of which waited for: 4 -> 2; matrix products, arithmetic and copies ran while one was open for 6% -> 2% of each run, Pallas kernels for 0% -> 0%
where the time goes in v3:
time: 606 us; the launch traced here: 605 us
  Pallas kernels  340 us (56%)
  waiting for transfers between devices  149 us (25%)
  blocking collectives  43.3 us (7%)
  local copies, waits for them, and re-layouts  33.1 us (5%)
  between operations  15.1 us (2%)
  other arithmetic  13.1 us (2%)
  matrix products  10.7 us (2%)
    pallas_call x1, Pallas kernels, ffn_call(): pl.pallas_call(ffn_kernel, out_shape=(sds((T, D), F32), sds((T, D), F32),...  228 us
    unnamed x4, waiting for transfers between devices  149 us
    pallas_call x1, Pallas kernels, attn_call(): pl.pallas_call(attn_kernel, out_shape=(row, sds((T, 128), F32), sds((8, T...  112 us
    psum x1, blocking collectives, body(): smalls = lax.psum(jnp.stack([gg1, gb1, gg2, gb2] + gw), BOTH)  43.3 us
  transfers between devices with their start and end apart: 2, of which 2 were waited for; matrix products, arithmetic and copies ran while one was open for 2% of the time, Pallas kernels for 0%

profile of v3, /device:TPU:0, one launch (start us, length us, event | category | flops | bytes accessed | tf_op | source)
XLA Modules:
  0.0 605.3 jit_solution(6947309370328285071)
XLA Ops:
  8.8 1.3 fusion.15
  10.7 112.0 %attn.1 = (bf16[128,1024]{1,0:T(8,128)(2,1)}, f32[128,128]{1,0:T(8,128)}, f32[8,128]{1,0:T(8,128)}, f32[128,1024]{1,0:T(8,128)}, f32[128,1024]{1,0:T(8,128)}, /*...) custom-call(bf16[128,1024]{1,0:T(8,128)(2,1)} %x_ref.1, ...), custom_call_target="tpu_custom_call" | custom-call | flops 2000000000 | bytes 41943040 | tf_op jit(solution)/shard_map/attn/pallas_call | solution.py:777
  122.8 228.3 %ffn.1 = (f32[128,1024]{1,0:T(8,128)}, f32[128,1024]{1,0:T(8,128)}, f32[8,128]{1,0:T(8,128)}, bf16[16,3,32,256]{3,2,1,0:T(8,128)(2,1)}, f32[128,1024]{1,0:T(8,128)}, /*index=5*/f32[2,128,1024]{2,1,0:T(8,128)}) custom-call(bf16[128,1024]{1,0:T(8,128)(2,1)} %get-tuple-element.43.h_ref, f32[8,128]{1,0:T(8,128)} %get-tuple-element.44.scal_ref, ...), custom_call_target="tpu_custom_call" | custom-call | flops 15000000512 | bytes 20971520 | tf_op jit(solution)/shard_map/ffn/pallas_call | solution.py:373
  352.2 1.0 multiply_reduce_fusion.12
  353.2 1.7 multiply_reduce_fusion.1
  354.9 5.8 fusion.16
  362.8 1.1 copy.101
  363.9 1.1 copy.105
  365.0 1.1 copy.99
  375.0 3.8 maximum_bitcast_fusion
  380.0 37.8 %all-reduce.5.cloned.1.call-done = bf16[2,16,4,32,1024]{4,3,1,0,2:T(8,128)(2,1)} async-done(((bf16[2,16,4,32,1024]{4,3,1,0,2:T(8,128)(2,1)}), bf16[2,16,4,32,1024]{4,3,1,0,2:T(8,128)(2,1)}) %all-reduce.5.cloned.1.call-update) | async-done | bytes 8388624
  417.8 5.6 dynamic-slice_bitcast_fusion
  423.5 1.1 copy-done.9
  425.4 1.0 slice.193
  427.0 1.2 slice.187
  428.9 1.8 copy.112
  430.8 1.2 slice.186
  432.2 0.9 squeeze.52
  433.2 43.3 %psum.7 = f32[8,1024]{1,0:T(8,128)S(1)} all-reduce(f32[8,1024]{1,0:T(8,128)S(1)} %stack.91), channel_id=1, replica_groups=mesh['dp'=2,'shard'=16] {'dp','shard'}, use_global_device_ids=true, to_apply=%region_14.15 | all-reduce | flops 8192 | bytes 65536 | tf_op jit(solution)/shard_map/psum | solution.py:1028
  479.6 2.0 convolution_convert_fusion.6
  481.6 1.1 convolution_convert_fusion.1
  482.7 111.6 %all-reduce.7.cloned.1.call-done = bf16[16,4,32,1024]{3,2,0,1:T(8,128)(2,1)} async-done(((bf16[16,4,32,1024]{3,2,0,1:T(8,128)(2,1)}), bf16[16,4,32,1024]{3,2,0,1:T(8,128)(2,1)}) %all-reduce.7.cloned.1.call-update) | async-done | bytes 4194320
  594.2 1.6 dynamic-slice_convert_fusion
  597.5 1.0 copy.130
  (91 shorter events, 21.7 us)
Async XLA Ops:
  7.2 410.6 %all-reduce.5.cloned.1.call-start = ((), (), s32[]{:S(2)}) async-start(), calls=%async_computation | async-start | bytes 16777216
  122.7 229.4 %copy-start.14 = (f32[8,1024]{1,0:T(8,128)S(1)}, f32[8,1024]{1,0:T(8,128)}, u32[]{:S(2)}) copy-start(f32[8,1024]{1,0:T(8,128)} %get-tuple-element.52) | copy-start | bytes 98308
  122.7 229.5 %copy-start.4 = (f32[128,128]{1,0:T(8,128)S(1)}, f32[128,128]{1,0:T(8,128)}, u32[]{:S(2)}) copy-start(f32[128,128]{1,0:T(8,128)} %get-tuple-element.49) | copy-start | bytes 196612
  122.8 230.4 %copy-start.7 = (f32[128,1024]{1,0:T(8,128)S(1)}, f32[128,1024]{1,0:T(8,128)}, u32[]{:S(2)}) copy-start(f32[128,1024]{1,0:T(8,128)} %get-tuple-element.53) | copy-start | bytes 1572868
  354.9 5.8 copy-start.13
  360.9 1.2 copy-start.3
  366.5 1.6 copy-start
  367.2 1.8 copy-start.2
  368.9 1.6 copy-start.1
  369.8 1.6 copy-start.5
  373.3 1.0 copy-start.12
  378.8 0.7 copy-start.19
  378.8 215.4 %all-reduce.7.cloned.1.call-start = ((), (), s32[]{:S(2)}) async-start(), calls=%async_computation.1 | async-start | bytes 8388608
  423.4 1.1 copy-start.9
  425.3 1.1 copy-start.18
  430.7 47.6 %copy-start.16 = (s32[128]{0:T(128)S(1)}, s32[128]{0:T(128)}, u32[]{:S(2)}) copy-start(s32[128]{0:T(128)} %param.22) | copy-start | bytes 1540
  430.7 47.6 %copy-start.17 = (s32[128]{0:T(128)S(1)}, s32[128]{0:T(128)}, u32[]{:S(2)}) copy-start(s32[128]{0:T(128)} %param.23) | copy-start | bytes 1540
  430.8 48.2 %copy-start.15 = (f32[2]{0:T(128)S(1)}, f32[2]{0:T(128)}, u32[]{:S(2)}) copy-start(f32[2]{0:T(128)} %param.39) | copy-start | bytes 28
  430.8 48.8 %copy-start.10 = (f32[128,1024]{1,0:T(8,128)S(1)}, f32[128,1024]{1,0:T(8,128)}, u32[]{:S(2)}) copy-start(f32[128,1024]{1,0:T(8,128)} %get-tuple-element.42) | copy-start | bytes 1572868
  431.9 49.7 %copy-start.6 = (f32[128,1024]{1,0:T(8,128)S(1)}, f32[128,1024]{1,0:T(8,128)}, u32[]{:S(2)}) copy-start(f32[128,1024]{1,0:T(8,128)} %get-tuple-element.60) | copy-start | bytes 1572868
  481.6 115.1 %copy-start.11 = (f32[128,1024]{1,0:T(8,128)S(1)}, f32[128,1024]{1,0:T(8,128)}, u32[]{:S(2)}) copy-start(f32[128,1024]{1,0:T(8,128)} %get-tuple-element.156) | copy-start | bytes 1572868
  481.6 115.9 %copy-start.8 = (f32[2,128,1024]{2,1,0:T(8,128)S(1)}, f32[2,128,1024]{2,1,0:T(8,128)}, u32[]{:S(2)}) copy-start(f32[2,128,1024]{2,1,0:T(8,128)} %get-tuple-element.160) | copy-start | bytes 3145732
Sparse Core Ops, SparseCore 0:
  378.9 38.8 all-reduce.4
  423.6 170.5 all-reduce.6

commit v4 on v3

--- a/solution.py
+++ b/solution.py
@@ -793,6 +793,316 @@
     )(x, dy, docs, es, ss, small, *ws, wu, eu, wd, ed)
 
 
+def tree_scatter(part, ra, rbx, rby, rd, final, ss, rs, dev, levels):
+    core, z, p, xq, yq, dq = dev
+    xn, yn = z * 4 + xq, z * 4 + yq
+    lev_of, L = levels
+    R = part.shape[1]
+
+    def copy(kind, lev, src, dst, to):
+        return remote(src, dst, ss.at[kind, lev], rs.at[kind, lev], (core, to))
+
+    class Stages:
+        @staticmethod
+        def a(k):
+            lev = lev_of(k)
+            odd = k % 2
+            copy(0, lev, part.at[lev * 4 + dq], ra.at[lev], yn + odd * (xn - yn)).start()
+
+        @staticmethod
+        def b(k):
+            lev = lev_of(k)
+            odd = k % 2
+            via = lev * 4 + xq + odd * (yq - xq)
+            copy(0, lev, ra.at[lev], ra.at[lev], xn).wait_recv()
+
+            def add(r):
+                t = pl.ds(r, 16)
+                part[via, t, :] = (part[via, t, :].astype(F32) + ra[lev, t, :].astype(F32)).astype(BF)
+
+            rows_loop(R, 16, add)
+            copy(1, lev, part.at[lev * 4 + xq], rbx.at[lev], xn).start()
+            copy(2, lev, part.at[lev * 4 + yq], rby.at[lev], yn).start()
+
+        @staticmethod
+        def c(k):
+            lev = lev_of(k)
+            own = lev * 4 + p
+            copy(1, lev, rbx.at[lev], rbx.at[lev], xn).wait_recv()
+            copy(2, lev, rby.at[lev], rby.at[lev], yn).wait_recv()
+
+            def add(r):
+                t = pl.ds(r, 16)
+                tot = part[own, t, :].astype(F32) + rbx[lev, t, :].astype(F32) + rby[lev, t, :].astype(F32)
+
+                @pl.when(k == 0)
+                def _():
+                    final[t, :] = tot
+
+                @pl.when(k > 0)
+                def _():
+                    part[own, t, :] = tot.astype(BF)
+
+            rows_loop(R, 16, add)
+
+            @pl.when(k > 0)
+            def _():
+                remote(part.at[own], rd.at[z], ss.at[3, lev], rs.at[3, z], (core, lev * 4 + p)).start()
+
+        @staticmethod
+        def d(k):
+            lev = lev_of(k)
+            copy(3, lev, rd.at[lev], rd.at[lev], xn).wait_recv()
+
+            def add(r):
+                t = pl.ds(r, 16)
+                final[t, :] = final[t, :] + rd[lev, t, :].astype(F32)
+
+            rows_loop(R, 16, add)
+
+        @staticmethod
+        def finish():
+            @pl.loop(0, L)
+            def _(k):
+                lev = lev_of(k)
+                for kind in range(3):
+                    copy(kind, lev, ra.at[0], ra.at[0], xn).wait_send()
+
+                @pl.when(k > 0)
+                def _():
+                    copy(3, lev, ra.at[0], ra.at[0], xn).wait_send()
+
+    return Stages
+
+
+def back_kernel(
+    dh_ref, y_ref, sc_ref, small_ref, stat_ref, u1_ref, u2_ref, x1_ref, dys_ref,
+    q_ref, k_ref, v_ref, p_ref, o_ref, e_ref, s_ref, w_hbm,
+    lo_out, ig_out, gqkv_out, go_out, smalls_out,
+    wbuf, perm, accs, dx1, dab, do, dq, dk, dv, h1b, dh1, tmpb, keep, send, recv,
+    part0, ra0, rbx0, rby0, rd0, part1, ra1, rbx1, rby1, rd1, smine, ssib, srecv,
+    rs_s, rs_r, sib_s, sib_r, sm_s, sm_r, loc,
+):
+    T, D = dh_ref.shape
+    S, WR = part0.shape[0], part0.shape[1]
+    L = S // 4
+    half = D // 2
+    me, core, z, p, xq, yq, dgq = place_of()
+    xn = z * 4 + xq
+    sgn = 1 - 2 * (z // (L // 2))
+    sib = (1 - core, me)
+    greet(S, core)
+
+    def lev_of(k):
+        return (z + k * sgn + L) % L
+
+    dev, levels = (core, z, p, xq, yq, dgq), (lev_of, L)
+    g0 = tree_scatter(part0, ra0, rbx0, rby0, rd0, go_out, rs_s.at[0], rs_r.at[0], dev, levels)
+    g1 = tree_scatter(part1, ra1, rbx1, rby1, rd1, gqkv_out, rs_s.at[1], rs_r.at[1], dev, levels)
+    loads = [pltpu.make_async_copy(w_hbm.at[i], wbuf.at[i], loc.at[i]) for i in range(4)]
+    for i in (3, 0, 1, 2):
+        loads[i].start()
+
+    perm_f, n0 = sort_matrix(e_ref[...], s_ref[...], T)
+    perm[...] = perm_f.astype(BF)
+    accs[...] = jnp.zeros_like(accs)
+    scol = jnp.concatenate([sc_ref[...], jnp.zeros((120, 128), F32)], axis=0).T
+    dh1[:, 0:128] = scol
+
+    def acc(i, v):
+        accs[i] = accs[i] + (v[0:8] + v[8:16])
+
+    def norm2(r):
+        t = pl.ds(r, 16)
+        st = stat_ref[t, :]
+        c1, c0, gate, r0, r1, inv = (st[:, i : i + 1] for i in (0, 3, 4, 5, 6, 9))
+        row = (lax.broadcasted_iota(jnp.int32, (16, 1), 0) + r).astype(F32)
+        is0 = row < n0
+        s3 = dh1[t, 0:128]
+        sm = s3[:, 0:1]
+        se = jnp.where(is0, s3[:, 1:2], s3[:, 2:3])
+        dc0, dc1 = gate * se, sm
+        tot = c0 * dc0 + c1 * dc1
+        dcl0, dcl1 = c0 * (dc0 - tot), c1 * (dc1 - tot)
+        dgate = c0 * se
+        dr0, dr1 = jnp.where(is0, dgate, 0.0), jnp.where(is0, 0.0, dgate)
+        tot = r0 * dr0 + r1 * dr1
+        drl0, drl1 = r0 * (dr0 - tot), r1 * (dr1 - tot)
+        u2 = u2_ref[t, :]
+        h2 = u2 * small_ref[2:3, :] + small_ref[3:4, :]
+        dh2 = dh_ref[t, :]
+        for i, d in enumerate((drl0, drl1, dcl0, dcl1)):
+            acc(4 + i, h2 * d)
+            dh2 = dh2 + d * small_ref[4 + i : 5 + i, :]
+        acc(2, dh2 * u2)
+        acc(3, dh2)
+        e = dh2 * small_ref[2:3, :]
+        inner = e - jnp.mean(e, axis=1, keepdims=True) - u2 * jnp.mean(e * u2, axis=1, keepdims=True)
+        g = dys_ref[t, :].astype(F32) + inv * inner
+        dx1[t, :] = g
+        dab[t, :] = g.astype(BF)
+        tmpb[t, :] = (x1_ref[t, :] + y_ref[t, :]).astype(BF)
+        h1b[t, :] = (u1_ref[t, :] * small_ref[0:1, :] + small_ref[1:2, :]).astype(BF)
+
+    rows_loop(T, 16, norm2)
+
+    other = pl.multiple_of((1 - core) * half, half)
+    mine = pl.multiple_of(core * half, half)
+
+    def weight_grad(i, left, right):
+        send[i] = mm(left[:, pl.ds(other, half)], right[...], ((0,), (0,))).astype(BF)
+        c = remote(send.at[i], recv.at[i], sib_s.at[i], sib_r.at[i], sib)
+        c.start()
+        keep[i] = mm(left[:, pl.ds(mine, half)], right[...], ((0,), (0,)))
+        return c
+
+    def join(i, c, part, at):
+        c.wait_recv()
+
+        @pl.loop(0, S)
+        def _(j):
+            t = pl.ds(pl.multiple_of(j * WR, WR), WR)
+            part[j, at : at + WR, :] = (keep[i, t, :] + recv[i, t, :].astype(F32)).astype(BF)
+
+    c_o = weight_grad(3, o_ref, dab)
+    loads[3].wait()
+    do[...] = mm(dab[...], wbuf[3], ((1,), (1,))).astype(BF)
+    join(3, c_o, part0, 0)
+    for k in reversed(range(L)):
+        g0.a(k)
+
+    lo_out[...] = mm(perm[...], tmpb[...], ((0,), (0,))).astype(BF)
+
+    low = lax.broadcasted_iota(jnp.int32, (T, 128), 1) < 64
+    lowb = low.astype(F32).astype(BF)
+    highb = (1.0 - low.astype(F32)).astype(BF)
+
+    def heads(j):
+        ln = pl.ds(pl.multiple_of(j * 128, 128), 128)
+        qp, dop = q_ref[:, ln], do[:, ln]
+        q2 = jnp.concatenate([qp * lowb, qp * highb], axis=0)
+        do2 = jnp.concatenate([dop * lowb, dop * highb], axis=0)
+        pr = p_ref[j]
+        dp = mm(do2, v_ref[:, ln], ((1,), (1,)))
+        ds = (pr * (dp - jnp.sum(pr * dp, axis=1, keepdims=True))).astype(BF)
+        dq2 = mm(ds, k_ref[:, ln])
+        dq[:, ln] = jnp.where(low, dq2[0:T], dq2[T:]).astype(BF) * BF(0.125)
+        dk[:, ln] = mm(ds, q2, ((0,), (0,))).astype(BF)
+        dv[:, ln] = mm(pr.astype(BF), do2, ((0,), (0,))).astype(BF)
+
+    @pl.loop(0, D // 128)
+    def _(j):
+        heads(j)
+
+    c_v = weight_grad(2, h1b, dv)
+    c_k = weight_grad(1, h1b, dk)
+    c_q = weight_grad(0, h1b, dq)
+    for k in reversed(range(L)):
+        g0.b(k)
+    join(2, c_v, part1, 2 * WR)
+    join(1, c_k, part1, WR)
+    join(0, c_q, part1, 0)
+    for k in reversed(range(L)):
+        g1.a(k)
+    for i in range(3):
+        loads[i].wait()
+    dh1[...] = mm(dq[...], wbuf[0], ((1,), (1,)))
+    dh1[...] = dh1[...] + mm(dk[...], wbuf[1], ((1,), (1,)))
+    dh1[...] = dh1[...] + mm(dv[...], wbuf[2], ((1,), (1,)))
+    for k in reversed(range(L)):
+        g0.c(k)
+
+    def norm1(r):
+        t = pl.ds(r, 16)
+        inv = stat_ref[t, :][:, 8:9]
+        u = u1_ref[t, :]
+        d = dh1[t, :]
+        acc(0, d * u)
+        acc(1, d)
+        e = d * small_ref[0:1, :]
+        inner = e - jnp.mean(e, axis=1, keepdims=True) - u * jnp.mean(e * u, axis=1, keepdims=True)
+        tmpb[t, :] = (dx1[t, :] + inv * inner).astype(BF)
+
+    rows_loop(T, 16, norm1)
+    for i in range(8):
+        smine[i : i + 1, :] = jnp.sum(accs[i], axis=0, keepdims=True)
+    c_s = remote(smine, ssib, sib_s.at[4], sib_r.at[4], sib)
+    c_s.start()
+    for k in reversed(range(L)):
+        g1.b(k)
+    ig_out[...] = mm(perm[...], tmpb[...], ((0,), (0,))).astype(BF)
+    c_s.wait()
+    smine[...] = smine[...] + ssib[...]
+    group = 128 // WR
+
+    def s_at(i):
+        return smine.at[:, pl.ds(pl.multiple_of((core * S + i) // group * 128, 128), 128)]
+
+    def s_copy(i):
+        to = (me + i) % S
+        return remote(s_at(to), srecv.at[me], sm_s.at[i], sm_r.at[0], (core, to))
+
+    @pl.loop(1, S)
+    def _(i):
+        s_copy(i).start()
+
+    srecv[me] = s_at(me)[...]
+    for k in reversed(range(L)):
+        g1.c(k)
+    for k in range(1, L):
+        g0.d(k)
+    allr = srecv.at[pl.ds(0, S - 1)]
+    remote(allr, allr, sm_s.at[0], sm_r.at[0], (core, xn)).wait_recv()
+    smalls_out[...] = jnp.sum(srecv[...], axis=0)
+    for k in range(1, L):
+        g1.d(k)
+    g0.finish()
+    g1.finish()
+    for c in (c_o, c_v, c_k, c_q):
+        c.wait_send()
+
+    @pl.loop(1, S)
+    def _(i):
+        s_copy(i).wait_send()
+
+
+def back_call(dh, y, sc, small, stat, u1, u2, x1, dys, q, k, v, p, o, es, ss, wa, S):
+    T, D = dh.shape
+    WR = D // (2 * S)
+    L = S // 4
+    vm = pl.BlockSpec(memory_space=pltpu.VMEM)
+    hb = pl.BlockSpec(memory_space=pl.ANY)
+    V = pltpu.VMEM
+    dma = pltpu.SemaphoreType.DMA
+    sds = jax.ShapeDtypeStruct
+    row = V((T, D), BF)
+
+    def rs_bufs(R):
+        return [V((S, R, D), BF)] + [V((L, R, D), BF)] * 4
+
+    return pl.pallas_call(
+        back_kernel,
+        out_shape=(
+            sds((T, D), BF), sds((T, D), BF), sds((3 * WR, D), F32), sds((WR, D), F32), sds((8, 128), F32),
+        ),
+        in_specs=[vm] * 16 + [hb],
+        out_specs=(vm,) * 5,
+        scratch_shapes=[
+            V((4, D, D), BF), V((T, T), BF), V((8, 8, D), F32), V((T, D), F32), row, row, row, row, row, row,
+            V((T, D), F32), row, V((4, D // 2, D), F32), V((4, D // 2, D), BF), V((4, D // 2, D), BF),
+        ]
+        + rs_bufs(WR)
+        + rs_bufs(3 * WR)
+        + [
+            V((8, D), F32), V((8, D), F32), V((S, 8, 128), F32),
+            dma((2, 4, L)), dma((2, 4, L)), dma((5,)), dma((5,)), dma((S,)), dma((1,)), dma((4,)),
+        ],
+        compiler_params=pltpu.CompilerParams(collective_id=3, has_side_effects=True, vmem_limit_bytes=60000000),
+        cost_estimate=pl.CostEstimate(flops=4 * 10**9, bytes_accessed=20 * 2**20, transcendentals=2**20),
+        name="back",
+    )(dh, y, sc, small, stat, u1, u2, x1, dys, q, k, v, p, o, es, ss, wa)
+
+
 def body_plain(
     hidden_in, doc_ids, expert_ids, slot_ids, out_grad, ln1_gain, ln1_bias, w_query, w_key, w_value,
     w_out, ln2_gain, ln2_bias, w_up, w_down, w_router, w_mix, expert_up, expert_down, load_avg,
@@ -977,69 +1287,20 @@
         hidden_in, out_grad, doc_ids, expert_ids.reshape(1, T), slot_ids.reshape(1, T), small,
         (w_query, w_key, w_value, w_out), w_up, expert_up, w_down, expert_down, S,
     )
-    wa = wa.reshape(4, D, D)
-    wq, wk, wv, wo = wa[0], wa[1], wa[2], wa[3]
-    g1, b1, g2, b2 = small[0], small[1], small[2], small[3]
-    wr, wm = small[4:6], small[6:8]
-    place = lax.iota(jnp.int32, T)
-    n0 = jnp.sum((expert_ids == 0).astype(jnp.int32))
-    pos = jnp.where(expert_ids == 0, slot_ids, n0 + slot_ids)
-    perm = (pos[None, :] == place[:, None]).astype(BF)
-    is0 = (place < n0)[:, None]
-    i1, i2 = stat[:, 8:9], stat[:, 9:10]
-    c0, c1, gate, r = stat[:, 3:4], stat[:, 0:1], stat[:, 4:5], stat[:, 5:7]
-    h1b = (u1 * g1 + b1).astype(BF)
-    h2 = u2 * g2 + b2
-    p = p.reshape(H, T, T)
-    pb = p.astype(BF)
-    q, k, v = q.reshape(T, H, HD), k.reshape(T, H, HD), v.reshape(T, H, HD)
     yfull, dh2, sc, gup, gdn0, gdn12 = ffn_call(h2b, scal8, dy_all, ups, downs)
-    sm = sc[0][:, None]
-    se = jnp.where(is0, sc[1][:, None], sc[2][:, None])
-    dc0, dc1 = gate * se, sm
-    tot = c0 * dc0 + c1 * dc1
-    dcl0, dcl1 = c0 * (dc0 - tot), c1 * (dc1 - tot)
-    dgate = c0 * se
-    dr0, dr1 = jnp.where(is0, dgate, 0.0), jnp.where(is0, 0.0, dgate)
-    tot = r[:, 0:1] * dr0 + r[:, 1:2] * dr1
-    drl0, drl1 = r[:, 0:1] * (dr0 - tot), r[:, 1:2] * (dr1 - tot)
-    layer_out = (x1 + yfull).astype(BF)
-    dh2 = dh2 + drl0 * wr[0] + drl1 * wr[1] + dcl0 * wm[0] + dcl1 * wm[1]
-    gw = [jnp.sum(h2 * t, axis=0) for t in (drl0, drl1, dcl0, dcl1)]
-    dx1, gg2, gb2 = norm_back(dh2, u2, i2, g2)
-    dx1 = dx1 + dys.astype(F32)
-    dab = dx1.astype(BF)
-    gwo = mm(o, dab, ((0,), (0,)))
-    do = mm(dab, wo, ((1,), (1,))).astype(BF).reshape(T, H, HD)
-    dp = jnp.einsum("ihd,jhd->hij", do, v, preferred_element_type=F32)
-    ds = (p * (dp - jnp.sum(p * dp, axis=-1, keepdims=True))).astype(BF)
-    dq = jnp.einsum("hij,jhd->ihd", ds, k, preferred_element_type=F32).astype(BF)
-    dq = (dq * BF(0.125)).reshape(T, D)
-    dk = jnp.einsum("hij,ihd->jhd", ds, q, preferred_element_type=F32).astype(BF).reshape(T, D)
-    dv = jnp.einsum("hij,ihd->jhd", pb, do, preferred_element_type=F32).astype(BF).reshape(T, D)
-    dh1 = mm(dq, wq, ((1,), (1,))) + mm(dk, wk, ((1,), (1,))) + mm(dv, wv, ((1,), (1,)))
-    ga = jnp.stack([mm(h1b, dq, ((0,), (0,))), mm(h1b, dk, ((0,), (0,))), mm(h1b, dv, ((0,), (0,))), gwo])
-    dxn, gg1, gb1 = norm_back(dh1, u1, i1, g1)
-    input_grad = (dx1 + dxn).astype(BF)
-
-    layer_out = mm(perm, layer_out, ((0,), (0,))).astype(BF)
-    input_grad = mm(perm, input_grad, ((0,), (0,))).astype(BF)
-
-    smalls = lax.psum(jnp.stack([gg1, gb1, gg2, gb2] + gw), BOTH)
-    mine = lax.dynamic_slice_in_dim(smalls, lax.axis_index(BOTH) * WR, WR, 1)
-    ga = ga.reshape(4, C, S, WR, D).transpose(1, 2, 0, 3, 4)
-    ga = lax.psum_scatter(ga.astype(BF), "dp", scatter_dimension=0, tiled=False)
-    ga = lax.psum_scatter(ga, "shard", scatter_dimension=0, tiled=False).astype(F32)
-    gup = gup.astype(F32)
-    gup = gup.reshape(S, 3, WR, C, FR).transpose(1, 2, 3, 0, 4).reshape(3, WR, FF)
-
+    layer_out, input_grad, gqkv, gwo, smalls = back_call(
+        dh2, yfull, sc, small, stat, u1, u2, x1, dys, q, k, v, p, o,
+        expert_ids.reshape(1, T), slot_ids.reshape(1, T), wa.reshape(4, D, D), S,
+    )
+    mine = lax.dynamic_slice_in_dim(smalls, dev % group * WR, WR, 1)
+    ga = gqkv.reshape(3, WR, D)
+    gup = gup.astype(F32).reshape(S, 3, WR, C, FR).transpose(1, 2, 3, 0, 4).reshape(3, WR, FF)
     tokens0 = count[0, 0].astype(jnp.int32)
     counts = jnp.stack([tokens0, T * ndev - tokens0])
-    load_new = 0.9 * load_avg + 0.1 * counts.astype(F32) * E / (T * C * S)
+    load_new = 0.9 * load_avg + 0.1 * counts.astype(F32) * E / (T * ndev)
     return (
-        layer_out, input_grad, mine[0], mine[1], ga[0], ga[1], ga[2], ga[3], mine[2], mine[3],
-        gup[0], gdn0, jnp.stack([mine[4], mine[5]], axis=1), jnp.stack([mine[6], mine[7]], axis=1),
-        gup[1:], gdn12, counts, load_new,
+        layer_out, input_grad, mine[0], mine[1], ga[0], ga[1], ga[2], gwo, mine[2], mine[3],
+        gup[0], gdn0, mine[4:6].T, mine[6:8].T, gup[1:], gdn12, counts, load_new,
     )
 
 

time: 606 us -> 419 us (0.69)
  waiting for transfers between devices: 149 us -> 0 us
  Pallas kernels: 340 us -> 399 us
  blocking collectives: 43.3 us -> 0 us
  local copies, waits for them, and re-layouts: 33.1 us -> 14.1 us
  between operations: 15.1 us -> 1.45 us
  other arithmetic: 13.1 us -> 1.21 us
  matrix products: 10.7 us -> 0 us
    unnamed x4 -> x0, waiting for transfers between devices: 149 us -> none
    pallas_call x0 -> x1, Pallas kernels: none -> 59.2 us  [back_call(): pl.pallas_call(back_kernel, out_shape=(sds((T, D), BF), sds((T, D), BF),...]
    psum x1 -> x0, blocking collectives: 43.3 us -> none  [body(): smalls = lax.psum(jnp.stack([gg1, gb1, gg2, gb2] + gw), BOTH)]
    dot_general x14 -> x0, matrix products: 10.7 us -> none  [the longest x10 9.31 us: mm(): return lax.dot_general(a, b, (dims, ((), ())), preferred_element_type=F32)]
  transfers between devices with their start and end apart: 2 -> 0, of which waited for: 2 -> 0; matrix products, arithmetic and copies ran while one was open for 2% -> 0% of each run, Pallas kernels for 0% -> 0%
where the time goes in v4:
time: 419 us; the launch traced here: 416 us
  Pallas kernels  399 us (95%)
  local copies, waits for them, and re-layouts  14.1 us (3%)
    pallas_call x1, Pallas kernels, ffn_call(): pl.pallas_call(ffn_kernel, out_shape=(sds((T, D), F32), sds((T, D), F32),...  228 us
    pallas_call x1, Pallas kernels, attn_call(): pl.pallas_call(attn_kernel, out_shape=(row, sds((T, 128), F32), sds((8, T...  112 us
    pallas_call x1, Pallas kernels, back_call(): pl.pallas_call(back_kernel, out_shape=(sds((T, D), BF), sds((T, D), BF),...  59.2 us

profile of v4, /device:TPU:0, one launch (start us, length us, event | category | flops | bytes accessed | tf_op | source)
XLA Modules:
  0.0 416.1 jit_solution(10017395759694565725)
XLA Ops:
  0.7 0.7 slice_bitcast_fusion.6
  1.4 0.7 stack.40
  2.2 0.1 tile.10
  2.3 0.6 fusion.small_ref
  2.9 112.0 %attn.1 = (bf16[128,1024]{1,0:T(8,128)(2,1)}, f32[128,128]{1,0:T(8,128)}, f32[8,128]{1,0:T(8,128)}, f32[128,1024]{1,0:T(8,128)}, f32[128,1024]{1,0:T(8,128)}, /*...) custom-call(bf16[128,1024]{1,0:T(8,128)(2,1)} %x_ref.1, ...), custom_call_target="tpu_custom_call" | custom-call | flops 2000000000 | bytes 41943040 | tf_op jit(solution)/shard_map/attn/pallas_call | solution.py:777
  114.9 1.2 slice.71
  116.7 228.1 %ffn.1 = (f32[128,1024]{1,0:T(8,128)}, f32[128,1024]{1,0:T(8,128)}, f32[8,128]{1,0:T(8,128)}, bf16[16,3,32,256]{3,2,1,0:T(8,128)(2,1)}, f32[128,1024]{1,0:T(8,128)}, /*index=5*/f32[2,128,1024]{2,1,0:T(8,128)}) custom-call(bf16[128,1024]{1,0:T(8,128)(2,1)} %get-tuple-element.47.h_ref, f32[8,128]{1,0:T(8,128)} %get-tuple-element.48.scal_ref, ...), custom_call_target="tpu_custom_call" | custom-call | flops 15000000512 | bytes 20971520 | tf_op jit(solution)/shard_map/ffn/pallas_call | solution.py:373
  344.9 59.2 %back.1 = (bf16[128,1024]{1,0:T(8,128)(2,1)}, bf16[128,1024]{1,0:T(8,128)(2,1)}, f32[96,1024]{1,0:T(8,128)}, f32[32,1024]{1,0:T(8,128)}, f32[8,128]{1,0:T(8,128)}) custom-call(f32[128,1024]{1,0:T(8,128)} %get-tuple-element.52.dh_ref, f32[128,1024]{1,0:T(8,128)} %get-tuple-element.53.y_ref, f32[8,128]{1,0:T(8,128)} %get-tuple-element.54.sc_ref, ...), custom_call_target="tpu_custom_call" | custom-call | flops 4000000000 | bytes 20971520 | tf_op jit(solution)/shard_map/back/pallas_call | solution.py:1083
  404.1 0.6 multiply_add_fusion
  404.7 0.7 constant_dynamic-slice_fusion
  405.4 0.5 slice_bitcast_fusion.2
  406.0 0.6 slice_bitcast_fusion
  406.5 1.8 fusion.1
  408.3 0.8 reshape.139
  409.1 0.1 slice.73
  409.2 0.6 copy.39
  409.9 1.2 slice.70
  411.0 0.3 copy.38
  411.4 0.9 squeeze.23
  412.3 0.7 copy.45
  413.0 0.7 copy.46
  413.7 0.7 copy.47
  414.3 0.8 copy.48
  415.1 1.0 copy.49
  (18 shorter events, 0.1 us)
Async XLA Ops:
  344.8 59.3 %copy-start.6 = (f32[2]{0:T(128)S(1)}, f32[2]{0:T(128)}, u32[]{:S(2)}) copy-start(f32[2]{0:T(128)} %param.39) | copy-start | bytes 28
  344.9 63.5 %copy-start.1 = (bf16[16,3,32,256]{3,2,1,0:T(8,128)(2,1)S(1)}, bf16[16,3,32,256]{3,2,1,0:T(8,128)(2,1)}, u32[]{:S(2)}) copy-start(bf16[16,3,32,256]{3,2,1,0:T(8,128)(2,1)} %get-tuple-element.72) | copy-start | bytes 2359300
  411.0 1.2 copy-start.4
  411.0 1.9 copy-start.3
  411.0 2.6 copy-start.5
  411.0 3.3 copy-start.2
  411.3 3.8 copy-start

commit v5 on v4

--- a/solution.py
+++ b/solution.py
@@ -80,10 +80,197 @@
         fn(pl.multiple_of(i * step, step))
 
 
+def level_order(z, L):
+    upper = z // (L // 2)
+    y = z + upper * (L - 1 - 2 * z)
+
+    def lev_of(k):
+        low = k - 1 + (k - 1 - y + L) // L
+        lev = low + upper * (L - 1 - 2 * low)
+        first = 1 - (k + L - 1) // L
+        return lev + first * (z - lev)
+
+    return lev_of
+
+
+def tree_gather(at, own, ss, rs, dev, levels):
+    core, z, p, xq, yq, dq = dev
+    xn, yn = z * 4 + xq, z * 4 + yq
+    me = z * 4 + p
+    lev_of, L = levels
+
+    def copy(kind, slot, src, idx, to):
+        return remote(src, at(idx), ss.at[kind, slot], rs.at[kind, slot], (core, to))
+
+    def up_line(src, send):
+        return remote(src, at(me), send, rs.at[0, z], (core, me + 4))
+
+    def down_line(src, send):
+        return remote(src, at(me), send, rs.at[0, z], (core, me - 4))
+
+    def onward(k):
+        lev = lev_of(k)
+        step = 1 - 2 * ((lev - z + L) // L)
+        to = z + step
+        idx = lev * 4 + p
+        ok = (to >= 0) & (to < L)
+        return ok, remote(at(idx), at(idx), ss.at[0, lev], rs.at[0, lev], (core, me + 4 * step))
+
+    class Stages:
+        @staticmethod
+        def start():
+            @pl.when(z < L - 1)
+            def _():
+                up_line(own, ss.at[0, z]).start()
+
+            @pl.when(z > 0)
+            def _():
+                down_line(own, ss.at[4, 0]).start()
+
+            copy(1, z, own, me, xn).start()
+            copy(2, z, own, me, yn).start()
+
+        @staticmethod
+        def a(k):
+            lev = lev_of(k)
+            idx = lev * 4 + p
+            copy(0, lev, own, idx, xn).wait_recv()
+            ok, on = onward(k)
+
+            @pl.when(ok)
+            def _():
+                on.start()
+
+            copy(1, lev, at(idx), idx, xn).start()
+            copy(2, lev, at(idx), idx, yn).start()
+
+        @staticmethod
+        def b(k):
+            lev = lev_of(k)
+            odd = k % 2
+            copy(1, lev, own, lev * 4 + xq, xn).wait_recv()
+            copy(2, lev, own, lev * 4 + yq, yn).wait_recv()
+            idx = lev * 4 + xq + odd * (yq - xq)
+            copy(3, lev, at(idx), idx, yn + odd * (xn - yn)).start()
+
+        @staticmethod
+        def c(k):
+            lev = lev_of(k)
+            copy(3, lev, own, lev * 4 + dq, xn).wait_recv()
+
+        @staticmethod
+        def finish():
+            @pl.when(z < L - 1)
+            def _():
+                up_line(own, ss.at[0, z]).wait_send()
+
+            @pl.when(z > 0)
+            def _():
+                down_line(own, ss.at[4, 0]).wait_send()
+
+            @pl.loop(0, L)
+            def _(k):
+                lev = lev_of(k)
+                for kind in range(1, 4):
+                    copy(kind, lev, own, me, xn).wait_send()
+
+            @pl.loop(1, L)
+            def _(k):
+                ok, on = onward(k)
+
+                @pl.when(ok)
+                def _():
+                    on.wait_send()
+
+    return Stages
+
+
+def tree_scatter(part, ra, rbx, rby, rd, final, ss, rs, dev, levels):
+    core, z, p, xq, yq, dq = dev
+    xn, yn = z * 4 + xq, z * 4 + yq
+    lev_of, L = levels
+    R = part.shape[1]
+
+    def copy(kind, lev, src, dst, to):
+        return remote(src, dst, ss.at[kind, lev], rs.at[kind, lev], (core, to))
+
+    class Stages:
+        @staticmethod
+        def a(k):
+            lev = lev_of(k)
+            odd = k % 2
+            copy(0, lev, part.at[lev * 4 + dq], ra.at[lev], yn + odd * (xn - yn)).start()
+
+        @staticmethod
+        def b(k):
+            lev = lev_of(k)
+            odd = k % 2
+            via = lev * 4 + xq + odd * (yq - xq)
+            copy(0, lev, ra.at[lev], ra.at[lev], xn).wait_recv()
+
+            def add(r):
+                t = pl.ds(r, 32)
+                part[via, t, :] = (part[via, t, :].astype(F32) + ra[lev, t, :].astype(F32)).astype(BF)
+
+            rows_loop(R, 32, add)
+            copy(1, lev, part.at[lev * 4 + xq], rbx.at[lev], xn).start()
+            copy(2, lev, part.at[lev * 4 + yq], rby.at[lev], yn).start()
+
+        @staticmethod
+        def c(k):
+            lev = lev_of(k)
+            own = lev * 4 + p
+            copy(1, lev, rbx.at[lev], rbx.at[lev], xn).wait_recv()
+            copy(2, lev, rby.at[lev], rby.at[lev], yn).wait_recv()
+
+            def add(r):
+                t = pl.ds(r, 32)
+                tot = part[own, t, :].astype(F32) + rbx[lev, t, :].astype(F32) + rby[lev, t, :].astype(F32)
+
+                @pl.when(k == 0)
+                def _():
+                    final[t, :] = tot
+
+                @pl.when(k > 0)
+                def _():
+                    part[own, t, :] = tot.astype(BF)
+
+            rows_loop(R, 32, add)
+
+            @pl.when(k > 0)
+            def _():
+                remote(part.at[own], rd.at[z], ss.at[3, lev], rs.at[3, z], (core, lev * 4 + p)).start()
+
+        @staticmethod
+        def d(k):
+            lev = lev_of(k)
+            copy(3, lev, rd.at[lev], rd.at[lev], xn).wait_recv()
+
+            def add(r):
+                t = pl.ds(r, 32)
+                final[t, :] = final[t, :] + rd[lev, t, :].astype(F32)
+
+            rows_loop(R, 32, add)
+
+        @staticmethod
+        def finish():
+            @pl.loop(0, L)
+            def _(k):
+                lev = lev_of(k)
+                for kind in range(3):
+                    copy(kind, lev, ra.at[0], ra.at[0], xn).wait_send()
+
+                @pl.when(k > 0)
+                def _():
+                    copy(3, lev, ra.at[0], ra.at[0], xn).wait_send()
+
+    return Stages
+
+
 def ffn_kernel(
     h_ref, scal_ref, dy_ref, up_ref, dn_ref,
     y_out, dh_out, sc_out, gup_out, gdn0_out, gdn12_out,
-    hall, scall, psc, screcv, wcol, scol, part, ra, rbx, rby, rd, final,
+    hall, scall, psc, screcv, wcol, scol, part, ra, rbx, rby, rd,
     pre, der, ub, dg, dm, m, yacc, dxacc, gdn, gup, sib_dn, sib_up, gsend, grecv,
     ag_s, ag_r, rs_s, rs_r, one_s, one_r, sm_s, sm_r,
 ):
@@ -93,23 +280,13 @@
     LO = 80
     HI = T - LO
     me, core, z, p, xq, yq, dq = place_of()
-    xn, yn = z * 4 + xq, z * 4 + yq
-    sgn = 1 - 2 * (z // (L // 2))
+    xn = z * 4 + xq
+    lev_of = level_order(z, L)
+    dev, levels = (core, z, p, xq, yq, dq), (lev_of, L)
     greet(S, core)
-
-    def lev_of(k):
-        return (z + k * sgn + L) % L
-
-    def h_copy(kind, slot, src, idx, dev):
-        return remote(src, hall.at[idx], ag_s.at[kind, slot], ag_r.at[kind, slot], (core, dev))
-
-    @pl.loop(1, L)
-    def _(k):
-        lev = lev_of(k)
-        remote(h_ref, hall.at[me], ag_s.at[0, lev], ag_r.at[0, z], (core, lev * 4 + p)).start()
-
-    h_copy(1, z, h_ref, me, xn).start()
-    h_copy(2, z, h_ref, me, yn).start()
+    hg = tree_gather(lambda i: hall.at[i], h_ref, ag_s, ag_r, dev, levels)
+    rg = tree_scatter(part, ra, rbx, rby, rd, dh_out, rs_s, rs_r, dev, levels)
+    hg.start()
 
     @pl.loop(1, S)
     def _(i):
@@ -121,23 +298,8 @@
     gup[...] = jnp.zeros_like(gup)
     remote(scall.at[pl.ds(0, S - 1)], scall.at[pl.ds(0, S - 1)], sm_s.at[0, 0], sm_r.at[0], (core, xn)).wait_recv()
 
-    def stage_a(k):
-        lev = lev_of(k)
-        idx = lev * 4 + p
-        h_copy(0, lev, hall.at[idx], idx, xn).wait_recv()
-        h_copy(1, lev, hall.at[idx], idx, xn).start()
-        h_copy(2, lev, hall.at[idx], idx, yn).start()
-
-    def stage_b(k):
-        lev = lev_of(k)
-        odd = k % 2
-        h_copy(1, lev, h_ref, lev * 4 + xq, xn).wait_recv()
-        h_copy(2, lev, h_ref, lev * 4 + yq, yn).wait_recv()
-        idx = lev * 4 + xq + odd * (yq - xq)
-        h_copy(3, lev, hall.at[idx], idx, yn + odd * (xn - yn)).start()
-        h_copy(3, lev, h_ref, lev * 4 + dq, xn).wait_recv()
-
-    lane = lax.broadcasted_iota(jnp.int32, (16, 128), 1)
+    size = (4 * T, 4 * LO, 4 * LO)
+    first = (0, 4 * T, 4 * T + 4 * LO)
 
     def compute(lev):
         base = lev * 4
@@ -147,135 +309,99 @@
         for e in range(3):
             n = LO if e else T
             off = HI if e == 2 else 0
-            rows = 4 * n
+            rows, at0 = size[e], first[e]
+            here = slice(at0, at0 + rows)
             hm = hall[pl.ds(base, 4), off : off + n, :].reshape(rows, D)
             pre[0:rows, :] = mm(hm, up_ref[e])
 
             def act(r):
-                val, d = gelu_pair(pre[pl.ds(r, 32), :])
-                ub[pl.ds(r, 32), :] = val.astype(BF)
-                der[pl.ds(r, 32), :] = d
-
-            rows_loop(rows, 32, act)
-            m[0:rows, :] = mm(ub[0:rows, :], dn_ref[e])
+                t = pl.ds(r, rows // 4)
+                val, d = gelu_pair(pre[t, :])
+                ub[pl.ds(pl.multiple_of(at0 + r, 16), rows // 4), :] = val.astype(BF)
+                der[t, :] = d
+
+            rows_loop(rows, rows // 4, act)
+            m[0:rows, :] = mm(ub[here, :], dn_ref[e])
+            step = n if e else T // 2
+            lane = lax.broadcasted_iota(jnp.int32, (step, 128), 1)
             for q in range(4):
 
                 def elem(r):
-                    at = pl.multiple_of(r + off, 16)
-                    mine = pl.ds(pl.multiple_of(q * n + r, 16), 16)
-                    t = pl.ds(pl.multiple_of(q * T + off + r, 16), 16)
-                    w = wcol[q, pl.ds(at, 16), :][:, e : e + 1]
-                    dyv = dy_ref[base + q, pl.ds(at, 16), :].astype(F32)
+                    at = pl.ds(pl.multiple_of(r + off, 16), step)
+                    mine = pl.ds(pl.multiple_of(q * n + r, 16), step)
+                    keep = pl.ds(pl.multiple_of(at0 + q * n + r, 16), step)
+                    t = pl.ds(pl.multiple_of(q * T + off + r, 16), step)
+                    w = wcol[q, at, :][:, e : e + 1]
+                    dyv = dy_ref[base + q, at, :].astype(F32)
                     mv = m[mine, :]
                     s = jnp.sum(dyv * mv, axis=1, keepdims=True)
                     s = jnp.where(lane == e, s, 0.0)
-                    dm[mine, :] = (dyv * w).astype(BF)
+                    dm[keep, :] = (dyv * w).astype(BF)
                     if e:
                         yacc[t, :] = yacc[t, :] + mv * w
-                        scol[q, pl.ds(at, 16), :] = scol[q, pl.ds(at, 16), :] + s
+                        scol[q, at, :] = scol[q, at, :] + s
                     else:
                         yacc[t, :] = mv * w
-                        scol[q, pl.ds(at, 16), :] = s
-
-                rows_loop(n, 16, elem)
-            pre[0:rows, :] = mm(dm[0:rows, :], dn_ref[e], ((1,), (1,)))
+                        scol[q, at, :] = s
+
+                rows_loop(n, step, elem)
+            pre[0:rows, :] = mm(dm[here, :], dn_ref[e], ((1,), (1,)))
 
             def back(r):
-                dg[pl.ds(r, 32), :] = (pre[pl.ds(r, 32), :] * der[pl.ds(r, 32), :]).astype(BF)
-
-            rows_loop(rows, 32, back)
-            gdn[e] = gdn[e] + mm(ub[0:rows, :], dm[0:rows, :], ((0,), (0,)))
-            gup[e] = gup[e] + mm(dg[0:rows, :], hm, ((0,), (0,)))
+                t = pl.ds(r, rows // 4)
+                dg[pl.ds(pl.multiple_of(at0 + r, 16), rows // 4), :] = (pre[t, :] * der[t, :]).astype(BF)
+
+            rows_loop(rows, rows // 4, back)
             if e:
-                m[0:rows, :] = mm(dg[0:rows, :], up_ref[e], ((1,), (1,)))
+                m[0:rows, :] = mm(dg[here, :], up_ref[e], ((1,), (1,)))
                 for q in range(4):
-
-                    def addx(r):
-                        t = pl.ds(pl.multiple_of(q * T + off + r, 16), 16)
-                        dxacc[t, :] = dxacc[t, :] + m[pl.ds(pl.multiple_of(q * n + r, 16), 16), :]
-
-                    rows_loop(n, 16, addx)
+                    t = slice(q * T + off, q * T + off + n)
+                    dxacc[t, :] = dxacc[t, :] + m[q * n : q * n + n, :]
             else:
-                dxacc[...] = mm(dg[...], up_ref[0], ((1,), (1,)))
+                dxacc[...] = mm(dg[here, :], up_ref[0], ((1,), (1,)))
         for q in range(4):
             psc[base + q] = scol[q].T[0:8, :]
-
-            def out(r):
-                t = pl.ds(pl.multiple_of(q * T + r, 16), 16)
-                part[0, base + q, pl.ds(r, 16), :] = dxacc[t, :].astype(BF)
-                part[1, base + q, pl.ds(r, 16), :] = yacc[t, :].astype(BF)
-
-            rows_loop(T, 16, out)
-
-    def r_copy(kind, a, lev, src, dst, dev):
-        return remote(src, dst, rs_s.at[kind, a, lev], rs_r.at[kind, a, lev], (core, dev))
-
-    def rs_a(k):
-        lev = lev_of(k)
-        odd = k % 2
-        for a in range(2):
-            r_copy(0, a, lev, part.at[a, lev * 4 + dq], ra.at[a, lev], yn + odd * (xn - yn)).start()
-
-    def rs_b(k):
-        lev = lev_of(k)
-        odd = k % 2
-        via = lev * 4 + xq + odd * (yq - xq)
-        for a in range(2):
-            r_copy(0, a, lev, ra.at[a, lev], ra.at[a, lev], xn).wait_recv()
-
-            def add(r):
-                t = pl.ds(r, 16)
-                part[a, via, t, :] = (part[a, via, t, :].astype(F32) + ra[a, lev, t, :].astype(F32)).astype(BF)
-
-            rows_loop(T, 16, add)
-            r_copy(1, a, lev, part.at[a, lev * 4 + xq], rbx.at[a, lev], xn).start()
-            r_copy(2, a, lev, part.at[a, lev * 4 + yq], rby.at[a, lev], yn).start()
-
-    def rs_c(k):
-        lev = lev_of(k)
-        own = lev * 4 + p
-        for a in range(2):
-            r_copy(1, a, lev, rbx.at[a, lev], rbx.at[a, lev], xn).wait_recv()
-            r_copy(2, a, lev, rby.at[a, lev], rby.at[a, lev], yn).wait_recv()
-
-            def add(r):
-                t = pl.ds(r, 16)
-                tot = part[a, own, t, :].astype(F32) + rbx[a, lev, t, :].astype(F32) + rby[a, lev, t, :].astype(F32)
-
-                @pl.when(k == 0)
-                def _():
-                    final[a, t, :] = tot
-
-                @pl.when(k > 0)
-                def _():
-                    part[a, own, t, :] = tot.astype(BF)
-
-            rows_loop(T, 16, add)
-
-            @pl.when(k > 0)
-            def _():
-                remote(
-                    part.at[a, own], rd.at[a, z], rs_s.at[3, a, lev], rs_r.at[3, a, z], (core, lev * 4 + p)
-                ).start()
-
-    stage_a(1)
+            t = slice(q * T, q * T + T)
+            part[base + q] = dxacc[t, :].astype(BF)
+            y_out[base + q] = yacc[t, :].astype(BF)
+
+    def weight_grads(lev):
+        for e in range(3):
+            n = LO if e else T
+            off = HI if e == 2 else 0
+            here = slice(first[e], first[e] + size[e])
+            hm = hall[pl.ds(lev * 4, 4), off : off + n, :].reshape(size[e], D)
+            gdn[e] = gdn[e] + mm(ub[here, :], dm[here, :], ((0,), (0,)))
+            gup[e] = gup[e] + mm(dg[here, :], hm, ((0,), (0,)))
+
+    hg.a(1)
+    hg.b(0)
+    hg.a(2)
 
     @pl.loop(0, L)
     def _(k):
-        stage_b(k)
-
-        @pl.when(k < L - 2)
+        hg.c(k)
+
+        @pl.when(k < L - 1)
         def _():
-            stage_a(k + 2)
+            hg.b(k + 1)
+
+        @pl.when(k < L - 3)
+        def _():
+            hg.a(k + 3)
 
         compute(lev_of(k))
-        rs_a(k)
+        rg.a(k)
 
         @pl.when(k > 0)
         def _():
-            rs_c(k - 1)
-
-        rs_b(k)
+            rg.b(k - 1)
+
+        @pl.when(k > 1)
+        def _():
+            rg.c(k - 2)
+
+        weight_grads(lev_of(k))
 
     half = D // 2
     other = pl.multiple_of((1 - core) * half, half)
@@ -294,11 +420,13 @@
         to = (me + i) % S
         remote(psc.at[to], screcv.at[i], sm_s.at[1, i], sm_r.at[1], (core, to)).start()
 
-    rs_c(L - 1)
+    rg.b(L - 1)
+    rg.c(L - 2)
     c_up.wait_recv()
     for e in range(3):
         tot = gup[e, :, pl.ds(mine_d, half)] + sib_up[e]
         gsend[e] = tot.T.astype(BF)
+    rg.c(L - 1)
     WR = half // S
     screcv[0] = psc[me]
 
@@ -316,21 +444,8 @@
     gdn0_out[...] = gdn[0, pl.ds(mine_f, FR), :] + sib_dn[0]
     for e in range(1, 3):
         gdn12_out[e - 1] = gdn[e, pl.ds(mine_f, FR), :] + sib_dn[e]
-
-    @pl.loop(1, L)
-    def _(k):
-        lev = lev_of(k)
-        for a in range(2):
-            r_copy(3, a, lev, rd.at[a, lev], rd.at[a, lev], xn).wait_recv()
-
-            def add(r):
-                t = pl.ds(r, 16)
-                final[a, t, :] = final[a, t, :] + rd[a, lev, t, :].astype(F32)
-
-            rows_loop(T, 16, add)
-
-    dh_out[...] = final[0]
-    y_out[...] = final[1]
+    for k in range(1, L):
+        rg.d(k)
     remote(screcv.at[pl.ds(1, S - 1)], screcv.at[pl.ds(1, S - 1)], sm_s.at[1, 0], sm_r.at[1], (core, xn)).wait_recv()
     sc_out[...] = jnp.sum(screcv[...], axis=0)
     remote(grecv.at[pl.ds(0, S - 1)], grecv.at[pl.ds(0, S - 1)], sm_s.at[2, 0], sm_r.at[2], (core, xn)).wait_recv()
@@ -338,6 +453,8 @@
 
     c_up.wait_send()
     c_dn.wait_send()
+    hg.finish()
+    rg.finish()
 
     @pl.loop(1, S)
     def _(i):
@@ -345,35 +462,22 @@
         remote(psc.at[0], screcv.at[0], sm_s.at[1, i], sm_r.at[1], (core, xn)).wait_send()
         g_copy(i, (me + i) % S).wait_send()
 
-    @pl.loop(0, L)
-    def _(k):
-        lev = lev_of(k)
-        for kind in range(1, 4):
-            h_copy(kind, lev, hall.at[0], 0, xn).wait_send()
-        for a in range(2):
-            for kind in range(3):
-                r_copy(kind, a, lev, ra.at[a, 0], ra.at[a, 0], xn).wait_send()
-
-        @pl.when(k > 0)
-        def _():
-            h_copy(0, lev, hall.at[0], 0, xn).wait_send()
-            for a in range(2):
-                r_copy(3, a, lev, ra.at[a, 0], ra.at[a, 0], xn).wait_send()
-
 
 def ffn_call(h2b, scal, dy_all, ups, downs):
     S, T, D = dy_all.shape
     F = ups.shape[2]
     L = S // 4
     WR = D // 2 // S
+    rows = 4 * T + 8 * 80
     vm = pl.BlockSpec(memory_space=pltpu.VMEM)
     V = pltpu.VMEM
     dma = pltpu.SemaphoreType.DMA
     sds = jax.ShapeDtypeStruct
+    blocks = V((L, T, D), BF)
     return pl.pallas_call(
         ffn_kernel,
         out_shape=(
-            sds((T, D), F32), sds((T, D), F32), sds((8, 128), F32), sds((S, 3, WR, F), BF),
+            sds((S, T, D), BF), sds((T, D), F32), sds((8, 128), F32), sds((S, 3, WR, F), BF),
             sds((F // 2, D), F32), sds((2, F // 2, D), F32),
         ),
         in_specs=[vm] * 5,
@@ -381,75 +485,17 @@
         scratch_shapes=[
             V((S, T, D), BF), V((S, 8, 128), F32), V((S, 8, 128), F32), V((S, 8, 128), F32),
             V((4, T, 128), F32), V((4, T, 128), F32),
-            V((2, S, T, D), BF), V((2, L, T, D), BF), V((2, L, T, D), BF), V((2, L, T, D), BF), V((2, L, T, D), BF),
-            V((2, T, D), F32),
-            V((4 * T, F), F32), V((4 * T, F), F32), V((4 * T, F), BF), V((4 * T, F), BF), V((4 * T, D), BF),
+            V((S, T, D), BF), blocks, blocks, blocks, blocks,
+            V((4 * T, F), F32), V((4 * T, F), F32), V((rows, F), BF), V((rows, F), BF), V((rows, D), BF),
             V((4 * T, D), F32), V((4 * T, D), F32), V((4 * T, D), F32),
             V((3, F, D), F32), V((3, F, D), F32), V((3, F // 2, D), F32), V((3, F, D // 2), F32),
             V((3, D // 2, F), BF), V((S, 3, WR, F), BF),
-            dma((4, L)), dma((4, L)), dma((4, 2, L)), dma((4, 2, L)), dma((2,)), dma((2,)), dma((3, S)), dma((3,)),
+            dma((5, L)), dma((5, L)), dma((4, L)), dma((4, L)), dma((2,)), dma((2,)), dma((3, S)), dma((3,)),
         ],
         compiler_params=pltpu.CompilerParams(collective_id=2, has_side_effects=True, vmem_limit_bytes=64000000),
         cost_estimate=pl.CostEstimate(flops=15 * 10**9, bytes_accessed=20 * 2**20, transcendentals=2**20),
         name="ffn",
     )(h2b, scal, dy_all, ups, downs)
-
-
-def tree_gather(at, own, ss, rs, dev, levels):
-    core, z, p, xq, yq, dq = dev
-    xn, yn = z * 4 + xq, z * 4 + yq
-    me = z * 4 + p
-    lev_of, L = levels
-
-    def copy(kind, slot, src, idx, to):
-        return remote(src, at(idx), ss.at[kind, slot], rs.at[kind, slot], (core, to))
-
-    class Stages:
-        @staticmethod
-        def start():
-            @pl.loop(1, L)
-            def _(k):
-                lev = lev_of(k)
-                remote(own, at(me), ss.at[0, lev], rs.at[0, z], (core, lev * 4 + p)).start()
-
-            copy(1, z, own, me, xn).start()
-            copy(2, z, own, me, yn).start()
-
-        @staticmethod
-        def a(k):
-            lev = lev_of(k)
-            idx = lev * 4 + p
-            copy(0, lev, own, idx, xn).wait_recv()
-            copy(1, lev, at(idx), idx, xn).start()
-            copy(2, lev, at(idx), idx, yn).start()
-
-        @staticmethod
-        def b(k):
-            lev = lev_of(k)
-            odd = k % 2
-            copy(1, lev, own, lev * 4 + xq, xn).wait_recv()
-            copy(2, lev, own, lev * 4 + yq, yn).wait_recv()
-            idx = lev * 4 + xq + odd * (yq - xq)
-            copy(3, lev, at(idx), idx, yn + odd * (xn - yn)).start()
-
-        @staticmethod
-        def c(k):
-            lev = lev_of(k)
-            copy(3, lev, own, lev * 4 + dq, xn).wait_recv()
-
-        @staticmethod
-        def finish():
-            @pl.loop(0, L)
-            def _(k):
-                lev = lev_of(k)
-                for kind in range(1, 4):
-                    copy(kind, lev, own, me, xn).wait_send()
-
-                @pl.when(k > 0)
-                def _():
-                    copy(0, lev, own, me, xn).wait_send()
-
-    return Stages
 
 
 def sort_matrix(ids_e, ids_s, T):
@@ -477,13 +523,10 @@
     L = S // 4
     me, core, z, p, xq, yq, dq = place_of()
     xn = z * 4 + xq
-    sgn = 1 - 2 * (z // (L // 2))
     my = core * S + me
     sib = (1 - core, me)
     greet(S, core)
-
-    def lev_of(k):
-        return (z + k * sgn + L) % L
+    lev_of = level_order(z, L)
 
     dev, levels = (core, z, p, xq, yq, dq), (lev_of, L)
 
@@ -539,17 +582,17 @@
     ord_row = mm(place[0:16, :].astype(BF), permb, ((1,), (1,)))[0:1, :]
     bias[...] = jnp.where((same > 0.5) & (ord_row <= ord_col), 0.0, -1e30)
 
-    lane = lax.broadcasted_iota(jnp.int32, (16, 128), 1)
+    lane = lax.broadcasted_iota(jnp.int32, (64, 128), 1)
 
     def norm1(r):
-        t = pl.ds(r, 16)
+        t = pl.ds(r, 64)
         v = xs[t, :]
         cen = v - jnp.mean(v, axis=1, keepdims=True)
         inv = lax.rsqrt(jnp.mean(cen * cen, axis=1, keepdims=True) + 1e-05)
         u1_out[t, :] = cen * inv
         stat_out[t, :] = jnp.where(lane == 8, inv, 0.0)
 
-    rows_loop(T, 16, norm1)
+    rows_loop(T, 64, norm1)
 
     w1.a(1)
     w1.b(0)
@@ -625,10 +668,10 @@
     count_out[...] = cnt
 
     def norm1b(r):
-        t = pl.ds(r, 16)
+        t = pl.ds(r, 64)
         h1b[t, :] = (u1_out[t, :] * small_out[0:1, :] + small_out[1:2, :]).astype(BF)
 
-    rows_loop(T, 16, norm1b)
+    rows_loop(T, 64, norm1b)
     c1(L - 1)
     w2.a(1)
     w2.b(0)
@@ -694,7 +737,7 @@
     tmp[...] = mm(o_out[...], full(3))
 
     def norm2(r):
-        t = pl.ds(r, 16)
+        t = pl.ds(r, 64)
         v = xs[t, :] + tmp[t, :]
         x1_out[t, :] = v
         cen = v - jnp.mean(v, axis=1, keepdims=True)
@@ -712,7 +755,7 @@
 
         r0, r1 = soft(lg[0], lg[1])
         k0, k1 = soft(lg[2], lg[3])
-        row = (lax.broadcasted_iota(jnp.int32, (16, 1), 0) + r).astype(F32)
+        row = (lax.broadcasted_iota(jnp.int32, (64, 1), 0) + r).astype(F32)
         is0 = row < n0
         gate = jnp.where(is0, r0, r1)
         we = k0 * gate
@@ -722,7 +765,7 @@
             st = st + jnp.where(lane == i, col, 0.0)
         stat_out[t, :] = st
 
-    rows_loop(T, 16, norm2)
+    rows_loop(T, 64, norm2)
     scal_out[...] = stat_out[...].T[0:8, :]
 
     for k in range(2, L):
@@ -785,7 +828,7 @@
         out_specs=(vm,) * 14 + (hb,) * 4,
         scratch_shapes=[
             V((4, N, WR, D), BF), V((N, 16, 128), F32), V((T, D), BF), V((T, T), F32), V((T, D), F32), V((T, D), F32),
-            dma((3, 4, L)), dma((3, 4, L)), dma((3, max(L, 4))), dma((3, max(L, 4))), dma((2, S)), dma((2,)), dma((10,)),
+            dma((3, 5, L)), dma((3, 5, L)), dma((3, max(L, 4))), dma((3, max(L, 4))), dma((2, S)), dma((2,)), dma((10,)),
         ],
         compiler_params=pltpu.CompilerParams(collective_id=1, has_side_effects=True, vmem_limit_bytes=60000000),
         cost_estimate=pl.CostEstimate(flops=2 * 10**9, bytes_accessed=40 * 2**20, transcendentals=2**20),
@@ -793,94 +836,12 @@
     )(x, dy, docs, es, ss, small, *ws, wu, eu, wd, ed)
 
 
-def tree_scatter(part, ra, rbx, rby, rd, final, ss, rs, dev, levels):
-    core, z, p, xq, yq, dq = dev
-    xn, yn = z * 4 + xq, z * 4 + yq
-    lev_of, L = levels
-    R = part.shape[1]
-
-    def copy(kind, lev, src, dst, to):
-        return remote(src, dst, ss.at[kind, lev], rs.at[kind, lev], (core, to))
-
-    class Stages:
-        @staticmethod
-        def a(k):
-            lev = lev_of(k)
-            odd = k % 2
-            copy(0, lev, part.at[lev * 4 + dq], ra.at[lev], yn + odd * (xn - yn)).start()
-
-        @staticmethod
-        def b(k):
-            lev = lev_of(k)
-            odd = k % 2
-            via = lev * 4 + xq + odd * (yq - xq)
-            copy(0, lev, ra.at[lev], ra.at[lev], xn).wait_recv()
-
-            def add(r):
-                t = pl.ds(r, 16)
-                part[via, t, :] = (part[via, t, :].astype(F32) + ra[lev, t, :].astype(F32)).astype(BF)
-
-            rows_loop(R, 16, add)
-            copy(1, lev, part.at[lev * 4 + xq], rbx.at[lev], xn).start()
-            copy(2, lev, part.at[lev * 4 + yq], rby.at[lev], yn).start()
-
-        @staticmethod
-        def c(k):
-            lev = lev_of(k)
-            own = lev * 4 + p
-            copy(1, lev, rbx.at[lev], rbx.at[lev], xn).wait_recv()
-            copy(2, lev, rby.at[lev], rby.at[lev], yn).wait_recv()
-
-            def add(r):
-                t = pl.ds(r, 16)
-                tot = part[own, t, :].astype(F32) + rbx[lev, t, :].astype(F32) + rby[lev, t, :].astype(F32)
-
-                @pl.when(k == 0)
-                def _():
-                    final[t, :] = tot
-
-                @pl.when(k > 0)
-                def _():
-                    part[own, t, :] = tot.astype(BF)
-
-            rows_loop(R, 16, add)
-
-            @pl.when(k > 0)
-            def _():
-                remote(part.at[own], rd.at[z], ss.at[3, lev], rs.at[3, z], (core, lev * 4 + p)).start()
-
-        @staticmethod
-        def d(k):
-            lev = lev_of(k)
-            copy(3, lev, rd.at[lev], rd.at[lev], xn).wait_recv()
-
-            def add(r):
-                t = pl.ds(r, 16)
-                final[t, :] = final[t, :] + rd[lev, t, :].astype(F32)
-
-            rows_loop(R, 16, add)
-
-        @staticmethod
-        def finish():
-            @pl.loop(0, L)
-            def _(k):
-                lev = lev_of(k)
-                for kind in range(3):
-                    copy(kind, lev, ra.at[0], ra.at[0], xn).wait_send()
-
-                @pl.when(k > 0)
-                def _():
-                    copy(3, lev, ra.at[0], ra.at[0], xn).wait_send()
-
-    return Stages
-
-
 def back_kernel(
-    dh_ref, y_ref, sc_ref, small_ref, stat_ref, u1_ref, u2_ref, x1_ref, dys_ref,
-    q_ref, k_ref, v_ref, p_ref, o_ref, e_ref, s_ref, w_hbm,
+    dh_ref, sc_ref, small_ref, stat_ref, u1_ref, u2_ref, x1_ref, dys_ref,
+    q_ref, k_ref, v_ref, p_ref, o_ref, e_ref, s_ref, y_hbm, w_hbm,
     lo_out, ig_out, gqkv_out, go_out, smalls_out,
     wbuf, perm, accs, dx1, dab, do, dq, dk, dv, h1b, dh1, tmpb, keep, send, recv,
-    part0, ra0, rbx0, rby0, rd0, part1, ra1, rbx1, rby1, rd1, smine, ssib, srecv,
+    part0, ra0, rbx0, rby0, rd0, part1, ra1, rbx1, rby1, rd1, ypart, ray, rbxy, rbyy, rdy, ysum, lsort, smine, ssib, srecv,
     rs_s, rs_r, sib_s, sib_r, sm_s, sm_r, loc,
 ):
     T, D = dh_ref.shape
@@ -889,20 +850,28 @@
     half = D // 2
     me, core, z, p, xq, yq, dgq = place_of()
     xn = z * 4 + xq
-    sgn = 1 - 2 * (z // (L // 2))
     sib = (1 - core, me)
     greet(S, core)
-
-    def lev_of(k):
-        return (z + k * sgn + L) % L
+    lev_of = level_order(z, L)
 
     dev, levels = (core, z, p, xq, yq, dgq), (lev_of, L)
     g0 = tree_scatter(part0, ra0, rbx0, rby0, rd0, go_out, rs_s.at[0], rs_r.at[0], dev, levels)
     g1 = tree_scatter(part1, ra1, rbx1, rby1, rd1, gqkv_out, rs_s.at[1], rs_r.at[1], dev, levels)
+    gy = tree_scatter(ypart, ray, rbxy, rbyy, rdy, ysum, rs_s.at[2], rs_r.at[2], dev, levels)
+    far = list(reversed(range(L)))
+    fetch = []
+    for k in far:
+        some = pl.ds(lev_of(k) * 4, 4)
+        fetch.append(pltpu.make_async_copy(y_hbm.at[some], ypart.at[some], loc.at[4 + k]))
+    for c in fetch:
+        c.start()
     loads = [pltpu.make_async_copy(w_hbm.at[i], wbuf.at[i], loc.at[i]) for i in range(4)]
     for i in (3, 0, 1, 2):
         loads[i].start()
 
+    for k, c in zip(far, fetch):
+        c.wait()
+        gy.a(k)
     perm_f, n0 = sort_matrix(e_ref[...], s_ref[...], T)
     perm[...] = perm_f.astype(BF)
     accs[...] = jnp.zeros_like(accs)
@@ -910,13 +879,13 @@
     dh1[:, 0:128] = scol
 
     def acc(i, v):
-        accs[i] = accs[i] + (v[0:8] + v[8:16])
+        accs[i] = accs[i] + jnp.sum(v.reshape(32 // 8, 8, v.shape[1]), axis=0)
 
     def norm2(r):
-        t = pl.ds(r, 16)
+        t = pl.ds(r, 32)
         st = stat_ref[t, :]
         c1, c0, gate, r0, r1, inv = (st[:, i : i + 1] for i in (0, 3, 4, 5, 6, 9))
-        row = (lax.broadcasted_iota(jnp.int32, (16, 1), 0) + r).astype(F32)
+        row = (lax.broadcasted_iota(jnp.int32, (32, 1), 0) + r).astype(F32)
         is0 = row < n0
         s3 = dh1[t, 0:128]
         sm = s3[:, 0:1]
@@ -941,10 +910,9 @@
         g = dys_ref[t, :].astype(F32) + inv * inner
         dx1[t, :] = g
         dab[t, :] = g.astype(BF)
-        tmpb[t, :] = (x1_ref[t, :] + y_ref[t, :]).astype(BF)
         h1b[t, :] = (u1_ref[t, :] * small_ref[0:1, :] + small_ref[1:2, :]).astype(BF)
 
-    rows_loop(T, 16, norm2)
+    rows_loop(T, 32, norm2)
 
     other = pl.multiple_of((1 - core) * half, half)
     mine = pl.multiple_of(core * half, half)
@@ -964,14 +932,14 @@
             t = pl.ds(pl.multiple_of(j * WR, WR), WR)
             part[j, at : at + WR, :] = (keep[i, t, :] + recv[i, t, :].astype(F32)).astype(BF)
 
+    for k in far:
+        gy.b(k)
     c_o = weight_grad(3, o_ref, dab)
     loads[3].wait()
     do[...] = mm(dab[...], wbuf[3], ((1,), (1,))).astype(BF)
     join(3, c_o, part0, 0)
-    for k in reversed(range(L)):
+    for k in far:
         g0.a(k)
-
-    lo_out[...] = mm(perm[...], tmpb[...], ((0,), (0,))).astype(BF)
 
     low = lax.broadcasted_iota(jnp.int32, (T, 128), 1) < 64
     lowb = low.astype(F32).astype(BF)
@@ -990,7 +958,14 @@
         dk[:, ln] = mm(ds, q2, ((0,), (0,))).astype(BF)
         dv[:, ln] = mm(pr.astype(BF), do2, ((0,), (0,))).astype(BF)
 
-    @pl.loop(0, D // 128)
+    @pl.loop(0, D // 256)
+    def _(j):
+        heads(j)
+
+    for k in far:
+        gy.c(k)
+
+    @pl.loop(D // 256, D // 128)
     def _(j):
         heads(j)
 
@@ -1013,7 +988,7 @@
         g0.c(k)
 
     def norm1(r):
-        t = pl.ds(r, 16)
+        t = pl.ds(r, 32)
         inv = stat_ref[t, :][:, 8:9]
         u = u1_ref[t, :]
         d = dh1[t, :]
@@ -1023,7 +998,7 @@
         inner = e - jnp.mean(e, axis=1, keepdims=True) - u * jnp.mean(e * u, axis=1, keepdims=True)
         tmpb[t, :] = (dx1[t, :] + inv * inner).astype(BF)
 
-    rows_loop(T, 16, norm1)
+    rows_loop(T, 32, norm1)
     for i in range(8):
         smine[i : i + 1, :] = jnp.sum(accs[i], axis=0, keepdims=True)
     c_s = remote(smine, ssib, sib_s.at[4], sib_r.at[4], sib)
@@ -1047,7 +1022,11 @@
         s_copy(i).start()
 
     srecv[me] = s_at(me)[...]
-    for k in reversed(range(L)):
+    for k in range(1, L):
+        gy.d(k)
+    lsort[...] = (x1_ref[...] + ysum[...]).astype(BF)
+    lo_out[...] = mm(perm[...], lsort[...], ((0,), (0,))).astype(BF)
+    for k in far:
         g1.c(k)
     for k in range(1, L):
         g0.d(k)
@@ -1056,6 +1035,7 @@
     smalls_out[...] = jnp.sum(srecv[...], axis=0)
     for k in range(1, L):
         g1.d(k)
+    gy.finish()
     g0.finish()
     g1.finish()
     for c in (c_o, c_v, c_k, c_q):
@@ -1085,7 +1065,7 @@
         out_shape=(
             sds((T, D), BF), sds((T, D), BF), sds((3 * WR, D), F32), sds((WR, D), F32), sds((8, 128), F32),
         ),
-        in_specs=[vm] * 16 + [hb],
+        in_specs=[vm] * 15 + [hb, hb],
         out_specs=(vm,) * 5,
         scratch_shapes=[
             V((4, D, D), BF), V((T, T), BF), V((8, 8, D), F32), V((T, D), F32), row, row, row, row, row, row,
@@ -1093,14 +1073,16 @@
         ]
         + rs_bufs(WR)
         + rs_bufs(3 * WR)
+        + rs_bufs(T)
         + [
+            V((T, D), F32), V((T, D), BF),
             V((8, D), F32), V((8, D), F32), V((S, 8, 128), F32),
-            dma((2, 4, L)), dma((2, 4, L)), dma((5,)), dma((5,)), dma((S,)), dma((1,)), dma((4,)),
+            dma((3, 4, L)), dma((3, 4, L)), dma((5,)), dma((5,)), dma((S,)), dma((1,)), dma((4 + L,)),
         ],
         compiler_params=pltpu.CompilerParams(collective_id=3, has_side_effects=True, vmem_limit_bytes=60000000),
         cost_estimate=pl.CostEstimate(flops=4 * 10**9, bytes_accessed=20 * 2**20, transcendentals=2**20),
         name="back",
-    )(dh, y, sc, small, stat, u1, u2, x1, dys, q, k, v, p, o, es, ss, wa)
+    )(dh, sc, small, stat, u1, u2, x1, dys, q, k, v, p, o, es, ss, y, wa)
 
 
 def body_plain(
@@ -1287,9 +1269,9 @@
         hidden_in, out_grad, doc_ids, expert_ids.reshape(1, T), slot_ids.reshape(1, T), small,
         (w_query, w_key, w_value, w_out), w_up, expert_up, w_down, expert_down, S,
     )
-    yfull, dh2, sc, gup, gdn0, gdn12 = ffn_call(h2b, scal8, dy_all, ups, downs)
+    y_parts, dh2, sc, gup, gdn0, gdn12 = ffn_call(h2b, scal8, dy_all, ups, downs)
     layer_out, input_grad, gqkv, gwo, smalls = back_call(
-        dh2, yfull, sc, small, stat, u1, u2, x1, dys, q, k, v, p, o,
+        dh2, y_parts, sc, small, stat, u1, u2, x1, dys, q, k, v, p, o,
         expert_ids.reshape(1, T), slot_ids.reshape(1, T), wa.reshape(4, D, D), S,
     )
     mine = lax.dynamic_slice_in_dim(smalls, dev % group * WR, WR, 1)

time: 419 us -> 334 us (0.80)
  Pallas kernels: 399 us -> 316 us
    pallas_call x1, Pallas kernels: 228 us -> 120 us  [ffn_call(): pl.pallas_call(ffn_kernel, out_shape=(sds((S, T, D), BF), sds((T, D), F32...]
    pallas_call x1, Pallas kernels: 59.2 us -> 86.4 us  [back_call(): pl.pallas_call(back_kernel, out_shape=(sds((T, D), BF), sds((T, D), BF),...]
where the time goes in v5:
time: 334 us
  Pallas kernels  316 us (95%)
  local copies, waits for them, and re-layouts  15.1 us (5%)
    pallas_call x1, Pallas kernels, ffn_call(): pl.pallas_call(ffn_kernel, out_shape=(sds((S, T, D), BF), sds((T, D), F32...  120 us
    pallas_call x1, Pallas kernels, attn_call(): pl.pallas_call(attn_kernel, out_shape=(row, sds((T, 128), F32), sds((8, T...  109 us
    pallas_call x1, Pallas kernels, back_call(): pl.pallas_call(back_kernel, out_shape=(sds((T, D), BF), sds((T, D), BF),...  86.4 us

profile of v5, /device:TPU:0, one launch (start us, length us, event | category | flops | bytes accessed | tf_op | source)
XLA Modules:
  0.0 333.7 jit_solution(11651219472058090791)
XLA Ops:
  0.7 0.7 slice_bitcast_fusion.6
  1.4 0.7 stack.40
  2.2 0.1 tile.10
  2.3 0.6 fusion.small_ref
  2.9 109.3 %attn.1 = (bf16[128,1024]{1,0:T(8,128)(2,1)}, f32[128,128]{1,0:T(8,128)}, f32[8,128]{1,0:T(8,128)}, f32[128,1024]{1,0:T(8,128)}, f32[128,1024]{1,0:T(8,128)}, /*...) custom-call(bf16[128,1024]{1,0:T(8,128)(2,1)} %x_ref.1, ...), custom_call_target="tpu_custom_call" | custom-call | flops 2000000000 | bytes 41943040 | tf_op jit(solution)/shard_map/attn/pallas_call | solution.py:820
  112.2 1.2 slice.71
  114.0 120.3 %ffn.1 = (bf16[16,128,1024]{2,1,0:T(8,128)(2,1)}, f32[128,1024]{1,0:T(8,128)}, f32[8,128]{1,0:T(8,128)}, bf16[16,3,32,256]{3,2,1,0:T(8,128)(2,1)}, f32[128,1024]{1,0:T(8,128)}, /*index=5*/f32[2,128,1024]{2,1,0:T(8,128)}) custom-call(bf16[128,1024]{1,0:T(8,128)(2,1)} %get-tuple-element.47.h_ref, f32[8,128]{1,0:T(8,128)} %get-tuple-element.48.scal_ref, ...), custom_call_target="tpu_custom_call" | custom-call | flops 15000000512 | bytes 20971520 | tf_op jit(solution)/shard_map/ffn/pallas_call | solution.py:477
  234.3 86.4 %back.1 = (bf16[128,1024]{1,0:T(8,128)(2,1)}, bf16[128,1024]{1,0:T(8,128)(2,1)}, f32[96,1024]{1,0:T(8,128)}, f32[32,1024]{1,0:T(8,128)}, f32[8,128]{1,0:T(8,128)}) custom-call(f32[128,1024]{1,0:T(8,128)} %get-tuple-element.52.dh_ref, f32[8,128]{1,0:T(8,128)} %get-tuple-element.53.sc_ref, f32[8,1024]{1,0:T(8,128)} %get-tuple-element.54.small_ref, ...), custom_call_target="tpu_custom_call" | custom-call | flops 4000000000 | bytes 20971520 | tf_op jit(solution)/shard_map/back/pallas_call | solution.py:1063
  320.7 0.6 multiply_add_fusion
  321.3 0.7 constant_dynamic-slice_fusion
  322.0 0.5 slice_bitcast_fusion.2
  322.6 0.6 slice_bitcast_fusion
  323.1 1.8 fusion.1
  324.9 0.8 reshape.139
  325.7 0.1 slice.73
  325.9 0.6 copy.39
  326.5 1.2 slice.70
  327.7 0.3 copy.38
  328.0 0.9 squeeze.23
  328.9 1.7 copy.45
  330.5 0.7 copy.46
  331.2 0.7 copy.47
  331.9 0.8 copy.48
  332.7 1.0 copy.49
  (16 shorter events, 0.1 us)
Async XLA Ops:
  234.3 86.4 %copy-start.5 = (f32[2]{0:T(128)S(1)}, f32[2]{0:T(128)}, u32[]{:S(2)}) copy-start(f32[2]{0:T(128)} %param.39) | copy-start | bytes 28
  234.3 90.6 %copy-start.1 = (bf16[16,3,32,256]{3,2,1,0:T(8,128)(2,1)S(1)}, bf16[16,3,32,256]{3,2,1,0:T(8,128)(2,1)}, u32[]{:S(2)}) copy-start(bf16[16,3,32,256]{3,2,1,0:T(8,128)(2,1)} %get-tuple-element.72) | copy-start | bytes 2359300
  325.7 4.8 %copy-start.3 = (bf16[128,1024]{1,0:T(8,128)(2,1)S(1)}, bf16[128,1024]{1,0:T(8,128)(2,1)}, u32[]{:S(2)}) copy-start(bf16[128,1024]{1,0:T(8,128)(2,1)} %get-tuple-element.114) | copy-start | bytes 786436
  325.9 5.4 %copy-start.4 = (f32[32,1024]{1,0:T(8,128)S(1)}, f32[32,1024]{1,0:T(8,128)}, u32[]{:S(2)}) copy-start(f32[32,1024]{1,0:T(8,128)} %get-tuple-element.120) | copy-start | bytes 393220
  325.9 6.0 %copy-start.2 = (f32[128,1024]{1,0:T(8,128)S(1)}, f32[128,1024]{1,0:T(8,128)}, u32[]{:S(2)}) copy-start(f32[128,1024]{1,0:T(8,128)} %get-tuple-element.124) | copy-start | bytes 1572868
  325.9 6.8 %copy-start = (f32[2,128,1024]{2,1,0:T(8,128)S(1)}, f32[2,128,1024]{2,1,0:T(8,128)}, u32[]{:S(2)}) copy-start(f32[2,128,1024]{2,1,0:T(8,128)} %get-tuple-element.128) | copy-start | bytes 3145732

commit v6 on v5

--- a/solution.py
+++ b/solution.py
@@ -97,6 +97,7 @@
     core, z, p, xq, yq, dq = dev
     xn, yn = z * 4 + xq, z * 4 + yq
     me = z * 4 + p
+    pair = me + 4 - 8 * (z % 2)
     lev_of, L = levels
 
     def copy(kind, slot, src, idx, to):
@@ -147,16 +148,32 @@
         @staticmethod
         def b(k):
             lev = lev_of(k)
-            odd = k % 2
+            odd = lev // 2 % 2
             copy(1, lev, own, lev * 4 + xq, xn).wait_recv()
             copy(2, lev, own, lev * 4 + yq, yn).wait_recv()
             idx = lev * 4 + xq + odd * (yq - xq)
-            copy(3, lev, at(idx), idx, yn + odd * (xn - yn)).start()
+
+            @pl.when((lev + z) % 2 == 0)
+            def _():
+                copy(3, lev, at(idx), idx, yn + odd * (xn - yn)).start()
 
         @staticmethod
         def c(k):
             lev = lev_of(k)
-            copy(3, lev, own, lev * 4 + dq, xn).wait_recv()
+            idx = lev * 4 + dq
+
+            @pl.when((lev + z) % 2 == 0)
+            def _():
+                copy(3, lev, own, idx, xn).wait_recv()
+                copy(5, lev, at(idx), idx, pair).start()
+
+        @staticmethod
+        def d(k):
+            lev = lev_of(k)
+
+            @pl.when((lev + z) % 2 == 1)
+            def _():
+                copy(5, lev, own, lev * 4 + dq, pair).wait_recv()
 
         @staticmethod
         def finish():
@@ -171,8 +188,13 @@
             @pl.loop(0, L)
             def _(k):
                 lev = lev_of(k)
-                for kind in range(1, 4):
+                for kind in range(1, 3):
                     copy(kind, lev, own, me, xn).wait_send()
+
+                @pl.when((lev + z) % 2 == 0)
+                def _():
+                    for kind in (3, 5):
+                        copy(kind, lev, own, me, xn).wait_send()
 
             @pl.loop(1, L)
             def _(k):
@@ -185,26 +207,57 @@
     return Stages
 
 
-def tree_scatter(part, ra, rbx, rby, rd, final, ss, rs, dev, levels):
+def tree_scatter(part, ra, rbx, rby, rd, final, ss, rs, dev, levels, rz=None):
     core, z, p, xq, yq, dq = dev
     xn, yn = z * 4 + xq, z * 4 + yq
+    pair = z * 4 + p + 4 - 8 * (z % 2)
     lev_of, L = levels
     R = part.shape[1]
 
     def copy(kind, lev, src, dst, to):
         return remote(src, dst, ss.at[kind, lev], rs.at[kind, lev], (core, to))
 
+    def sides(lev):
+        copy(1, lev, part.at[lev * 4 + xq], rbx.at[lev], xn).start()
+        copy(2, lev, part.at[lev * 4 + yq], rby.at[lev], yn).start()
+
     class Stages:
+        @staticmethod
+        def share(k):
+            lev = lev_of(k)
+
+            @pl.when((lev + z) % 2 == 1)
+            def _():
+                copy(4, lev, part.at[lev * 4 + dq], rz.at[lev // 2], pair).start()
+
         @staticmethod
         def a(k):
             lev = lev_of(k)
-            odd = k % 2
-            copy(0, lev, part.at[lev * 4 + dq], ra.at[lev], yn + odd * (xn - yn)).start()
+            odd = k % 2 if rz is None else lev // 2 % 2
+            diag = lev * 4 + dq
+
+            def send():
+                copy(0, lev, part.at[diag], ra.at[lev], yn + odd * (xn - yn)).start()
+
+            def join():
+                copy(4, lev, rz.at[lev // 2], rz.at[lev // 2], pair).wait_recv()
+
+                def add(r):
+                    t = pl.ds(r, 32)
+                    part[diag, t, :] = (part[diag, t, :].astype(F32) + rz[lev // 2, t, :].astype(F32)).astype(BF)
+
+                rows_loop(R, 32, add)
+                send()
+
+            if rz is None:
+                send()
+            else:
+                pl.when((lev + z) % 2 == 0)(join)
 
         @staticmethod
         def b(k):
             lev = lev_of(k)
-            odd = k % 2
+            odd = k % 2 if rz is None else lev // 2 % 2
             via = lev * 4 + xq + odd * (yq - xq)
             copy(0, lev, ra.at[lev], ra.at[lev], xn).wait_recv()
 
@@ -213,8 +266,23 @@
                 part[via, t, :] = (part[via, t, :].astype(F32) + ra[lev, t, :].astype(F32)).astype(BF)
 
             rows_loop(R, 32, add)
-            copy(1, lev, part.at[lev * 4 + xq], rbx.at[lev], xn).start()
-            copy(2, lev, part.at[lev * 4 + yq], rby.at[lev], yn).start()
+            sides(lev)
+
+        @staticmethod
+        def b0(k):
+            pl.when((lev_of(k) + z) % 2 == 1)(lambda: sides(lev_of(k)))
+
+        @staticmethod
+        def b1(k):
+            pl.when((lev_of(k) + z) % 2 == 0)(lambda: Stages.b(k))
+
+        @staticmethod
+        def c0(k):
+            pl.when((lev_of(k) + z) % 2 == 1)(lambda: Stages.c(k))
+
+        @staticmethod
+        def c1(k):
+            pl.when((lev_of(k) + z) % 2 == 0)(lambda: Stages.c(k))
 
         @staticmethod
         def c(k):
@@ -223,23 +291,26 @@
             copy(1, lev, rbx.at[lev], rbx.at[lev], xn).wait_recv()
             copy(2, lev, rby.at[lev], rby.at[lev], yn).wait_recv()
 
-            def add(r):
+            def add(r, last):
                 t = pl.ds(r, 32)
                 tot = part[own, t, :].astype(F32) + rbx[lev, t, :].astype(F32) + rby[lev, t, :].astype(F32)
-
-                @pl.when(k == 0)
-                def _():
+                if last:
                     final[t, :] = tot
-
-                @pl.when(k > 0)
-                def _():
+                else:
                     part[own, t, :] = tot.astype(BF)
 
-            rows_loop(R, 32, add)
-
-            @pl.when(k > 0)
-            def _():
+            def close():
+                rows_loop(R, 32, lambda r: add(r, True))
+
+            def send():
+                rows_loop(R, 32, lambda r: add(r, False))
                 remote(part.at[own], rd.at[z], ss.at[3, lev], rs.at[3, z], (core, lev * 4 + p)).start()
+
+            if isinstance(k, int):
+                (send if k else close)()
+            else:
+                pl.when(k == 0)(close)
+                pl.when(k > 0)(send)
 
         @staticmethod
         def d(k):
@@ -257,7 +328,13 @@
             @pl.loop(0, L)
             def _(k):
                 lev = lev_of(k)
-                for kind in range(3):
+                for kind in (1, 2):
+                    copy(kind, lev, ra.at[0], ra.at[0], xn).wait_send()
+
+                if rz is None:
+                    copy(0, lev, ra.at[0], ra.at[0], xn).wait_send()
+                else:
+                    kind = (lev + z) % 2 * 4
                     copy(kind, lev, ra.at[0], ra.at[0], xn).wait_send()
 
                 @pl.when(k > 0)
@@ -268,14 +345,14 @@
 
 
 def ffn_kernel(
-    h_ref, scal_ref, dy_ref, up_ref, dn_ref,
+    h_ref, scal_ref, dy_hbm, up_hbm, wd_hbm, ed_hbm, dn_hbm,
     y_out, dh_out, sc_out, gup_out, gdn0_out, gdn12_out,
-    hall, scall, psc, screcv, wcol, scol, part, ra, rbx, rby, rd,
-    pre, der, ub, dg, dm, m, yacc, dxacc, gdn, gup, sib_dn, sib_up, gsend, grecv,
-    ag_s, ag_r, rs_s, rs_r, one_s, one_r, sm_s, sm_r,
+    dy_ref, up_ref, dn_ref, ypart, hall, scall, psc, screcv, wcol, scol, part, ra, rbx, rby, rd,
+    pre, der, ub, dg, dm, m, yacc, dxacc, gdn, gup, sib_dn, sib_up,
+    ag_s, ag_r, rs_s, rs_r, one_s, one_r, sm_s, sm_r, loc, yloc,
 ):
     S, T, D = hall.shape
-    F = up_ref.shape[2]
+    F = up_hbm.shape[2]
     L = S // 4
     LO = 80
     HI = T - LO
@@ -285,8 +362,25 @@
     dev, levels = (core, z, p, xq, yq, dq), (lev_of, L)
     greet(S, core)
     hg = tree_gather(lambda i: hall.at[i], h_ref, ag_s, ag_r, dev, levels)
-    rg = tree_scatter(part, ra, rbx, rby, rd, dh_out, rs_s, rs_r, dev, levels)
+    rgs = []
+    for i in range(2):
+        t = pl.ds(i * (T // 2), T // 2)
+        bufs = [b.at[:, t, :] for b in (part, ra, rbx, rby, rd)]
+        rgs.append(tree_scatter(*bufs, dh_out.at[t], rs_s.at[i], rs_r.at[i], dev, levels))
     hg.start()
+    half_f = F // 2
+    mine_f = pl.ds(pl.multiple_of(core * half_f, half_f), half_f)
+    other_f = pl.ds(pl.multiple_of((1 - core) * half_f, half_f), half_f)
+    pairs = (
+        (up_hbm, up_ref),
+        (wd_hbm, dn_ref.at[0, mine_f]),
+        (ed_hbm, dn_ref.at[pl.ds(1, 2), mine_f]),
+        (dn_hbm, dn_ref.at[:, other_f]),
+        (dy_hbm, dy_ref),
+    )
+    loads = [pltpu.make_async_copy(a, b, loc.at[i]) for i, (a, b) in enumerate(pairs)]
+    for c in loads:
+        c.start()
 
     @pl.loop(1, S)
     def _(i):
@@ -301,7 +395,7 @@
     size = (4 * T, 4 * LO, 4 * LO)
     first = (0, 4 * T, 4 * T + 4 * LO)
 
-    def compute(lev):
+    def compute(lev, between):
         base = lev * 4
         for q in range(4):
             full = jnp.concatenate([scall[base + q], jnp.zeros((120, 128), F32)], axis=0)
@@ -359,11 +453,14 @@
                     dxacc[t, :] = dxacc[t, :] + m[q * n : q * n + n, :]
             else:
                 dxacc[...] = mm(dg[here, :], up_ref[0], ((1,), (1,)))
+            between(e)
         for q in range(4):
             psc[base + q] = scol[q].T[0:8, :]
             t = slice(q * T, q * T + T)
             part[base + q] = dxacc[t, :].astype(BF)
-            y_out[base + q] = yacc[t, :].astype(BF)
+            ypart[base + q] = yacc[t, :].astype(BF)
+        some = pl.ds(base, 4)
+        pltpu.make_async_copy(ypart.at[some], y_out.at[some], yloc.at[lev]).start()
 
     def weight_grads(lev):
         for e in range(3):
@@ -374,44 +471,59 @@
             gdn[e] = gdn[e] + mm(ub[here, :], dm[here, :], ((0,), (0,)))
             gup[e] = gup[e] + mm(dg[here, :], hm, ((0,), (0,)))
 
+    end = (z == 0) | (z == L - 1)
     hg.a(1)
     hg.b(0)
     hg.a(2)
+    pl.when(jnp.logical_not(end))(lambda: hg.a(3))
+    hg.c(0)
+    for c in loads:
+        c.wait()
+
+    def far_a(i):
+        pl.when(end)(lambda: hg.a(i))
 
     @pl.loop(0, L)
     def _(k):
-        hg.c(k)
-
-        @pl.when(k < L - 1)
-        def _():
-            hg.b(k + 1)
-
-        @pl.when(k < L - 3)
-        def _():
-            hg.a(k + 3)
-
-        compute(lev_of(k))
-        rg.a(k)
-
         @pl.when(k > 0)
         def _():
-            rg.b(k - 1)
-
-        @pl.when(k > 1)
+            hg.d(k)
+
+        def between(e):
+            @pl.when(k == 0)
+            def _():
+                for call, i in (((far_a, 3), (hg.b, 1)), ((hg.c, 1), (hg.b, 2)), ())[e]:
+                    call(i)
+
+            @pl.when(k == 1)
+            def _():
+                for call, i in (((hg.c, 2), (hg.b, 3)), ((hg.c, 3),), ())[e]:
+                    call(i)
+
+            if e == 1:
+
+                @pl.when(k > 0)
+                def _():
+                    for g in rgs:
+                        g.b(k - 1)
+
+        compute(lev_of(k), between)
+        for g in rgs:
+            g.a(k)
+
+        @pl.when(k > 0)
         def _():
-            rg.c(k - 2)
+            for g in rgs:
+                g.c(k - 1)
 
         weight_grads(lev_of(k))
 
     half = D // 2
     other = pl.multiple_of((1 - core) * half, half)
     mine_d = pl.multiple_of(core * half, half)
-    FR = F // 2
-    other_f = pl.multiple_of((1 - core) * FR, FR)
-    mine_f = pl.multiple_of(core * FR, FR)
     sib = (1 - core, me)
     c_up = remote(gup.at[:, :, pl.ds(other, half)], sib_up, one_s.at[0], one_r.at[0], sib)
-    c_dn = remote(gdn.at[:, pl.ds(other_f, FR), :], sib_dn, one_s.at[1], one_r.at[1], sib)
+    c_dn = remote(gdn.at[:, other_f, :], sib_dn, one_s.at[1], one_r.at[1], sib)
     c_up.start()
     c_dn.start()
 
@@ -420,56 +532,48 @@
         to = (me + i) % S
         remote(psc.at[to], screcv.at[i], sm_s.at[1, i], sm_r.at[1], (core, to)).start()
 
-    rg.b(L - 1)
-    rg.c(L - 2)
+    for g in rgs:
+        g.b(L - 1)
     c_up.wait_recv()
     for e in range(3):
         tot = gup[e, :, pl.ds(mine_d, half)] + sib_up[e]
-        gsend[e] = tot.T.astype(BF)
-    rg.c(L - 1)
-    WR = half // S
+        gup_out[e] = tot.T.astype(BF)
+        if e == 0:
+            for g in rgs:
+                g.c(L - 1)
     screcv[0] = psc[me]
-
-    def g_copy(i, to):
-        return remote(
-            gsend.at[:, pl.ds(pl.multiple_of(to * WR, WR), WR), :], grecv.at[me], sm_s.at[2, i], sm_r.at[2], (core, to)
-        )
-
-    @pl.loop(1, S)
-    def _(i):
-        g_copy(i, (me + i) % S).start()
-
-    grecv[me] = gsend[:, pl.ds(pl.multiple_of(me * WR, WR), WR), :]
     c_dn.wait_recv()
-    gdn0_out[...] = gdn[0, pl.ds(mine_f, FR), :] + sib_dn[0]
+    gdn0_out[...] = gdn[0, mine_f, :] + sib_dn[0]
     for e in range(1, 3):
-        gdn12_out[e - 1] = gdn[e, pl.ds(mine_f, FR), :] + sib_dn[e]
+        gdn12_out[e - 1] = gdn[e, mine_f, :] + sib_dn[e]
     for k in range(1, L):
-        rg.d(k)
+        for g in rgs:
+            g.d(k)
     remote(screcv.at[pl.ds(1, S - 1)], screcv.at[pl.ds(1, S - 1)], sm_s.at[1, 0], sm_r.at[1], (core, xn)).wait_recv()
     sc_out[...] = jnp.sum(screcv[...], axis=0)
-    remote(grecv.at[pl.ds(0, S - 1)], grecv.at[pl.ds(0, S - 1)], sm_s.at[2, 0], sm_r.at[2], (core, xn)).wait_recv()
-    gup_out[...] = grecv[...]
-
+
+    for i in range(L):
+        some = pl.ds(i * 4, 4)
+        pltpu.make_async_copy(ypart.at[some], y_out.at[some], yloc.at[i]).wait()
     c_up.wait_send()
     c_dn.wait_send()
     hg.finish()
-    rg.finish()
+    for g in rgs:
+        g.finish()
 
     @pl.loop(1, S)
     def _(i):
         remote(scal_ref, scall.at[0], sm_s.at[0, i], sm_r.at[0], (core, xn)).wait_send()
         remote(psc.at[0], screcv.at[0], sm_s.at[1, i], sm_r.at[1], (core, xn)).wait_send()
-        g_copy(i, (me + i) % S).wait_send()
-
-
-def ffn_call(h2b, scal, dy_all, ups, downs):
+
+
+def ffn_call(h2b, scal, dy_all, ups, wd, ed, downs):
     S, T, D = dy_all.shape
     F = ups.shape[2]
     L = S // 4
-    WR = D // 2 // S
     rows = 4 * T + 8 * 80
     vm = pl.BlockSpec(memory_space=pltpu.VMEM)
+    hb = pl.BlockSpec(memory_space=pl.ANY)
     V = pltpu.VMEM
     dma = pltpu.SemaphoreType.DMA
     sds = jax.ShapeDtypeStruct
@@ -477,25 +581,24 @@
     return pl.pallas_call(
         ffn_kernel,
         out_shape=(
-            sds((S, T, D), BF), sds((T, D), F32), sds((8, 128), F32), sds((S, 3, WR, F), BF),
+            sds((S, T, D), BF), sds((T, D), F32), sds((8, 128), F32), sds((3, D // 2, F), BF),
             sds((F // 2, D), F32), sds((2, F // 2, D), F32),
         ),
-        in_specs=[vm] * 5,
-        out_specs=(vm,) * 6,
+        in_specs=[vm] * 2 + [hb] * 5,
+        out_specs=(hb,) + (vm,) * 5,
         scratch_shapes=[
-            V((S, T, D), BF), V((S, 8, 128), F32), V((S, 8, 128), F32), V((S, 8, 128), F32),
+            V((S, T, D), BF), V((3, D, F), BF), V((3, F, D), BF), V((S, T, D), BF), V((S, T, D), BF), V((S, 8, 128), F32), V((S, 8, 128), F32), V((S, 8, 128), F32),
             V((4, T, 128), F32), V((4, T, 128), F32),
             V((S, T, D), BF), blocks, blocks, blocks, blocks,
             V((4 * T, F), F32), V((4 * T, F), F32), V((rows, F), BF), V((rows, F), BF), V((rows, D), BF),
             V((4 * T, D), F32), V((4 * T, D), F32), V((4 * T, D), F32),
             V((3, F, D), F32), V((3, F, D), F32), V((3, F // 2, D), F32), V((3, F, D // 2), F32),
-            V((3, D // 2, F), BF), V((S, 3, WR, F), BF),
-            dma((5, L)), dma((5, L)), dma((4, L)), dma((4, L)), dma((2,)), dma((2,)), dma((3, S)), dma((3,)),
+            dma((6, L)), dma((6, L)), dma((2, 4, L)), dma((2, 4, L)), dma((2,)), dma((2,)), dma((2, S)), dma((2,)), dma((5,)), dma((L,)),
         ],
         compiler_params=pltpu.CompilerParams(collective_id=2, has_side_effects=True, vmem_limit_bytes=64000000),
         cost_estimate=pl.CostEstimate(flops=15 * 10**9, bytes_accessed=20 * 2**20, transcendentals=2**20),
         name="ffn",
-    )(h2b, scal, dy_all, ups, downs)
+    )(h2b, scal, dy_all, ups, wd, ed, downs)
 
 
 def sort_matrix(ids_e, ids_s, T):
@@ -512,7 +615,7 @@
     wu_ref, eu_ref, wd_ref, ed_ref,
     h2b_out, stat_out, scal_out, u1_out, u2_out, x1_out, dys_out, q_out, k_out, v_out, p_out, o_out,
     small_out, count_out, w_out, dyall_out, up_out, dn_out,
-    wbuf, smallbuf, h1b, bias, xs, tmp,
+    wbuf, upb, smallbuf, h1b, bias, xs, tmp,
     ag_s, ag_r, sib_s, sib_r, sm_s, sm_r, loc,
 ):
     T, D = x_ref.shape
@@ -530,19 +633,15 @@
 
     dev, levels = (core, z, p, xq, yq, dq), (lev_of, L)
 
-    def w1_at(i):
-        return wbuf.at[pl.ds(0, 3), core * S + i]
-
-    def w2_at(i):
-        return wbuf.at[3, core * S + i]
-
-    w1 = tree_gather(w1_at, w1_at(me), ag_s.at[0], ag_r.at[0], dev, levels)
-    w2 = tree_gather(w2_at, w2_at(me), ag_s.at[1], ag_r.at[1], dev, levels)
+    def w_at(i):
+        return wbuf.at[:, core * S + i]
+
+    wg = tree_gather(w_at, w_at(me), ag_s.at[0], ag_r.at[0], dev, levels)
     dyg = tree_gather(lambda i: dyall_out.at[i], dys_out, ag_s.at[2], ag_r.at[2], dev, levels)
 
     for i, w in enumerate((wq_ref, wk_ref, wv_ref, wo_ref)):
         wbuf[i, my] = w[...]
-    w1.start()
+    wg.start()
 
     perm, n0 = sort_matrix(e_ref[...], s_ref[...], T)
     smallbuf[my, 0:8, :] = small_ref[...]
@@ -553,21 +652,12 @@
     def _(i):
         remote(smallbuf.at[my], smallbuf.at[my], sm_s.at[0, i], sm_r.at[0], (core, (me + i) % S)).start()
 
-    def dn_own(e0, n, src):
-        dst = dn_out.at[pl.ds(e0, n), pl.ds(pl.multiple_of(core * FR, FR), FR), :]
-        return src, dst
-
-    d0 = dn_own(0, 1, wd_ref)
-    d0 = (wd_ref, dn_out.at[0, pl.ds(pl.multiple_of(core * FR, FR), FR), :])
-    d1 = dn_own(1, 2, ed_ref)
-    dn_copies = []
-    for j, (src, dst) in enumerate((d0, d1)):
-        r = remote(src, dst, sib_s.at[2, j], sib_r.at[2, j], sib)
-        lc = pltpu.make_async_copy(src, dst, loc.at[j])
-        r.start()
-        lc.start()
-        dn_copies.append((r, lc))
-
+    dn_copies = (
+        remote(wd_ref, dn_out.at[0], sib_s.at[2, 0], sib_r.at[2, 0], sib),
+        remote(ed_ref, dn_out.at[pl.ds(1, 2)], sib_s.at[2, 1], sib_r.at[2, 1], sib),
+    )
+    for c in dn_copies:
+        c.start()
     permb = perm.astype(BF)
     xs[...] = mm(permb, x_ref[...])
     dys_out[...] = mm(permb, dy_ref[...]).astype(BF)
@@ -594,10 +684,12 @@
 
     rows_loop(T, 64, norm1)
 
-    w1.a(1)
-    w1.b(0)
-    w1.a(2)
-    w1.b(1)
+    wg.a(1)
+    wg.b(0)
+    wg.a(2)
+    wg.b(1)
+    wg.a(3)
+    wg.c(0)
 
     group = 128 // WR
     remote(smallbuf.at[pl.ds(0, S - 1)], smallbuf.at[pl.ds(0, S - 1)], sm_s.at[0, 0], sm_r.at[0], (core, xn)).wait_recv()
@@ -605,45 +697,13 @@
     c_small = remote(mine_small, mine_small, sib_s.at[2, 2], sib_r.at[2, 2], sib)
     c_small.start()
 
-    def w1_sib(lev, who):
-        b = wbuf.at[pl.ds(0, 3), pl.ds(who * S + lev * 4, 4)]
-        return remote(b, b, sib_s.at[0, lev], sib_r.at[0, lev], sib)
-
-    def w2_sib(lev, who):
-        b = wbuf.at[3, pl.ds(who * S + lev * 4, 4)]
-        return remote(b, b, sib_s.at[1, lev], sib_r.at[1, lev], sib)
-
-    def c1(k):
-        w1.c(k)
-        w1_sib(lev_of(k), core).start()
-
-    def c2(k):
-        w2.c(k)
-        w2_sib(lev_of(k), core).start()
-
-    for k in range(3, L):
-        w1.a(k)
-    c1(0)
-    w2.start()
-    for k in range(2, L):
-        w1.b(k)
-        c1(k - 1)
-
     def up_copy(e, h, i):
         to = (me + i) % S
         src = wu_ref if e == 0 else eu_ref.at[e - 1]
         return remote(
             src.at[:, pl.ds(pl.multiple_of((h * S + to) * FR, FR), FR)],
-            up_out.at[e, pl.ds(pl.multiple_of(my * WR, WR), WR), pl.ds(h * FR, FR)],
+            upb.at[e, pl.ds(pl.multiple_of(my * WR, WR), WR), pl.ds(h * FR, FR)],
             sm_s.at[1, i], sm_r.at[1], (core, to),
-        )
-
-    def up_local(e, h):
-        src = wu_ref if e == 0 else eu_ref.at[e - 1]
-        return pltpu.make_async_copy(
-            src.at[:, pl.ds(pl.multiple_of((h * S + me) * FR, FR), FR)],
-            up_out.at[e, pl.ds(pl.multiple_of(my * WR, WR), WR), pl.ds(h * FR, FR)],
-            loc.at[4 + 2 * e + h],
         )
 
     @pl.loop(1, S)
@@ -654,8 +714,30 @@
 
     for e in range(3):
         for h in range(2):
-            up_local(e, h).start()
-
+            src = wu_ref if e == 0 else eu_ref.at[e - 1]
+            block = src[:, pl.ds(pl.multiple_of((h * S + me) * FR, FR), FR)]
+            upb[e, pl.ds(pl.multiple_of(my * WR, WR), WR), h * FR : (h + 1) * FR] = block
+
+    def w_sib(lev, who):
+        b = wbuf.at[:, pl.ds(who * S + lev * 4, 4)]
+        return remote(b, b, sib_s.at[0, lev], sib_r.at[0, lev], sib)
+
+    def pass_on(k):
+        wg.d(k)
+        w_sib(lev_of(k), core).start()
+
+    pass_on(0)
+    wg.b(2)
+    wg.c(1)
+    wg.b(3)
+    dyg.start()
+    pass_on(1)
+    wg.c(2)
+    pass_on(2)
+    wg.c(3)
+    pass_on(3)
+    dyg.a(1)
+    dyg.b(0)
     c_small.wait_recv()
     for g in range(D // 128):
         part = smallbuf[g * group, 0:8, :]
@@ -672,32 +754,26 @@
         h1b[t, :] = (u1_out[t, :] * small_out[0:1, :] + small_out[1:2, :]).astype(BF)
 
     rows_loop(T, 64, norm1b)
-    c1(L - 1)
-    w2.a(1)
-    w2.b(0)
+    dyg.a(2)
+    dyg.b(1)
     for k in range(L):
-        w1_sib(lev_of(k), 1 - core).wait_recv()
+        w_sib(lev_of(k), 1 - core).wait_recv()
+    w_save = pltpu.make_async_copy(wbuf, w_out, loc.at[3])
+    w_save.start()
 
     def full(i):
         return wbuf[i].reshape(D, D)
 
     tmp[...] = mm(h1b[...], full(0))
     q_out[...] = (tmp[...] * 0.125).astype(BF)
-    for k in range(2, L):
-        w2.a(k)
-    w2.b(1)
+    dyg.a(3)
+    dyg.c(0)
     tmp[...] = mm(h1b[...], full(1))
     k_out[...] = tmp[...].astype(BF)
-    c2(0)
-    dyg.start()
-    for k in range(2, L):
-        w2.b(k)
-        c2(k - 1)
     tmp[...] = mm(h1b[...], full(2))
     v_out[...] = tmp[...].astype(BF)
-    c2(L - 1)
-    dyg.a(1)
-    dyg.b(0)
+    dyg.b(2)
+    dyg.c(1)
 
     low = lax.broadcasted_iota(jnp.int32, (T, 128), 1) < 64
     lowb = low.astype(F32).astype(BF)
@@ -715,25 +791,11 @@
         o2 = mm(pr.astype(BF), v_out[:, ln])
         o_out[:, ln] = jnp.where(low, o2[0:T], o2[T:]).astype(BF)
 
-    half = D // 256
-
-    @pl.loop(0, half)
+    @pl.loop(0, D // 128)
     def _(j):
         heads(j)
 
-    dyg.a(2)
-    dyg.b(1)
-
-    @pl.loop(half, 2 * half)
-    def _(j):
-        heads(j)
-
-    for k in range(3, L):
-        dyg.a(k)
-    for k in range(L):
-        w2_sib(lev_of(k), 1 - core).wait_recv()
-    w_save = pltpu.make_async_copy(wbuf, w_out, loc.at[3])
-    w_save.start()
+    dyg.b(3)
     tmp[...] = mm(o_out[...], full(3))
 
     def norm2(r):
@@ -765,37 +827,34 @@
             st = st + jnp.where(lane == i, col, 0.0)
         stat_out[t, :] = st
 
+    dyg.c(2)
     rows_loop(T, 64, norm2)
     scal_out[...] = stat_out[...].T[0:8, :]
 
-    for k in range(2, L):
-        dyg.b(k)
+    dyg.c(3)
     for k in range(L):
-        dyg.c(k)
-
-    got = up_out.at[:, pl.ds(0, (S - 1) * WR), :]
+        dyg.d(k)
+
+    got = upb.at[:, pl.ds(0, (S - 1) * WR), :]
     remote(got, got, sm_s.at[1, 0], sm_r.at[1], (core, xn)).wait_recv()
-    for e in range(3):
-        for h in range(2):
-            up_local(e, h).wait()
-    mine_up = up_out.at[:, pl.ds(pl.multiple_of(core * S * WR, S * WR), S * WR), :]
+    mine_up = upb.at[:, pl.ds(pl.multiple_of(core * S * WR, S * WR), S * WR), :]
     c_up = remote(mine_up, mine_up, sib_s.at[2, 3], sib_r.at[2, 3], sib)
     c_up.start()
     c_up.wait()
+    up_save = pltpu.make_async_copy(upb, up_out, loc.at[0])
+    up_save.start()
     w_save.wait()
+    up_save.wait()
     dy_local.wait()
-    for r, lc in dn_copies:
-        r.wait()
-        lc.wait()
+    for c in dn_copies:
+        c.wait()
     c_small.wait_send()
-    w1.finish()
-    w2.finish()
+    wg.finish()
     dyg.finish()
 
     @pl.loop(0, L)
     def _(k):
-        w1_sib(k, core).wait_send()
-        w2_sib(k, core).wait_send()
+        w_sib(k, core).wait_send()
 
     @pl.loop(1, S)
     def _(i):
@@ -822,13 +881,13 @@
         out_shape=(
             row, sds((T, 128), F32), sds((8, T), F32), rowf, rowf, rowf, row, row, row, row,
             sds((D // 128, 2 * T, T), F32), row, sds((8, D), F32), sds((8, 128), F32),
-            sds((4, N, WR, D), BF), sds((S, T, D), BF), sds((3, D, 2 * FR), BF), sds((3, 2 * FR, D), BF),
+            sds((4, N, WR, D), BF), sds((S, T, D), BF), sds((3, D, 2 * FR), BF), sds((3, FR, D), BF),
         ),
-        in_specs=[vm] * 10 + [hb] * 4,
+        in_specs=[vm] * 14,
         out_specs=(vm,) * 14 + (hb,) * 4,
         scratch_shapes=[
-            V((4, N, WR, D), BF), V((N, 16, 128), F32), V((T, D), BF), V((T, T), F32), V((T, D), F32), V((T, D), F32),
-            dma((3, 5, L)), dma((3, 5, L)), dma((3, max(L, 4))), dma((3, max(L, 4))), dma((2, S)), dma((2,)), dma((10,)),
+            V((4, N, WR, D), BF), V((3, D, 2 * FR), BF), V((N, 16, 128), F32), V((T, D), BF), V((T, T), F32), V((T, D), F32), V((T, D), F32),
+            dma((3, 6, L)), dma((3, 6, L)), dma((3, max(L, 4))), dma((3, max(L, 4))), dma((2, S)), dma((2,)), dma((10,)),
         ],
         compiler_params=pltpu.CompilerParams(collective_id=1, has_side_effects=True, vmem_limit_bytes=60000000),
         cost_estimate=pl.CostEstimate(flops=2 * 10**9, bytes_accessed=40 * 2**20, transcendentals=2**20),
@@ -838,10 +897,11 @@
 
 def back_kernel(
     dh_ref, sc_ref, small_ref, stat_ref, u1_ref, u2_ref, x1_ref, dys_ref,
-    q_ref, k_ref, v_ref, p_ref, o_ref, e_ref, s_ref, y_hbm, w_hbm,
-    lo_out, ig_out, gqkv_out, go_out, smalls_out,
+    q_ref, k_ref, v_ref, p_ref, o_ref, e_ref, s_ref, y_hbm, w_hbm, gup_ref,
+    lo_out, ig_out, gq_out, gk_out, gv_out, go_out, smalls_out, gup_out,
     wbuf, perm, accs, dx1, dab, do, dq, dk, dv, h1b, dh1, tmpb, keep, send, recv,
-    part0, ra0, rbx0, rby0, rd0, part1, ra1, rbx1, rby1, rd1, ypart, ray, rbxy, rbyy, rdy, ysum, lsort, smine, ssib, srecv,
+    part0, ra0, rbx0, rby0, rd0, rz0, partv, rav, rbxv, rbyv, rdv, rzv, partk, rak, rbxk, rbyk, rdk, rzk,
+    partq, raq, rbxq, rbyq, rdq, rzq, ypart, ray, rbxy, rbyy, rdy, rzy, ysum, lsort, smine, ssib, srecv,
     rs_s, rs_r, sib_s, sib_r, sm_s, sm_r, loc,
 ):
     T, D = dh_ref.shape
@@ -851,13 +911,7 @@
     me, core, z, p, xq, yq, dgq = place_of()
     xn = z * 4 + xq
     sib = (1 - core, me)
-    greet(S, core)
     lev_of = level_order(z, L)
-
-    dev, levels = (core, z, p, xq, yq, dgq), (lev_of, L)
-    g0 = tree_scatter(part0, ra0, rbx0, rby0, rd0, go_out, rs_s.at[0], rs_r.at[0], dev, levels)
-    g1 = tree_scatter(part1, ra1, rbx1, rby1, rd1, gqkv_out, rs_s.at[1], rs_r.at[1], dev, levels)
-    gy = tree_scatter(ypart, ray, rbxy, rbyy, rdy, ysum, rs_s.at[2], rs_r.at[2], dev, levels)
     far = list(reversed(range(L)))
     fetch = []
     for k in far:
@@ -865,13 +919,23 @@
         fetch.append(pltpu.make_async_copy(y_hbm.at[some], ypart.at[some], loc.at[4 + k]))
     for c in fetch:
         c.start()
+    greet(S, core)
+
+    dev, levels = (core, z, p, xq, yq, dgq), (lev_of, L)
+    g0 = tree_scatter(part0, ra0, rbx0, rby0, rd0, go_out, rs_s.at[0], rs_r.at[0], dev, levels, rz0)
+    gv = tree_scatter(partv, rav, rbxv, rbyv, rdv, gv_out, rs_s.at[1], rs_r.at[1], dev, levels, rzv)
+    gk = tree_scatter(partk, rak, rbxk, rbyk, rdk, gk_out, rs_s.at[3], rs_r.at[3], dev, levels, rzk)
+    gq = tree_scatter(partq, raq, rbxq, rbyq, rdq, gq_out, rs_s.at[4], rs_r.at[4], dev, levels, rzq)
+    gy = tree_scatter(ypart, ray, rbxy, rbyy, rdy, ysum, rs_s.at[2], rs_r.at[2], dev, levels, rzy)
+    far = list(reversed(range(L)))
     loads = [pltpu.make_async_copy(w_hbm.at[i], wbuf.at[i], loc.at[i]) for i in range(4)]
     for i in (3, 0, 1, 2):
         loads[i].start()
 
     for k, c in zip(far, fetch):
         c.wait()
-        gy.a(k)
+        gy.share(k)
+        gy.b0(k)
     perm_f, n0 = sort_matrix(e_ref[...], s_ref[...], T)
     perm[...] = perm_f.astype(BF)
     accs[...] = jnp.zeros_like(accs)
@@ -924,23 +988,25 @@
         keep[i] = mm(left[:, pl.ds(mine, half)], right[...], ((0,), (0,)))
         return c
 
-    def join(i, c, part, at):
+    def join(i, c, part):
         c.wait_recv()
 
         @pl.loop(0, S)
         def _(j):
             t = pl.ds(pl.multiple_of(j * WR, WR), WR)
-            part[j, at : at + WR, :] = (keep[i, t, :] + recv[i, t, :].astype(F32)).astype(BF)
-
-    for k in far:
-        gy.b(k)
-    c_o = weight_grad(3, o_ref, dab)
-    loads[3].wait()
-    do[...] = mm(dab[...], wbuf[3], ((1,), (1,))).astype(BF)
-    join(3, c_o, part0, 0)
-    for k in far:
-        g0.a(k)
-
+            part[j] = (keep[i, t, :] + recv[i, t, :].astype(F32)).astype(BF)
+
+
+    def g_copy(i):
+        to = (me + i) % S
+        src = gup_ref.at[:, pl.ds(pl.multiple_of(to * WR, WR), WR), :]
+        return remote(src, gup_out.at[me], sm_s.at[1, i], sm_r.at[1], (core, to))
+
+    @pl.loop(1, S)
+    def _(i):
+        g_copy(i).start()
+
+    gup_out[me] = gup_ref[:, pl.ds(pl.multiple_of(me * WR, WR), WR), :]
     low = lax.broadcasted_iota(jnp.int32, (T, 128), 1) < 64
     lowb = low.astype(F32).astype(BF)
     highb = (1.0 - low.astype(F32)).astype(BF)
@@ -958,35 +1024,6 @@
         dk[:, ln] = mm(ds, q2, ((0,), (0,))).astype(BF)
         dv[:, ln] = mm(pr.astype(BF), do2, ((0,), (0,))).astype(BF)
 
-    @pl.loop(0, D // 256)
-    def _(j):
-        heads(j)
-
-    for k in far:
-        gy.c(k)
-
-    @pl.loop(D // 256, D // 128)
-    def _(j):
-        heads(j)
-
-    c_v = weight_grad(2, h1b, dv)
-    c_k = weight_grad(1, h1b, dk)
-    c_q = weight_grad(0, h1b, dq)
-    for k in reversed(range(L)):
-        g0.b(k)
-    join(2, c_v, part1, 2 * WR)
-    join(1, c_k, part1, WR)
-    join(0, c_q, part1, 0)
-    for k in reversed(range(L)):
-        g1.a(k)
-    for i in range(3):
-        loads[i].wait()
-    dh1[...] = mm(dq[...], wbuf[0], ((1,), (1,)))
-    dh1[...] = dh1[...] + mm(dk[...], wbuf[1], ((1,), (1,)))
-    dh1[...] = dh1[...] + mm(dv[...], wbuf[2], ((1,), (1,)))
-    for k in reversed(range(L)):
-        g0.c(k)
-
     def norm1(r):
         t = pl.ds(r, 32)
         inv = stat_ref[t, :][:, 8:9]
@@ -998,13 +1035,62 @@
         inner = e - jnp.mean(e, axis=1, keepdims=True) - u * jnp.mean(e * u, axis=1, keepdims=True)
         tmpb[t, :] = (dx1[t, :] + inv * inner).astype(BF)
 
+    def each(*calls):
+        for k in far:
+            for call in calls:
+                call(k)
+
+    def start(i, c, part, g):
+        join(i, c, part)
+        each(g.share, g.b0)
+
+    c_o = weight_grad(3, o_ref, dab)
+    each(gy.a)
+    loads[3].wait()
+    do[...] = mm(dab[...], wbuf[3], ((1,), (1,))).astype(BF)
+    start(3, c_o, part0, g0)
+    each(gy.c0)
+
+    @pl.loop(0, D // 256)
+    def _(j):
+        heads(j)
+
+    each(gy.b1)
+
+    @pl.loop(D // 256, D // 128)
+    def _(j):
+        heads(j)
+
+    each(g0.a)
+    c_v = weight_grad(2, h1b, dv)
+    each(g0.c0)
+    c_k = weight_grad(1, h1b, dk)
+    start(2, c_v, partv, gv)
+    c_q = weight_grad(0, h1b, dq)
+    start(1, c_k, partk, gk)
+    each(g0.b1)
+    each(gy.c1)
+    for i in range(3):
+        loads[i].wait()
+    dh1[...] = mm(dq[...], wbuf[0], ((1,), (1,)))
+    start(0, c_q, partq, gq)
+    each(gv.a)
+    dh1[...] = dh1[...] + mm(dk[...], wbuf[1], ((1,), (1,)))
+    each(gk.a, gv.c0)
+    dh1[...] = dh1[...] + mm(dv[...], wbuf[2], ((1,), (1,)))
+    each(gq.a, gv.b1, g0.c1, gk.c0)
     rows_loop(T, 32, norm1)
+    each(gk.b1, gq.c0)
+    each(gq.b1, gv.c1)
+    for k in range(1, L):
+        gy.d(k)
     for i in range(8):
         smine[i : i + 1, :] = jnp.sum(accs[i], axis=0, keepdims=True)
     c_s = remote(smine, ssib, sib_s.at[4], sib_r.at[4], sib)
     c_s.start()
-    for k in reversed(range(L)):
-        g1.b(k)
+    lsort[...] = (x1_ref[...] + ysum[...]).astype(BF)
+    lo_out[...] = mm(perm[...], lsort[...], ((0,), (0,))).astype(BF)
+    each(gk.c1)
     ig_out[...] = mm(perm[...], tmpb[...], ((0,), (0,))).astype(BF)
     c_s.wait()
     smine[...] = smine[...] + ssib[...]
@@ -1015,38 +1101,35 @@
 
     def s_copy(i):
         to = (me + i) % S
-        return remote(s_at(to), srecv.at[me], sm_s.at[i], sm_r.at[0], (core, to))
+        return remote(s_at(to), srecv.at[me], sm_s.at[0, i], sm_r.at[0], (core, to))
 
     @pl.loop(1, S)
     def _(i):
         s_copy(i).start()
 
     srecv[me] = s_at(me)[...]
-    for k in range(1, L):
-        gy.d(k)
-    lsort[...] = (x1_ref[...] + ysum[...]).astype(BF)
-    lo_out[...] = mm(perm[...], lsort[...], ((0,), (0,))).astype(BF)
-    for k in far:
-        g1.c(k)
-    for k in range(1, L):
-        g0.d(k)
+    each(gq.c1)
+    for g in (g0, gv, gk, gq):
+        for k in range(1, L):
+            g.d(k)
     allr = srecv.at[pl.ds(0, S - 1)]
-    remote(allr, allr, sm_s.at[0], sm_r.at[0], (core, xn)).wait_recv()
+    remote(allr, allr, sm_s.at[0, 0], sm_r.at[0], (core, xn)).wait_recv()
     smalls_out[...] = jnp.sum(srecv[...], axis=0)
-    for k in range(1, L):
-        g1.d(k)
-    gy.finish()
-    g0.finish()
-    g1.finish()
+    for g in (gy, g0, gv, gk, gq):
+        g.finish()
     for c in (c_o, c_v, c_k, c_q):
         c.wait_send()
+
+    got = gup_out.at[pl.ds(0, S - 1)]
+    remote(got, got, sm_s.at[1, 0], sm_r.at[1], (core, xn)).wait_recv()
 
     @pl.loop(1, S)
     def _(i):
         s_copy(i).wait_send()
-
-
-def back_call(dh, y, sc, small, stat, u1, u2, x1, dys, q, k, v, p, o, es, ss, wa, S):
+        g_copy(i).wait_send()
+
+
+def back_call(dh, y, sc, small, stat, u1, u2, x1, dys, q, k, v, p, o, es, ss, wa, gup, S):
     T, D = dh.shape
     WR = D // (2 * S)
     L = S // 4
@@ -1058,31 +1141,84 @@
     row = V((T, D), BF)
 
     def rs_bufs(R):
-        return [V((S, R, D), BF)] + [V((L, R, D), BF)] * 4
+        return [V((S, R, D), BF)] + [V((L, R, D), BF)] * 4 + [V((L // 2, R, D), BF)]
 
     return pl.pallas_call(
         back_kernel,
         out_shape=(
-            sds((T, D), BF), sds((T, D), BF), sds((3 * WR, D), F32), sds((WR, D), F32), sds((8, 128), F32),
+            sds((T, D), BF), sds((T, D), BF), sds((WR, D), F32), sds((WR, D), F32), sds((WR, D), F32),
+            sds((WR, D), F32), sds((8, 128), F32),
+            sds((S, 3, WR, gup.shape[2]), BF),
         ),
-        in_specs=[vm] * 15 + [hb, hb],
-        out_specs=(vm,) * 5,
+        in_specs=[vm] * 15 + [hb, hb, vm],
+        out_specs=(vm,) * 8,
         scratch_shapes=[
             V((4, D, D), BF), V((T, T), BF), V((8, 8, D), F32), V((T, D), F32), row, row, row, row, row, row,
             V((T, D), F32), row, V((4, D // 2, D), F32), V((4, D // 2, D), BF), V((4, D // 2, D), BF),
         ]
         + rs_bufs(WR)
-        + rs_bufs(3 * WR)
+        + rs_bufs(WR)
+        + rs_bufs(WR)
+        + rs_bufs(WR)
         + rs_bufs(T)
         + [
             V((T, D), F32), V((T, D), BF),
             V((8, D), F32), V((8, D), F32), V((S, 8, 128), F32),
-            dma((3, 4, L)), dma((3, 4, L)), dma((5,)), dma((5,)), dma((S,)), dma((1,)), dma((4 + L,)),
+            dma((5, 5, L)), dma((5, 5, L)), dma((5,)), dma((5,)), dma((2, S)), dma((2,)), dma((5 + L,)),
         ],
         compiler_params=pltpu.CompilerParams(collective_id=3, has_side_effects=True, vmem_limit_bytes=60000000),
         cost_estimate=pl.CostEstimate(flops=4 * 10**9, bytes_accessed=20 * 2**20, transcendentals=2**20),
         name="back",
-    )(dh, sc, small, stat, u1, u2, x1, dys, q, k, v, p, o, es, ss, y, wa)
+    )(dh, sc, small, stat, u1, u2, x1, dys, q, k, v, p, o, es, ss, y, wa, gup)
+
+
+def finish_kernel(
+    lo_ref, ig_ref, gq_ref, gk_ref, gv_ref, go_ref, sm_ref, gup_ref, gdn0_ref, gdn12_ref,
+    lo_out, ig_out, q_out, k_out, v_out, o_out, up_out, dn_out, eu_out, ed_out, r_out, m_out, n_out,
+    turned,
+):
+    S, _, WR, F = gup_ref.shape
+    FR = F // 2
+    at = (lax.axis_index("dp") * S + lax.axis_index("shard")) % (128 // WR) * WR
+    lo_out[...] = lo_ref[...]
+    ig_out[...] = ig_ref[...]
+    for src, out in ((gq_ref, q_out), (gk_ref, k_out), (gv_ref, v_out), (go_ref, o_out)):
+        out[...] = src[...]
+    dn_out[...] = gdn0_ref[...]
+    ed_out[...] = gdn12_ref[...]
+    for s in range(S):
+        for c in range(2):
+            cols = slice((c * S + s) * FR, (c * S + s + 1) * FR)
+            part = slice(c * FR, (c + 1) * FR)
+            up_out[:, cols] = gup_ref[s, 0, :, part].astype(F32)
+            for e in range(2):
+                eu_out[e, :, cols] = gup_ref[s, 1 + e, :, part].astype(F32)
+    turned[...] = jnp.concatenate([sm_ref[...], jnp.zeros((120, 128), F32)], axis=0).T
+    mine = turned[pl.ds(pl.multiple_of(at, WR), WR), :]
+    r_out[...] = mine[:, 4:6]
+    m_out[...] = mine[:, 6:8]
+    n_out[...] = mine[:, 0:4]
+
+
+def finish_call(lo, ig, gwq, gwk, gwv, gwo, smalls, gup, gdn0, gdn12):
+    T, D = lo.shape
+    S, _, WR, F = gup.shape
+    FF = S * F
+    vm = pl.BlockSpec(memory_space=pltpu.VMEM)
+    sds = jax.ShapeDtypeStruct
+    sq = sds((WR, D), F32)
+    return pl.pallas_call(
+        finish_kernel,
+        out_shape=(
+            sds((T, D), BF), sds((T, D), BF), sq, sq, sq, sq, sds((WR, FF), F32), sds(gdn0.shape, F32),
+            sds((2, WR, FF), F32), sds(gdn12.shape, F32), sds((WR, 2), F32), sds((WR, 2), F32), sds((WR, 4), F32),
+        ),
+        in_specs=[vm] * 10,
+        out_specs=(vm,) * 13,
+        scratch_shapes=[pltpu.VMEM((128, 128), F32)],
+        compiler_params=pltpu.CompilerParams(vmem_limit_bytes=40000000),
+        name="finish",
+    )(lo, ig, gwq, gwk, gwv, gwo, smalls, gup, gdn0, gdn12)
 
 
 def body_plain(
@@ -1269,26 +1405,26 @@
         hidden_in, out_grad, doc_ids, expert_ids.reshape(1, T), slot_ids.reshape(1, T), small,
         (w_query, w_key, w_value, w_out), w_up, expert_up, w_down, expert_down, S,
     )
-    y_parts, dh2, sc, gup, gdn0, gdn12 = ffn_call(h2b, scal8, dy_all, ups, downs)
-    layer_out, input_grad, gqkv, gwo, smalls = back_call(
+    y_parts, dh2, sc, gup, gdn0, gdn12 = ffn_call(h2b, scal8, dy_all, ups, w_down, expert_down, downs)
+    layer_out, input_grad, gwq, gwk, gwv, gwo, smalls, gup = back_call(
         dh2, y_parts, sc, small, stat, u1, u2, x1, dys, q, k, v, p, o,
-        expert_ids.reshape(1, T), slot_ids.reshape(1, T), wa.reshape(4, D, D), S,
+        expert_ids.reshape(1, T), slot_ids.reshape(1, T), wa.reshape(4, D, D), gup, S,
     )
-    mine = lax.dynamic_slice_in_dim(smalls, dev % group * WR, WR, 1)
-    ga = gqkv.reshape(3, WR, D)
-    gup = gup.astype(F32).reshape(S, 3, WR, C, FR).transpose(1, 2, 3, 0, 4).reshape(3, WR, FF)
+    lo, ig, gq, gk, gv, go, gu, gd, geu, ged, gr, gm, gn = finish_call(
+        layer_out, input_grad, gwq, gwk, gwv, gwo, smalls, gup, gdn0, gdn12
+    )
     tokens0 = count[0, 0].astype(jnp.int32)
     counts = jnp.stack([tokens0, T * ndev - tokens0])
     load_new = 0.9 * load_avg + 0.1 * counts.astype(F32) * E / (T * ndev)
     return (
-        layer_out, input_grad, mine[0], mine[1], ga[0], ga[1], ga[2], gwo, mine[2], mine[3],
-        gup[0], gdn0, mine[4:6].T, mine[6:8].T, gup[1:], gdn12, counts, load_new,
+        lo, ig, gn[:, 0], gn[:, 1], gq, gk, gv, go, gn[:, 2], gn[:, 3],
+        gu, gd, gr, gm, geu, ged, counts, load_new,
     )
 
 
 def pick(*args):
     S, C, WR, FR = lax.axis_size("shard"), lax.axis_size("dp"), args[7].shape[0], args[14].shape[0]
-    fast = C == 2 and S % 4 == 0 and S >= 8 and WR % 16 == 0 and 128 % WR == 0 and FR % 128 == 0
+    fast = C == 2 and S // 4 == 4 and S % 4 == 0 and WR % 16 == 0 and 128 % WR == 0 and FR % 128 == 0
     return (body if fast else body_plain)(*args)
 
 

time: 334 us -> 313 us (0.937)
  Pallas kernels: 316 us -> 298 us
    pallas_call x1, Pallas kernels: 109 us -> 98.2 us  [attn_call(): pl.pallas_call(attn_kernel, out_shape=(row, sds((T, 128), F32), sds((8, T...]
    pallas_call x1, Pallas kernels: 120 us -> 111 us  [ffn_call(): pl.pallas_call(ffn_kernel, out_shape=(sds((S, T, D), BF), sds((T, D), F32...]
    unnamed x17 -> x24, local copies, waits for them, and re-layouts: 4.82 us -> 8.59 us
where the time goes in v6:
time: 313 us
  Pallas kernels  298 us (95%)
  local copies, waits for them, and re-layouts  12.1 us (4%)
    pallas_call x1, Pallas kernels, ffn_call(): pl.pallas_call(ffn_kernel, out_shape=(sds((S, T, D), BF), sds((T, D), F32...  111 us
    pallas_call x1, Pallas kernels, attn_call(): pl.pallas_call(attn_kernel, out_shape=(row, sds((T, 128), F32), sds((8, T...  98.2 us
    pallas_call x1, Pallas kernels, back_call(): pl.pallas_call(back_kernel, out_shape=(sds((T, D), BF), sds((T, D), BF),...  86.1 us
    unnamed x24, local copies, waits for them, and re-layouts  8.59 us

profile of v6, /device:TPU:0, one launch (start us, length us, event | category | flops | bytes accessed | tf_op | source)
XLA Modules:
  0.0 312.5 jit_solution(825349291796845195)
XLA Ops:
  0.7 0.0 copy-start.10
  0.7 0.7 slice_bitcast_fusion
  1.4 0.7 stack.40
  2.2 0.1 tile.10
  2.3 0.6 fusion.small_ref
  2.9 98.2 %attn.1 = (bf16[128,1024]{1,0:T(8,128)(2,1)}, f32[128,128]{1,0:T(8,128)}, f32[8,128]{1,0:T(8,128)}, f32[128,1024]{1,0:T(8,128)}, f32[128,1024]{1,0:T(8,128)}, /*...) custom-call(bf16[128,1024]{1,0:T(8,128)(2,1)} %x_ref.1, ...), custom_call_target="tpu_custom_call" | custom-call | flops 2000000000 | bytes 41943040 | tf_op jit(solution)/shard_map/attn/pallas_call | solution.py:879
  101.1 1.2 slice.35
  102.9 0.0 copy-done.10
  102.9 0.6 multiply_add_fusion
  103.5 111.4 %ffn.1 = (bf16[16,128,1024]{2,1,0:T(8,128)(2,1)}, f32[128,1024]{1,0:T(8,128)}, f32[8,128]{1,0:T(8,128)}, bf16[3,512,256]{2,1,0:T(8,128)(2,1)}, f32[128,1024]{1,0:T(8,128)}, /*index=5*/f32[2,128,1024]{2,1,0:T(8,128)}) custom-call(bf16[128,1024]{1,0:T(8,128)(2,1)} %get-tuple-element.63.h_ref, f32[8,128]{1,0:T(8,128)} %get-tuple-element.64.scal_ref, ...), custom_call_target="tpu_custom_call" | custom-call | flops 15000000512 | bytes 20971520 | tf_op jit(solution)/shard_map/ffn/pallas_call | solution.py:581
  214.9 0.0 copy-start
  215.0 86.1 %back.1 = (bf16[128,1024]{1,0:T(8,128)(2,1)}, bf16[128,1024]{1,0:T(8,128)(2,1)}, f32[32,1024]{1,0:T(8,128)}, f32[32,1024]{1,0:T(8,128)}, f32[32,1024]{1,0:T(8,12...) custom-call(f32[128,1024]{1,0:T(8,128)} %get-tuple-element.68.dh_ref, ...), custom_call_target="tpu_custom_call" | custom-call | flops 4000000000 | bytes 20971520 | tf_op jit(solution)/shard_map/back/pallas_call | solution.py:1146
  301.1 1.1 copy-done.1
  302.2 0.9 copy-done.3
  303.2 0.9 copy-done.4
  304.1 0.9 copy-done.5
  305.0 0.9 copy-done.6
  305.9 0.9 copy-done.7
  306.8 0.9 copy-done.8
  307.7 0.7 copy-done.9
  308.4 2.1 finish.1
  310.5 0.6 copy.40
  311.1 0.6 copy.41
  311.8 0.7 slice_reduce_fusion
  (14 shorter events, 0.0 us)
Async XLA Ops:
  0.7 102.3 %copy-start.10 = (f32[2]{0:T(128)S(1)}, f32[2]{0:T(128)}, u32[]{:S(2)}) copy-start(f32[2]{0:T(128)} %param.39) | copy-start | bytes 28
  214.9 86.1 %copy-start = (f32[2,128,1024]{2,1,0:T(8,128)S(1)}, f32[2,128,1024]{2,1,0:T(8,128)}, u32[]{:S(2)}) copy-start(f32[2,128,1024]{2,1,0:T(8,128)} %get-tuple-element.93.gdn12_ref) | copy-start | bytes 3145732
  215.0 86.1 %copy-start.2 = (f32[128,1024]{1,0:T(8,128)S(1)}, f32[128,1024]{1,0:T(8,128)}, u32[]{:S(2)}) copy-start(f32[128,1024]{1,0:T(8,128)} %get-tuple-element.92.gdn0_ref) | copy-start | bytes 1572868
  301.1 1.1 copy-start.1
  302.2 0.9 copy-start.3
  303.2 0.9 copy-start.4
  304.1 0.9 copy-start.5
  305.0 0.9 copy-start.6
  305.9 0.9 copy-start.7
  306.8 0.9 copy-start.8
  307.7 0.7 copy-start.9

commit v7 on v6

--- a/solution.py
+++ b/solution.py
@@ -176,33 +176,31 @@
                 copy(5, lev, own, lev * 4 + dq, pair).wait_recv()
 
         @staticmethod
+        def done(k):
+            lev = lev_of(k)
+            for kind in range(1, 3):
+                copy(kind, lev, own, me, xn).wait_send()
+
+            @pl.when((lev + z) % 2 == 0)
+            def _():
+                for kind in (3, 5):
+                    copy(kind, lev, own, me, xn).wait_send()
+
+            @pl.when(k > 0)
+            def _():
+                ok, on = onward(k)
+                pl.when(ok)(on.wait_send)
+
+            @pl.when(k == 0)
+            def _():
+                pl.when(z < L - 1)(lambda: up_line(own, ss.at[0, z]).wait_send())
+                pl.when(z > 0)(lambda: down_line(own, ss.at[4, 0]).wait_send())
+
+        @staticmethod
         def finish():
-            @pl.when(z < L - 1)
-            def _():
-                up_line(own, ss.at[0, z]).wait_send()
-
-            @pl.when(z > 0)
-            def _():
-                down_line(own, ss.at[4, 0]).wait_send()
-
             @pl.loop(0, L)
             def _(k):
-                lev = lev_of(k)
-                for kind in range(1, 3):
-                    copy(kind, lev, own, me, xn).wait_send()
-
-                @pl.when((lev + z) % 2 == 0)
-                def _():
-                    for kind in (3, 5):
-                        copy(kind, lev, own, me, xn).wait_send()
-
-            @pl.loop(1, L)
-            def _(k):
-                ok, on = onward(k)
-
-                @pl.when(ok)
-                def _():
-                    on.wait_send()
+                Stages.done(k)
 
     return Stages
 
@@ -344,263 +342,6 @@
     return Stages
 
 
-def ffn_kernel(
-    h_ref, scal_ref, dy_hbm, up_hbm, wd_hbm, ed_hbm, dn_hbm,
-    y_out, dh_out, sc_out, gup_out, gdn0_out, gdn12_out,
-    dy_ref, up_ref, dn_ref, ypart, hall, scall, psc, screcv, wcol, scol, part, ra, rbx, rby, rd,
-    pre, der, ub, dg, dm, m, yacc, dxacc, gdn, gup, sib_dn, sib_up,
-    ag_s, ag_r, rs_s, rs_r, one_s, one_r, sm_s, sm_r, loc, yloc,
-):
-    S, T, D = hall.shape
-    F = up_hbm.shape[2]
-    L = S // 4
-    LO = 80
-    HI = T - LO
-    me, core, z, p, xq, yq, dq = place_of()
-    xn = z * 4 + xq
-    lev_of = level_order(z, L)
-    dev, levels = (core, z, p, xq, yq, dq), (lev_of, L)
-    greet(S, core)
-    hg = tree_gather(lambda i: hall.at[i], h_ref, ag_s, ag_r, dev, levels)
-    rgs = []
-    for i in range(2):
-        t = pl.ds(i * (T // 2), T // 2)
-        bufs = [b.at[:, t, :] for b in (part, ra, rbx, rby, rd)]
-        rgs.append(tree_scatter(*bufs, dh_out.at[t], rs_s.at[i], rs_r.at[i], dev, levels))
-    hg.start()
-    half_f = F // 2
-    mine_f = pl.ds(pl.multiple_of(core * half_f, half_f), half_f)
-    other_f = pl.ds(pl.multiple_of((1 - core) * half_f, half_f), half_f)
-    pairs = (
-        (up_hbm, up_ref),
-        (wd_hbm, dn_ref.at[0, mine_f]),
-        (ed_hbm, dn_ref.at[pl.ds(1, 2), mine_f]),
-        (dn_hbm, dn_ref.at[:, other_f]),
-        (dy_hbm, dy_ref),
-    )
-    loads = [pltpu.make_async_copy(a, b, loc.at[i]) for i, (a, b) in enumerate(pairs)]
-    for c in loads:
-        c.start()
-
-    @pl.loop(1, S)
-    def _(i):
-        remote(scal_ref, scall.at[me], sm_s.at[0, i], sm_r.at[0], (core, (me + i) % S)).start()
-
-    hall[me] = h_ref[...]
-    scall[me] = scal_ref[...]
-    gdn[...] = jnp.zeros_like(gdn)
-    gup[...] = jnp.zeros_like(gup)
-    remote(scall.at[pl.ds(0, S - 1)], scall.at[pl.ds(0, S - 1)], sm_s.at[0, 0], sm_r.at[0], (core, xn)).wait_recv()
-
-    size = (4 * T, 4 * LO, 4 * LO)
-    first = (0, 4 * T, 4 * T + 4 * LO)
-
-    def compute(lev, between):
-        base = lev * 4
-        for q in range(4):
-            full = jnp.concatenate([scall[base + q], jnp.zeros((120, 128), F32)], axis=0)
-            wcol[q] = full.T
-        for e in range(3):
-            n = LO if e else T
-            off = HI if e == 2 else 0
-            rows, at0 = size[e], first[e]
-            here = slice(at0, at0 + rows)
-            hm = hall[pl.ds(base, 4), off : off + n, :].reshape(rows, D)
-            pre[0:rows, :] = mm(hm, up_ref[e])
-
-            def act(r):
-                t = pl.ds(r, rows // 4)
-                val, d = gelu_pair(pre[t, :])
-                ub[pl.ds(pl.multiple_of(at0 + r, 16), rows // 4), :] = val.astype(BF)
-                der[t, :] = d
-
-            rows_loop(rows, rows // 4, act)
-            m[0:rows, :] = mm(ub[here, :], dn_ref[e])
-            step = n if e else T // 2
-            lane = lax.broadcasted_iota(jnp.int32, (step, 128), 1)
-            for q in range(4):
-
-                def elem(r):
-                    at = pl.ds(pl.multiple_of(r + off, 16), step)
-                    mine = pl.ds(pl.multiple_of(q * n + r, 16), step)
-                    keep = pl.ds(pl.multiple_of(at0 + q * n + r, 16), step)
-                    t = pl.ds(pl.multiple_of(q * T + off + r, 16), step)
-                    w = wcol[q, at, :][:, e : e + 1]
-                    dyv = dy_ref[base + q, at, :].astype(F32)
-                    mv = m[mine, :]
-                    s = jnp.sum(dyv * mv, axis=1, keepdims=True)
-                    s = jnp.where(lane == e, s, 0.0)
-                    dm[keep, :] = (dyv * w).astype(BF)
-                    if e:
-                        yacc[t, :] = yacc[t, :] + mv * w
-                        scol[q, at, :] = scol[q, at, :] + s
-                    else:
-                        yacc[t, :] = mv * w
-                        scol[q, at, :] = s
-
-                rows_loop(n, step, elem)
-            pre[0:rows, :] = mm(dm[here, :], dn_ref[e], ((1,), (1,)))
-
-            def back(r):
-                t = pl.ds(r, rows // 4)
-                dg[pl.ds(pl.multiple_of(at0 + r, 16), rows // 4), :] = (pre[t, :] * der[t, :]).astype(BF)
-
-            rows_loop(rows, rows // 4, back)
-            if e:
-                m[0:rows, :] = mm(dg[here, :], up_ref[e], ((1,), (1,)))
-                for q in range(4):
-                    t = slice(q * T + off, q * T + off + n)
-                    dxacc[t, :] = dxacc[t, :] + m[q * n : q * n + n, :]
-            else:
-                dxacc[...] = mm(dg[here, :], up_ref[0], ((1,), (1,)))
-            between(e)
-        for q in range(4):
-            psc[base + q] = scol[q].T[0:8, :]
-            t = slice(q * T, q * T + T)
-            part[base + q] = dxacc[t, :].astype(BF)
-            ypart[base + q] = yacc[t, :].astype(BF)
-        some = pl.ds(base, 4)
-        pltpu.make_async_copy(ypart.at[some], y_out.at[some], yloc.at[lev]).start()
-
-    def weight_grads(lev):
-        for e in range(3):
-            n = LO if e else T
-            off = HI if e == 2 else 0
-            here = slice(first[e], first[e] + size[e])
-            hm = hall[pl.ds(lev * 4, 4), off : off + n, :].reshape(size[e], D)
-            gdn[e] = gdn[e] + mm(ub[here, :], dm[here, :], ((0,), (0,)))
-            gup[e] = gup[e] + mm(dg[here, :], hm, ((0,), (0,)))
-
-    end = (z == 0) | (z == L - 1)
-    hg.a(1)
-    hg.b(0)
-    hg.a(2)
-    pl.when(jnp.logical_not(end))(lambda: hg.a(3))
-    hg.c(0)
-    for c in loads:
-        c.wait()
-
-    def far_a(i):
-        pl.when(end)(lambda: hg.a(i))
-
-    @pl.loop(0, L)
-    def _(k):
-        @pl.when(k > 0)
-        def _():
-            hg.d(k)
-
-        def between(e):
-            @pl.when(k == 0)
-            def _():
-                for call, i in (((far_a, 3), (hg.b, 1)), ((hg.c, 1), (hg.b, 2)), ())[e]:
-                    call(i)
-
-            @pl.when(k == 1)
-            def _():
-                for call, i in (((hg.c, 2), (hg.b, 3)), ((hg.c, 3),), ())[e]:
-                    call(i)
-
-            if e == 1:
-
-                @pl.when(k > 0)
-                def _():
-                    for g in rgs:
-                        g.b(k - 1)
-
-        compute(lev_of(k), between)
-        for g in rgs:
-            g.a(k)
-
-        @pl.when(k > 0)
-        def _():
-            for g in rgs:
-                g.c(k - 1)
-
-        weight_grads(lev_of(k))
-
-    half = D // 2
-    other = pl.multiple_of((1 - core) * half, half)
-    mine_d = pl.multiple_of(core * half, half)
-    sib = (1 - core, me)
-    c_up = remote(gup.at[:, :, pl.ds(other, half)], sib_up, one_s.at[0], one_r.at[0], sib)
-    c_dn = remote(gdn.at[:, other_f, :], sib_dn, one_s.at[1], one_r.at[1], sib)
-    c_up.start()
-    c_dn.start()
-
-    @pl.loop(1, S)
-    def _(i):
-        to = (me + i) % S
-        remote(psc.at[to], screcv.at[i], sm_s.at[1, i], sm_r.at[1], (core, to)).start()
-
-    for g in rgs:
-        g.b(L - 1)
-    c_up.wait_recv()
-    for e in range(3):
-        tot = gup[e, :, pl.ds(mine_d, half)] + sib_up[e]
-        gup_out[e] = tot.T.astype(BF)
-        if e == 0:
-            for g in rgs:
-                g.c(L - 1)
-    screcv[0] = psc[me]
-    c_dn.wait_recv()
-    gdn0_out[...] = gdn[0, mine_f, :] + sib_dn[0]
-    for e in range(1, 3):
-        gdn12_out[e - 1] = gdn[e, mine_f, :] + sib_dn[e]
-    for k in range(1, L):
-        for g in rgs:
-            g.d(k)
-    remote(screcv.at[pl.ds(1, S - 1)], screcv.at[pl.ds(1, S - 1)], sm_s.at[1, 0], sm_r.at[1], (core, xn)).wait_recv()
-    sc_out[...] = jnp.sum(screcv[...], axis=0)
-
-    for i in range(L):
-        some = pl.ds(i * 4, 4)
-        pltpu.make_async_copy(ypart.at[some], y_out.at[some], yloc.at[i]).wait()
-    c_up.wait_send()
-    c_dn.wait_send()
-    hg.finish()
-    for g in rgs:
-        g.finish()
-
-    @pl.loop(1, S)
-    def _(i):
-        remote(scal_ref, scall.at[0], sm_s.at[0, i], sm_r.at[0], (core, xn)).wait_send()
-        remote(psc.at[0], screcv.at[0], sm_s.at[1, i], sm_r.at[1], (core, xn)).wait_send()
-
-
-def ffn_call(h2b, scal, dy_all, ups, wd, ed, downs):
-    S, T, D = dy_all.shape
-    F = ups.shape[2]
-    L = S // 4
-    rows = 4 * T + 8 * 80
-    vm = pl.BlockSpec(memory_space=pltpu.VMEM)
-    hb = pl.BlockSpec(memory_space=pl.ANY)
-    V = pltpu.VMEM
-    dma = pltpu.SemaphoreType.DMA
-    sds = jax.ShapeDtypeStruct
-    blocks = V((L, T, D), BF)
-    return pl.pallas_call(
-        ffn_kernel,
-        out_shape=(
-            sds((S, T, D), BF), sds((T, D), F32), sds((8, 128), F32), sds((3, D // 2, F), BF),
-            sds((F // 2, D), F32), sds((2, F // 2, D), F32),
-        ),
-        in_specs=[vm] * 2 + [hb] * 5,
-        out_specs=(hb,) + (vm,) * 5,
-        scratch_shapes=[
-            V((S, T, D), BF), V((3, D, F), BF), V((3, F, D), BF), V((S, T, D), BF), V((S, T, D), BF), V((S, 8, 128), F32), V((S, 8, 128), F32), V((S, 8, 128), F32),
-            V((4, T, 128), F32), V((4, T, 128), F32),
-            V((S, T, D), BF), blocks, blocks, blocks, blocks,
-            V((4 * T, F), F32), V((4 * T, F), F32), V((rows, F), BF), V((rows, F), BF), V((rows, D), BF),
-            V((4 * T, D), F32), V((4 * T, D), F32), V((4 * T, D), F32),
-            V((3, F, D), F32), V((3, F, D), F32), V((3, F // 2, D), F32), V((3, F, D // 2), F32),
-            dma((6, L)), dma((6, L)), dma((2, 4, L)), dma((2, 4, L)), dma((2,)), dma((2,)), dma((2, S)), dma((2,)), dma((5,)), dma((L,)),
-        ],
-        compiler_params=pltpu.CompilerParams(collective_id=2, has_side_effects=True, vmem_limit_bytes=64000000),
-        cost_estimate=pl.CostEstimate(flops=15 * 10**9, bytes_accessed=20 * 2**20, transcendentals=2**20),
-        name="ffn",
-    )(h2b, scal, dy_all, ups, wd, ed, downs)
-
-
 def sort_matrix(ids_e, ids_s, T):
     zero = ids_e == 0
     n0 = jnp.sum(jnp.where(zero, 1.0, 0.0), axis=1, keepdims=True)
@@ -610,13 +351,14 @@
     return jnp.where(sub == pos, 1.0, 0.0), n0
 
 
-def attn_kernel(
-    x_ref, dy_ref, doc_ref, e_ref, s_ref, small_ref, wq_ref, wk_ref, wv_ref, wo_ref,
+def front_kernel(
+    x_ref, dyin_ref, doc_ref, e_ref, s_ref, small_ref, wq_ref, wk_ref, wv_ref, wo_ref,
     wu_ref, eu_ref, wd_ref, ed_ref,
-    h2b_out, stat_out, scal_out, u1_out, u2_out, x1_out, dys_out, q_out, k_out, v_out, p_out, o_out,
-    small_out, count_out, w_out, dyall_out, up_out, dn_out,
-    wbuf, upb, smallbuf, h1b, bias, xs, tmp,
-    ag_s, ag_r, sib_s, sib_r, sm_s, sm_r, loc,
+    stat_out, u1_out, u2_out, x1_out, dys_out, q_out, k_out, v_out, p_out, o_out,
+    small_out, count_out, w_out, y_out, dh_out, sc_out, gup_out, gdn0_out, gdn12_out,
+    wbuf, up_ref, dn_ref, smallbuf, bias, dy_all, hall, scall, psc, screcv, wcol, scol, ra, rbx, rby, rd,
+    pre, der, ub, dg, dm, m, yacc, dxacc, gdn, gup, sib_dn, sib_up,
+    ag_s, ag_r, rs_s, rs_r, sib_s, sib_r, one_s, one_r, sm_s, sm_r, sn_s, sn_r, loc,
 ):
     T, D = x_ref.shape
     WR = wq_ref.shape[0]
@@ -637,7 +379,9 @@
         return wbuf.at[:, core * S + i]
 
     wg = tree_gather(w_at, w_at(me), ag_s.at[0], ag_r.at[0], dev, levels)
-    dyg = tree_gather(lambda i: dyall_out.at[i], dys_out, ag_s.at[2], ag_r.at[2], dev, levels)
+    dyg = tree_gather(lambda i: dy_all.at[i], dys_out, ag_s.at[1], ag_r.at[1], dev, levels)
+    hg = tree_gather(lambda i: hall.at[i], hall.at[me], ag_s.at[2], ag_r.at[2], dev, levels)
+    tmp, xs, h1b = m.at[pl.ds(0, T)], yacc.at[pl.ds(0, T)], dm.at[pl.ds(0, T)]
 
     for i, w in enumerate((wq_ref, wk_ref, wv_ref, wo_ref)):
         wbuf[i, my] = w[...]
@@ -652,17 +396,24 @@
     def _(i):
         remote(smallbuf.at[my], smallbuf.at[my], sm_s.at[0, i], sm_r.at[0], (core, (me + i) % S)).start()
 
+    F = 2 * FR
+    mine_f = pl.ds(pl.multiple_of(core * FR, FR), FR)
+    other_f = pl.ds(pl.multiple_of((1 - core) * FR, FR), FR)
     dn_copies = (
-        remote(wd_ref, dn_out.at[0], sib_s.at[2, 0], sib_r.at[2, 0], sib),
-        remote(ed_ref, dn_out.at[pl.ds(1, 2)], sib_s.at[2, 1], sib_r.at[2, 1], sib),
+        remote(wd_ref, dn_ref.at[0, mine_f], sib_s.at[1, 0], sib_r.at[1, 0], sib),
+        remote(ed_ref, dn_ref.at[pl.ds(1, 2), mine_f], sib_s.at[1, 1], sib_r.at[1, 1], sib),
     )
     for c in dn_copies:
         c.start()
+    dn_ref[0, mine_f, :] = wd_ref[...]
+    for e in range(2):
+        dn_ref[1 + e, mine_f, :] = ed_ref[e]
     permb = perm.astype(BF)
     xs[...] = mm(permb, x_ref[...])
-    dys_out[...] = mm(permb, dy_ref[...]).astype(BF)
-    dy_local = pltpu.make_async_copy(dys_out, dyall_out.at[me], loc.at[2])
-    dy_local.start()
+    dys_out[...] = mm(permb, dyin_ref[...]).astype(BF)
+    dy_all[me] = dys_out[...]
+    gdn[...] = jnp.zeros_like(gdn)
+    gup[...] = jnp.zeros_like(gup)
 
     docs = (doc_ref[...] == lax.broadcasted_iota(jnp.int32, (16, T), 0)).astype(F32).astype(BF)
     docs = mm(docs, permb, ((1,), (1,))).astype(BF)
@@ -694,7 +445,7 @@
     group = 128 // WR
     remote(smallbuf.at[pl.ds(0, S - 1)], smallbuf.at[pl.ds(0, S - 1)], sm_s.at[0, 0], sm_r.at[0], (core, xn)).wait_recv()
     mine_small = smallbuf.at[pl.ds(core * S, S)]
-    c_small = remote(mine_small, mine_small, sib_s.at[2, 2], sib_r.at[2, 2], sib)
+    c_small = remote(mine_small, mine_small, sib_s.at[1, 2], sib_r.at[1, 2], sib)
     c_small.start()
 
     def up_copy(e, h, i):
@@ -702,7 +453,7 @@
         src = wu_ref if e == 0 else eu_ref.at[e - 1]
         return remote(
             src.at[:, pl.ds(pl.multiple_of((h * S + to) * FR, FR), FR)],
-            upb.at[e, pl.ds(pl.multiple_of(my * WR, WR), WR), pl.ds(h * FR, FR)],
+            up_ref.at[e, pl.ds(pl.multiple_of(my * WR, WR), WR), pl.ds(h * FR, FR)],
             sm_s.at[1, i], sm_r.at[1], (core, to),
         )
 
@@ -716,7 +467,7 @@
         for h in range(2):
             src = wu_ref if e == 0 else eu_ref.at[e - 1]
             block = src[:, pl.ds(pl.multiple_of((h * S + me) * FR, FR), FR)]
-            upb[e, pl.ds(pl.multiple_of(my * WR, WR), WR), h * FR : (h + 1) * FR] = block
+            up_ref[e, pl.ds(pl.multiple_of(my * WR, WR), WR), h * FR : (h + 1) * FR] = block
 
     def w_sib(lev, who):
         b = wbuf.at[:, pl.ds(who * S + lev * 4, 4)]
@@ -758,7 +509,7 @@
     dyg.b(1)
     for k in range(L):
         w_sib(lev_of(k), 1 - core).wait_recv()
-    w_save = pltpu.make_async_copy(wbuf, w_out, loc.at[3])
+    w_save = pltpu.make_async_copy(wbuf, w_out, loc.at[L])
     w_save.start()
 
     def full(i):
@@ -807,7 +558,7 @@
         u = cen * inv
         u2_out[t, :] = u
         h2 = u * small_out[2:3, :] + small_out[3:4, :]
-        h2b_out[t, :] = h2.astype(BF)
+        hall[me, t, :] = h2.astype(BF)
         lg = [jnp.sum(h2 * small_out[i : i + 1, :], axis=1, keepdims=True) for i in range(4, 8)]
 
         def soft(a, b):
@@ -829,46 +580,227 @@
 
     dyg.c(2)
     rows_loop(T, 64, norm2)
-    scal_out[...] = stat_out[...].T[0:8, :]
+    scall[me] = stat_out[...].T[0:8, :]
+    hg.start()
+
+    @pl.loop(1, S)
+    def _(i):
+        remote(scall.at[me], scall.at[me], sn_s.at[0, i], sn_r.at[0], (core, (me + i) % S)).start()
 
     dyg.c(3)
-    for k in range(L):
-        dyg.d(k)
-
-    got = upb.at[:, pl.ds(0, (S - 1) * WR), :]
+    got = up_ref.at[:, pl.ds(0, (S - 1) * WR), :]
     remote(got, got, sm_s.at[1, 0], sm_r.at[1], (core, xn)).wait_recv()
-    mine_up = upb.at[:, pl.ds(pl.multiple_of(core * S * WR, S * WR), S * WR), :]
-    c_up = remote(mine_up, mine_up, sib_s.at[2, 3], sib_r.at[2, 3], sib)
-    c_up.start()
-    c_up.wait()
-    up_save = pltpu.make_async_copy(upb, up_out, loc.at[0])
-    up_save.start()
+    mine_up = up_ref.at[:, pl.ds(pl.multiple_of(core * S * WR, S * WR), S * WR), :]
+    c_slice = remote(mine_up, mine_up, sib_s.at[1, 3], sib_r.at[1, 3], sib)
+    c_slice.start()
+    end = (z == 0) | (z == L - 1)
+    hg.a(1)
+    hg.b(0)
+    hg.a(2)
+    pl.when(jnp.logical_not(end))(lambda: hg.a(3))
+
     w_save.wait()
-    up_save.wait()
-    dy_local.wait()
+    wg.finish()
+
+    @pl.loop(0, L)
+    def _(k):
+        w_sib(k, core).wait_send()
+
+    remote(scall.at[pl.ds(0, S - 1)], scall.at[pl.ds(0, S - 1)], sn_s.at[0, 0], sn_r.at[0], (core, xn)).wait_recv()
+    c_slice.wait()
     for c in dn_copies:
         c.wait()
     c_small.wait_send()
-    wg.finish()
-    dyg.finish()
+    hg.c(0)
+    rgs = []
+    for i in range(2):
+        t = pl.ds(i * (T // 2), T // 2)
+        bufs = [b.at[:, t, :] for b in (dy_all, ra, rbx, rby, rd)]
+        rgs.append(tree_scatter(*bufs, dh_out.at[t], rs_s.at[i], rs_r.at[i], dev, levels))
+    LO = 80
+    HI = T - LO
+    per = T // WR
+    fold = N // (4 * per)
+
+    size = (4 * T, 4 * LO, 4 * LO)
+    first = (0, 4 * T, 4 * T + 4 * LO)
+
+    def y_copy(lev):
+        src = wbuf.at[lev // fold, pl.ds(lev % fold * (4 * per), 4 * per)]
+        return pltpu.make_async_copy(src, y_out.at[pl.ds(lev * (4 * per), 4 * per)], loc.at[lev])
+
+    def compute(lev, between, settle):
+        base = lev * 4
+        for q in range(4):
+            full = jnp.concatenate([scall[base + q], jnp.zeros((120, 128), F32)], axis=0)
+            wcol[q] = full.T
+        for e in range(3):
+            n = LO if e else T
+            off = HI if e == 2 else 0
+            rows, at0 = size[e], first[e]
+            here = slice(at0, at0 + rows)
+            hm = hall[pl.ds(base, 4), off : off + n, :].reshape(rows, D)
+            pre[0:rows, :] = mm(hm, up_ref[e])
+
+            def act(r):
+                t = pl.ds(r, rows // 4)
+                val, d = gelu_pair(pre[t, :])
+                ub[pl.ds(pl.multiple_of(at0 + r, 16), rows // 4), :] = val.astype(BF)
+                der[t, :] = d
+
+            rows_loop(rows, rows // 4, act)
+            m[0:rows, :] = mm(ub[here, :], dn_ref[e])
+            step = n if e else T // 2
+            lane = lax.broadcasted_iota(jnp.int32, (step, 128), 1)
+            for q in range(4):
+
+                def elem(r):
+                    at = pl.ds(pl.multiple_of(r + off, 16), step)
+                    mine = pl.ds(pl.multiple_of(q * n + r, 16), step)
+                    keep = pl.ds(pl.multiple_of(at0 + q * n + r, 16), step)
+                    t = pl.ds(pl.multiple_of(q * T + off + r, 16), step)
+                    w = wcol[q, at, :][:, e : e + 1]
+                    dyv = dy_all[base + q, at, :].astype(F32)
+                    mv = m[mine, :]
+                    s = jnp.sum(dyv * mv, axis=1, keepdims=True)
+                    s = jnp.where(lane == e, s, 0.0)
+                    dm[keep, :] = (dyv * w).astype(BF)
+                    if e:
+                        yacc[t, :] = yacc[t, :] + mv * w
+                        scol[q, at, :] = scol[q, at, :] + s
+                    else:
+                        yacc[t, :] = mv * w
+                        scol[q, at, :] = s
+
+                rows_loop(n, step, elem)
+            pre[0:rows, :] = mm(dm[here, :], dn_ref[e], ((1,), (1,)))
+
+            def back(r):
+                t = pl.ds(r, rows // 4)
+                dg[pl.ds(pl.multiple_of(at0 + r, 16), rows // 4), :] = (pre[t, :] * der[t, :]).astype(BF)
+
+            rows_loop(rows, rows // 4, back)
+            if e:
+                m[0:rows, :] = mm(dg[here, :], up_ref[e], ((1,), (1,)))
+                for q in range(4):
+                    t = slice(q * T + off, q * T + off + n)
+                    dxacc[t, :] = dxacc[t, :] + m[q * n : q * n + n, :]
+            else:
+                dxacc[...] = mm(dg[here, :], up_ref[0], ((1,), (1,)))
+            between(e)
+        settle()
+        for q in range(4):
+            psc[base + q] = scol[q].T[0:8, :]
+            t = slice(q * T, q * T + T)
+            dy_all[base + q] = dxacc[t, :].astype(BF)
+            here = pl.ds(lev % fold * (4 * per) + q * per, per)
+            wbuf[lev // fold, here] = yacc[t, :].astype(BF).reshape(per, WR, D)
+        y_copy(lev).start()
+
+    def weight_grads(lev):
+        for e in range(3):
+            n = LO if e else T
+            off = HI if e == 2 else 0
+            here = slice(first[e], first[e] + size[e])
+            hm = hall[pl.ds(lev * 4, 4), off : off + n, :].reshape(size[e], D)
+            gdn[e] = gdn[e] + mm(ub[here, :], dm[here, :], ((0,), (0,)))
+            gup[e] = gup[e] + mm(dg[here, :], hm, ((0,), (0,)))
+
+    def far_a(i):
+        pl.when(end)(lambda: hg.a(i))
 
     @pl.loop(0, L)
     def _(k):
-        w_sib(k, core).wait_send()
+        @pl.when(k > 0)
+        def _():
+            hg.d(k)
+            dyg.d(k)
+
+        def between(e):
+            @pl.when(k == 0)
+            def _():
+                for call, i in (((far_a, 3), (hg.b, 1)), ((hg.c, 1), (hg.b, 2)), ())[e]:
+                    call(i)
+
+            @pl.when(k == 1)
+            def _():
+                for call, i in (((hg.c, 2), (hg.b, 3)), ((hg.c, 3),), ())[e]:
+                    call(i)
+
+            if e == 1:
+
+                @pl.when(k > 0)
+                def _():
+                    for g in rgs:
+                        g.b(k - 1)
+
+        compute(lev_of(k), between, lambda: dyg.done(k))
+        for g in rgs:
+            g.a(k)
+
+        @pl.when(k > 0)
+        def _():
+            for g in rgs:
+                g.c(k - 1)
+
+        weight_grads(lev_of(k))
+
+    half = D // 2
+    other = pl.multiple_of((1 - core) * half, half)
+    mine_d = pl.multiple_of(core * half, half)
+    c_up = remote(gup.at[:, :, pl.ds(other, half)], sib_up, one_s.at[0], one_r.at[0], sib)
+    c_dn = remote(gdn.at[:, other_f, :], sib_dn, one_s.at[1], one_r.at[1], sib)
+    c_up.start()
+    c_dn.start()
 
     @pl.loop(1, S)
     def _(i):
+        to = (me + i) % S
+        remote(psc.at[to], screcv.at[i], sn_s.at[1, i], sn_r.at[1], (core, to)).start()
+
+    for g in rgs:
+        g.b(L - 1)
+    c_up.wait_recv()
+    for e in range(3):
+        tot = gup[e, :, pl.ds(mine_d, half)] + sib_up[e]
+        gup_out[e] = tot.T.astype(BF)
+        if e == 0:
+            for g in rgs:
+                g.c(L - 1)
+    screcv[0] = psc[me]
+    c_dn.wait_recv()
+    gdn0_out[...] = gdn[0, mine_f, :] + sib_dn[0]
+    for e in range(1, 3):
+        gdn12_out[e - 1] = gdn[e, mine_f, :] + sib_dn[e]
+    for k in range(1, L):
+        for g in rgs:
+            g.d(k)
+    remote(screcv.at[pl.ds(1, S - 1)], screcv.at[pl.ds(1, S - 1)], sn_s.at[1, 0], sn_r.at[1], (core, xn)).wait_recv()
+    sc_out[...] = jnp.sum(screcv[...], axis=0)
+
+    for i in range(L):
+        y_copy(i).wait()
+    c_up.wait_send()
+    c_dn.wait_send()
+    hg.finish()
+    for g in rgs:
+        g.finish()
+
+    @pl.loop(1, S)
+    def _(i):
+        remote(scall.at[me], scall.at[0], sn_s.at[0, i], sn_r.at[0], (core, xn)).wait_send()
+        remote(psc.at[0], screcv.at[0], sn_s.at[1, i], sn_r.at[1], (core, xn)).wait_send()
         remote(smallbuf.at[my], smallbuf.at[my], sm_s.at[0, i], sm_r.at[0], (core, xn)).wait_send()
         for e in range(3):
             for h in range(2):
                 up_copy(e, h, i).wait_send()
 
 
-def attn_call(x, dy, docs, es, ss, small, ws, wu, eu, wd, ed, S):
+def front_call(x, dy, docs, es, ss, small, ws, wu, eu, wd, ed, S):
     T, D = x.shape
     WR, FR = ws[0].shape[0], wd.shape[0]
-    L = S // 4
-    N = 2 * S
+    L, N, F = S // 4, 2 * S, 2 * FR
+    many = 4 * T + 8 * 80
     vm = pl.BlockSpec(memory_space=pltpu.VMEM)
     hb = pl.BlockSpec(memory_space=pl.ANY)
     V = pltpu.VMEM
@@ -876,22 +808,29 @@
     sds = jax.ShapeDtypeStruct
     row = sds((T, D), BF)
     rowf = sds((T, D), F32)
+    tokens, blocks, side = V((S, T, D), BF), V((L, T, D), BF), V((S, 8, 128), F32)
     return pl.pallas_call(
-        attn_kernel,
+        front_kernel,
         out_shape=(
-            row, sds((T, 128), F32), sds((8, T), F32), rowf, rowf, rowf, row, row, row, row,
+            sds((T, 128), F32), rowf, rowf, rowf, row, row, row, row,
             sds((D // 128, 2 * T, T), F32), row, sds((8, D), F32), sds((8, 128), F32),
-            sds((4, N, WR, D), BF), sds((S, T, D), BF), sds((3, D, 2 * FR), BF), sds((3, FR, D), BF),
+            sds((4, N, WR, D), BF), sds((S * T // WR, WR, D), BF), rowf, sds((8, 128), F32), sds((3, D // 2, F), BF),
+            sds((FR, D), F32), sds((2, FR, D), F32),
         ),
         in_specs=[vm] * 14,
-        out_specs=(vm,) * 14 + (hb,) * 4,
+        out_specs=(vm,) * 12 + (hb, hb) + (vm,) * 5,
         scratch_shapes=[
-            V((4, N, WR, D), BF), V((3, D, 2 * FR), BF), V((N, 16, 128), F32), V((T, D), BF), V((T, T), F32), V((T, D), F32), V((T, D), F32),
-            dma((3, 6, L)), dma((3, 6, L)), dma((3, max(L, 4))), dma((3, max(L, 4))), dma((2, S)), dma((2,)), dma((10,)),
+            V((4, N, WR, D), BF), V((3, D, F), BF), V((3, F, D), BF), V((N, 16, 128), F32), V((T, T), F32),
+            tokens, tokens, side, side, side, V((4, T, 128), F32), V((4, T, 128), F32), blocks, blocks, blocks, blocks,
+            V((4 * T, F), F32), V((4 * T, F), F32), V((many, F), BF), V((many, F), BF), V((many, D), BF),
+            V((4 * T, D), F32), V((4 * T, D), F32), V((4 * T, D), F32),
+            V((3, F, D), F32), V((3, F, D), F32), V((3, FR, D), F32), V((3, F, D // 2), F32),
+            dma((3, 6, L)), dma((3, 6, L)), dma((2, 4, L)), dma((2, 4, L)), dma((2, max(L, 4))), dma((2, max(L, 4))),
+            dma((2,)), dma((2,)), dma((2, S)), dma((2,)), dma((2, S)), dma((2,)), dma((L + 1,)),
         ],
-        compiler_params=pltpu.CompilerParams(collective_id=1, has_side_effects=True, vmem_limit_bytes=60000000),
-        cost_estimate=pl.CostEstimate(flops=2 * 10**9, bytes_accessed=40 * 2**20, transcendentals=2**20),
-        name="attn",
+        compiler_params=pltpu.CompilerParams(collective_id=1, has_side_effects=True, vmem_limit_bytes=66000000),
+        cost_estimate=pl.CostEstimate(flops=17 * 10**9, bytes_accessed=40 * 2**20, transcendentals=2**20),
+        name="front",
     )(x, dy, docs, es, ss, small, *ws, wu, eu, wd, ed)
 
 
@@ -1401,11 +1340,13 @@
     group = 128 // WR
     slot_of = lax.broadcasted_iota(jnp.int32, (8, 128), 1) // WR
     small = jnp.where(slot_of == dev % group, jnp.tile(small, (1, group)), 0.0)
-    (h2b, stat, scal8, u1, u2, x1, dys, q, k, v, p, o, small, count, wa, dy_all, ups, downs) = attn_call(
+    (
+        stat, u1, u2, x1, dys, q, k, v, p, o, small, count, wa, y_parts, dh2, sc, gup, gdn0, gdn12,
+    ) = front_call(
         hidden_in, out_grad, doc_ids, expert_ids.reshape(1, T), slot_ids.reshape(1, T), small,
         (w_query, w_key, w_value, w_out), w_up, expert_up, w_down, expert_down, S,
     )
-    y_parts, dh2, sc, gup, gdn0, gdn12 = ffn_call(h2b, scal8, dy_all, ups, w_down, expert_down, downs)
+    y_parts = y_parts.reshape(S, T, D)
     layer_out, input_grad, gwq, gwk, gwv, gwo, smalls, gup = back_call(
         dh2, y_parts, sc, small, stat, u1, u2, x1, dys, q, k, v, p, o,
         expert_ids.reshape(1, T), slot_ids.reshape(1, T), wa.reshape(4, D, D), gup, S,

time: 313 us -> 293 us (0.936)
  Pallas kernels: 298 us -> 278 us
    pallas_call x2 -> x1, Pallas kernels: 210 us -> 190 us  [front_call(): pl.pallas_call(front_kernel, out_shape=(sds((T, 128), F32), rowf, rowf, r...]
where the time goes in v7:
time: 293 us
  Pallas kernels  278 us (95%)
  local copies, waits for them, and re-layouts  12.1 us (4%)
    pallas_call x1, Pallas kernels, front_call(): pl.pallas_call(front_kernel, out_shape=(sds((T, 128), F32), rowf, rowf, r...  190 us
    pallas_call x1, Pallas kernels, back_call(): pl.pallas_call(back_kernel, out_shape=(sds((T, D), BF), sds((T, D), BF),...  85.8 us
    unnamed x24, local copies, waits for them, and re-layouts  8.61 us

profile of v7, /device:TPU:0, one launch (start us, length us, event | category | flops | bytes accessed | tf_op | source)
XLA Modules:
  0.0 292.8 jit_solution(9755637011942205652)
XLA Ops:
  0.7 0.7 slice_bitcast_fusion
  1.4 0.7 stack.40
  2.2 0.1 tile.10
  2.3 0.6 fusion.small_ref
  2.9 190.1 %front.1 = (f32[128,128]{1,0:T(8,128)}, f32[128,1024]{1,0:T(8,128)}, f32[128,1024]{1,0:T(8,128)}, f32[128,1024]{1,0:T(8,128)}, bf16[128,1024]{1,0:T(8,128)(2,1)}...) custom-call(bf16[128,1024]{1,0:T(8,128)(2,1)} %x_ref.1, ...), custom_call_target="tpu_custom_call" | custom-call | flops 16999999488 | bytes 41943040 | tf_op jit(solution)/shard_map/front/pallas_call | solution.py:812
  193.0 1.2 slice.35
  194.8 0.0 copy-start.10
  194.8 0.0 copy-start
  194.9 85.8 %back.1 = (bf16[128,1024]{1,0:T(8,128)(2,1)}, bf16[128,1024]{1,0:T(8,128)(2,1)}, f32[32,1024]{1,0:T(8,128)}, f32[32,1024]{1,0:T(8,128)}, f32[32,1024]{1,0:T(8,12...) custom-call(f32[128,1024]{1,0:T(8,128)} %get-tuple-element.58.dh_ref, ...), custom_call_target="tpu_custom_call" | custom-call | flops 4000000000 | bytes 20971520 | tf_op jit(solution)/shard_map/back/pallas_call | solution.py:1085
  280.7 0.0 copy-done.10
  280.7 0.6 multiply_add_fusion
  281.3 0.0 copy-done.2
  281.3 1.1 copy-done.1
  282.4 0.9 copy-done.3
  283.4 0.9 copy-done.4
  284.3 0.9 copy-done.5
  285.3 0.9 copy-done.6
  286.2 0.9 copy-done.7
  287.1 0.9 copy-done.8
  288.0 0.7 copy-done.9
  288.6 2.1 finish.1
  290.8 0.6 copy.40
  291.4 0.6 copy.41
  292.0 0.7 slice_reduce_fusion
  (13 shorter events, 0.0 us)
Async XLA Ops:
  194.8 85.9 %copy-start.10 = (f32[2]{0:T(128)S(1)}, f32[2]{0:T(128)}, u32[]{:S(2)}) copy-start(f32[2]{0:T(128)} %param.39) | copy-start | bytes 28
  194.8 86.5 %copy-start = (f32[2,128,1024]{2,1,0:T(8,128)S(1)}, f32[2,128,1024]{2,1,0:T(8,128)}, u32[]{:S(2)}) copy-start(f32[2,128,1024]{2,1,0:T(8,128)} %get-tuple-element.83.gdn12_ref) | copy-start | bytes 3145732
  194.9 86.5 %copy-start.2 = (f32[128,1024]{1,0:T(8,128)S(1)}, f32[128,1024]{1,0:T(8,128)}, u32[]{:S(2)}) copy-start(f32[128,1024]{1,0:T(8,128)} %get-tuple-element.82.gdn0_ref) | copy-start | bytes 1572868
  281.3 1.1 copy-start.1
  282.4 0.9 copy-start.3
  283.4 0.9 copy-start.4
  284.3 0.9 copy-start.5
  285.2 0.9 copy-start.6
  286.2 0.9 copy-start.7
  287.1 0.9 copy-start.8
  288.0 0.7 copy-start.9

commit v8 on v7

--- a/solution.py
+++ b/solution.py
@@ -205,6 +205,17 @@
     return Stages
 
 
+def together(*machines):
+    class Stages:
+        pass
+
+    for name in vars(machines[0]):
+        if not name.startswith("_"):
+            calls = [getattr(mach, name) for mach in machines]
+            setattr(Stages, name, staticmethod(lambda *a, calls=calls: [call(*a) for call in calls] and None))
+    return Stages
+
+
 def tree_scatter(part, ra, rbx, rby, rd, final, ss, rs, dev, levels, rz=None):
     core, z, p, xq, yq, dq = dev
     xn, yn = z * 4 + xq, z * 4 + yq
@@ -356,8 +367,8 @@
     wu_ref, eu_ref, wd_ref, ed_ref,
     stat_out, u1_out, u2_out, x1_out, dys_out, q_out, k_out, v_out, p_out, o_out,
     small_out, count_out, w_out, y_out, dh_out, sc_out, gup_out, gdn0_out, gdn12_out,
-    wbuf, up_ref, dn_ref, smallbuf, bias, dy_all, hall, scall, psc, screcv, wcol, scol, ra, rbx, rby, rd,
-    pre, der, ub, dg, dm, m, yacc, dxacc, gdn, gup, sib_dn, sib_up,
+    wbuf, up_ref, dn_ref, smallbuf, h1b, bias, tmp, xs, dy_all, hall, dxp, scall, psc, screcv, wcol, scol, ra, rbx, rby, rd,
+    pre, dyw, uw, dg, gdn, gup, sib_dn, sib_up,
     ag_s, ag_r, rs_s, rs_r, sib_s, sib_r, one_s, one_r, sm_s, sm_r, sn_s, sn_r, loc,
 ):
     T, D = x_ref.shape
@@ -375,13 +386,15 @@
 
     dev, levels = (core, z, p, xq, yq, dq), (lev_of, L)
 
-    def w_at(i):
-        return wbuf.at[:, core * S + i]
-
-    wg = tree_gather(w_at, w_at(me), ag_s.at[0], ag_r.at[0], dev, levels)
-    dyg = tree_gather(lambda i: dy_all.at[i], dys_out, ag_s.at[1], ag_r.at[1], dev, levels)
-    hg = tree_gather(lambda i: hall.at[i], hall.at[me], ag_s.at[2], ag_r.at[2], dev, levels)
-    tmp, xs, h1b = m.at[pl.ds(0, T)], yacc.at[pl.ds(0, T)], dm.at[pl.ds(0, T)]
+    def split(at, j):
+        return tree_gather(at, at(me), ag_s.at[j], ag_r.at[j], dev, levels)
+
+    def rows_of(ref, j):
+        return lambda i: ref.at[i, pl.ds(j * (T // 2), T // 2)]
+
+    wg = together(*(split(lambda i, j=j: wbuf.at[pl.ds(2 * j, 2), core * S + i], j) for j in range(2)))
+    dyg = together(*(split(rows_of(dy_all, j), 2 + j) for j in range(2)))
+    hg = together(*(split(rows_of(hall, j), 4 + j) for j in range(2)))
 
     for i, w in enumerate((wq_ref, wk_ref, wv_ref, wo_ref)):
         wbuf[i, my] = w[...]
@@ -453,7 +466,7 @@
         src = wu_ref if e == 0 else eu_ref.at[e - 1]
         return remote(
             src.at[:, pl.ds(pl.multiple_of((h * S + to) * FR, FR), FR)],
-            up_ref.at[e, pl.ds(pl.multiple_of(my * WR, WR), WR), pl.ds(h * FR, FR)],
+            up_ref.at[pl.ds(pl.multiple_of(my * WR, WR), WR), pl.ds(e * F + h * FR, FR)],
             sm_s.at[1, i], sm_r.at[1], (core, to),
         )
 
@@ -467,7 +480,7 @@
         for h in range(2):
             src = wu_ref if e == 0 else eu_ref.at[e - 1]
             block = src[:, pl.ds(pl.multiple_of((h * S + me) * FR, FR), FR)]
-            up_ref[e, pl.ds(pl.multiple_of(my * WR, WR), WR), h * FR : (h + 1) * FR] = block
+            up_ref[pl.ds(pl.multiple_of(my * WR, WR), WR), e * F + h * FR : e * F + (h + 1) * FR] = block
 
     def w_sib(lev, who):
         b = wbuf.at[:, pl.ds(who * S + lev * 4, 4)]
@@ -588,9 +601,9 @@
         remote(scall.at[me], scall.at[me], sn_s.at[0, i], sn_r.at[0], (core, (me + i) % S)).start()
 
     dyg.c(3)
-    got = up_ref.at[:, pl.ds(0, (S - 1) * WR), :]
+    got = up_ref.at[pl.ds(0, (S - 1) * WR), :]
     remote(got, got, sm_s.at[1, 0], sm_r.at[1], (core, xn)).wait_recv()
-    mine_up = up_ref.at[:, pl.ds(pl.multiple_of(core * S * WR, S * WR), S * WR), :]
+    mine_up = up_ref.at[pl.ds(pl.multiple_of(core * S * WR, S * WR), S * WR), :]
     c_slice = remote(mine_up, mine_up, sib_s.at[1, 3], sib_r.at[1, 3], sib)
     c_slice.start()
     end = (z == 0) | (z == L - 1)
@@ -615,96 +628,64 @@
     rgs = []
     for i in range(2):
         t = pl.ds(i * (T // 2), T // 2)
-        bufs = [b.at[:, t, :] for b in (dy_all, ra, rbx, rby, rd)]
+        bufs = [b.at[:, t, :] for b in (dxp, ra, rbx, rby, rd)]
         rgs.append(tree_scatter(*bufs, dh_out.at[t], rs_s.at[i], rs_r.at[i], dev, levels))
     LO = 80
     HI = T - LO
     per = T // WR
     fold = N // (4 * per)
 
-    size = (4 * T, 4 * LO, 4 * LO)
-    first = (0, 4 * T, 4 * T + 4 * LO)
-
     def y_copy(lev):
         src = wbuf.at[lev // fold, pl.ds(lev % fold * (4 * per), 4 * per)]
         return pltpu.make_async_copy(src, y_out.at[pl.ds(lev * (4 * per), 4 * per)], loc.at[lev])
 
-    def compute(lev, between, settle):
+    def compute(lev, between):
         base = lev * 4
+        level = pl.ds(base, 4)
         for q in range(4):
             full = jnp.concatenate([scall[base + q], jnp.zeros((120, 128), F32)], axis=0)
             wcol[q] = full.T
-        for e in range(3):
-            n = LO if e else T
-            off = HI if e == 2 else 0
-            rows, at0 = size[e], first[e]
-            here = slice(at0, at0 + rows)
-            hm = hall[pl.ds(base, 4), off : off + n, :].reshape(rows, D)
-            pre[0:rows, :] = mm(hm, up_ref[e])
-
-            def act(r):
-                t = pl.ds(r, rows // 4)
-                val, d = gelu_pair(pre[t, :])
-                ub[pl.ds(pl.multiple_of(at0 + r, 16), rows // 4), :] = val.astype(BF)
-                der[t, :] = d
-
-            rows_loop(rows, rows // 4, act)
-            m[0:rows, :] = mm(ub[here, :], dn_ref[e])
-            step = n if e else T // 2
-            lane = lax.broadcasted_iota(jnp.int32, (step, 128), 1)
-            for q in range(4):
-
-                def elem(r):
-                    at = pl.ds(pl.multiple_of(r + off, 16), step)
-                    mine = pl.ds(pl.multiple_of(q * n + r, 16), step)
-                    keep = pl.ds(pl.multiple_of(at0 + q * n + r, 16), step)
-                    t = pl.ds(pl.multiple_of(q * T + off + r, 16), step)
-                    w = wcol[q, at, :][:, e : e + 1]
-                    dyv = dy_all[base + q, at, :].astype(F32)
-                    mv = m[mine, :]
-                    s = jnp.sum(dyv * mv, axis=1, keepdims=True)
-                    s = jnp.where(lane == e, s, 0.0)
-                    dm[keep, :] = (dyv * w).astype(BF)
-                    if e:
-                        yacc[t, :] = yacc[t, :] + mv * w
-                        scol[q, at, :] = scol[q, at, :] + s
-                    else:
-                        yacc[t, :] = mv * w
-                        scol[q, at, :] = s
-
-                rows_loop(n, step, elem)
-            pre[0:rows, :] = mm(dm[here, :], dn_ref[e], ((1,), (1,)))
-
-            def back(r):
-                t = pl.ds(r, rows // 4)
-                dg[pl.ds(pl.multiple_of(at0 + r, 16), rows // 4), :] = (pre[t, :] * der[t, :]).astype(BF)
-
-            rows_loop(rows, rows // 4, back)
-            if e:
-                m[0:rows, :] = mm(dg[here, :], up_ref[e], ((1,), (1,)))
-                for q in range(4):
-                    t = slice(q * T + off, q * T + off + n)
-                    dxacc[t, :] = dxacc[t, :] + m[q * n : q * n + n, :]
-            else:
-                dxacc[...] = mm(dg[here, :], up_ref[0], ((1,), (1,)))
-            between(e)
-        settle()
-        for q in range(4):
-            psc[base + q] = scol[q].T[0:8, :]
-            t = slice(q * T, q * T + T)
-            dy_all[base + q] = dxacc[t, :].astype(BF)
-            here = pl.ds(lev % fold * (4 * per) + q * per, per)
-            wbuf[lev // fold, here] = yacc[t, :].astype(BF).reshape(per, WR, D)
+        pre[...] = mm(hall[level].reshape(4 * T, D), up_ref[...])
+        between(0)
+        dyw[...] = mm(dy_all[level].reshape(4 * T, D), dn_ref[...].reshape(3 * F, D), ((1,), (1,)))
+        lane = lax.broadcasted_iota(jnp.int32, (T, 128), 1)
+
+        @pl.loop(0, 4)
+        def _(q):
+            t = pl.ds(pl.multiple_of(q * T, T), T)
+            score = jnp.zeros((T, 128), F32)
+            for e in range(3):
+                cols = slice(e * F, (e + 1) * F)
+                val, der = gelu_pair(pre[t, cols])
+                low = val.astype(BF).astype(F32)
+                back = dyw[t, cols]
+                w = wcol[q][:, e : e + 1]
+                score = score + jnp.where(lane == e, jnp.sum(low * back, axis=1, keepdims=True), 0.0)
+                uw[t, cols] = (low * w).astype(BF)
+                dg[t, cols] = (back * w * der).astype(BF)
+            psc[base + q] = score.T[0:8, :]
+
+        between(1)
+        dxp[level] = mm(dg[...], up_ref[...], ((1,), (1,))).astype(BF).reshape(4, T, D)
+        y = mm(uw[...], dn_ref[...].reshape(3 * F, D)).astype(BF)
+        wbuf[lev // fold, pl.ds(lev % fold * (4 * per), 4 * per)] = y.reshape(4 * per, WR, D)
         y_copy(lev).start()
+        between(2)
 
     def weight_grads(lev):
         for e in range(3):
             n = LO if e else T
             off = HI if e == 2 else 0
-            here = slice(first[e], first[e] + size[e])
-            hm = hall[pl.ds(lev * 4, 4), off : off + n, :].reshape(size[e], D)
-            gdn[e] = gdn[e] + mm(ub[here, :], dm[here, :], ((0,), (0,)))
-            gup[e] = gup[e] + mm(dg[here, :], hm, ((0,), (0,)))
+            level = pl.ds(lev * 4, 4)
+
+            def some(a):
+                a = a[:, e * F : (e + 1) * F]
+                return a.reshape(4, T, F)[:, off : off + n].reshape(4 * n, F)
+
+            hm = hall[level, off : off + n, :].reshape(4 * n, D)
+            dyb = dy_all[level, off : off + n, :].reshape(4 * n, D)
+            gdn[e] = gdn[e] + mm(some(uw), dyb, ((0,), (0,)))
+            gup[e] = gup[e] + mm(some(dg), hm, ((0,), (0,)))
 
     def far_a(i):
         pl.when(end)(lambda: hg.a(i))
@@ -734,7 +715,7 @@
                     for g in rgs:
                         g.b(k - 1)
 
-        compute(lev_of(k), between, lambda: dyg.done(k))
+        compute(lev_of(k), between)
         for g in rgs:
             g.a(k)
 
@@ -783,6 +764,7 @@
     c_up.wait_send()
     c_dn.wait_send()
     hg.finish()
+    dyg.finish()
     for g in rgs:
         g.finish()
 
@@ -800,7 +782,6 @@
     T, D = x.shape
     WR, FR = ws[0].shape[0], wd.shape[0]
     L, N, F = S // 4, 2 * S, 2 * FR
-    many = 4 * T + 8 * 80
     vm = pl.BlockSpec(memory_space=pltpu.VMEM)
     hb = pl.BlockSpec(memory_space=pl.ANY)
     V = pltpu.VMEM
@@ -820,12 +801,11 @@
         in_specs=[vm] * 14,
         out_specs=(vm,) * 12 + (hb, hb) + (vm,) * 5,
         scratch_shapes=[
-            V((4, N, WR, D), BF), V((3, D, F), BF), V((3, F, D), BF), V((N, 16, 128), F32), V((T, T), F32),
-            tokens, tokens, side, side, side, V((4, T, 128), F32), V((4, T, 128), F32), blocks, blocks, blocks, blocks,
-            V((4 * T, F), F32), V((4 * T, F), F32), V((many, F), BF), V((many, F), BF), V((many, D), BF),
-            V((4 * T, D), F32), V((4 * T, D), F32), V((4 * T, D), F32),
+            V((4, N, WR, D), BF), V((D, 3 * F), BF), V((3, F, D), BF), V((N, 16, 128), F32), V((T, D), BF), V((T, T), F32),
+            V((T, D), F32), V((T, D), F32), tokens, tokens, tokens, side, side, side, V((4, T, 128), F32), V((4, T, 128), F32), blocks, blocks, blocks, blocks,
+            V((4 * T, 3 * F), F32), V((4 * T, 3 * F), F32), V((4 * T, 3 * F), BF), V((4 * T, 3 * F), BF),
             V((3, F, D), F32), V((3, F, D), F32), V((3, FR, D), F32), V((3, F, D // 2), F32),
-            dma((3, 6, L)), dma((3, 6, L)), dma((2, 4, L)), dma((2, 4, L)), dma((2, max(L, 4))), dma((2, max(L, 4))),
+            dma((6, 6, L)), dma((6, 6, L)), dma((2, 4, L)), dma((2, 4, L)), dma((2, max(L, 4))), dma((2, max(L, 4))),
             dma((2,)), dma((2,)), dma((2, S)), dma((2,)), dma((2, S)), dma((2,)), dma((L + 1,)),
         ],
         compiler_params=pltpu.CompilerParams(collective_id=1, has_side_effects=True, vmem_limit_bytes=66000000),
@@ -1112,19 +1092,22 @@
 
 
 def finish_kernel(
-    lo_ref, ig_ref, gq_ref, gk_ref, gv_ref, go_ref, sm_ref, gup_ref, gdn0_ref, gdn12_ref,
+    lo_hbm, ig_hbm, gq_hbm, gk_hbm, gv_hbm, go_hbm, sm_hbm, gup_hbm, gdn0_hbm, gdn12_hbm,
     lo_out, ig_out, q_out, k_out, v_out, o_out, up_out, dn_out, eu_out, ed_out, r_out, m_out, n_out,
-    turned,
+    sm_ref, gup_ref, turned, sems,
 ):
+    pairs = (
+        (gup_hbm, gup_ref), (sm_hbm, sm_ref), (lo_hbm, lo_out), (ig_hbm, ig_out), (gq_hbm, q_out), (gk_hbm, k_out),
+        (gv_hbm, v_out), (go_hbm, o_out), (gdn0_hbm, dn_out), (gdn12_hbm, ed_out),
+    )
+    copies = [pltpu.make_async_copy(a, b, sems.at[i]) for i, (a, b) in enumerate(pairs)]
+    for c in copies:
+        c.start()
+    copies[0].wait()
+    copies[1].wait()
     S, _, WR, F = gup_ref.shape
     FR = F // 2
     at = (lax.axis_index("dp") * S + lax.axis_index("shard")) % (128 // WR) * WR
-    lo_out[...] = lo_ref[...]
-    ig_out[...] = ig_ref[...]
-    for src, out in ((gq_ref, q_out), (gk_ref, k_out), (gv_ref, v_out), (go_ref, o_out)):
-        out[...] = src[...]
-    dn_out[...] = gdn0_ref[...]
-    ed_out[...] = gdn12_ref[...]
     for s in range(S):
         for c in range(2):
             cols = slice((c * S + s) * FR, (c * S + s + 1) * FR)
@@ -1137,6 +1120,8 @@
     r_out[...] = mine[:, 4:6]
     m_out[...] = mine[:, 6:8]
     n_out[...] = mine[:, 0:4]
+    for c in copies[2:]:
+        c.wait()
 
 
 def finish_call(lo, ig, gwq, gwk, gwv, gwo, smalls, gup, gdn0, gdn12):
@@ -1152,10 +1137,12 @@
             sds((T, D), BF), sds((T, D), BF), sq, sq, sq, sq, sds((WR, FF), F32), sds(gdn0.shape, F32),
             sds((2, WR, FF), F32), sds(gdn12.shape, F32), sds((WR, 2), F32), sds((WR, 2), F32), sds((WR, 4), F32),
         ),
-        in_specs=[vm] * 10,
+        in_specs=[pl.BlockSpec(memory_space=pl.ANY)] * 10,
         out_specs=(vm,) * 13,
-        scratch_shapes=[pltpu.VMEM((128, 128), F32)],
-        compiler_params=pltpu.CompilerParams(vmem_limit_bytes=40000000),
+        scratch_shapes=[
+            pltpu.VMEM(smalls.shape, F32), pltpu.VMEM(gup.shape, BF), pltpu.VMEM((128, 128), F32), pltpu.SemaphoreType.DMA((10,)),
+        ],
+        compiler_params=pltpu.CompilerParams(vmem_limit_bytes=66000000),
         name="finish",
     )(lo, ig, gwq, gwk, gwv, gwo, smalls, gup, gdn0, gdn12)
 

time: 293 us -> 288 us (0.983)
  local copies, waits for them, and re-layouts: 12.1 us -> 7.08 us
    pallas_call x1, Pallas kernels: 190 us -> 183 us  [front_call(): pl.pallas_call(front_kernel, out_shape=(sds((T, 128), F32), rowf, rowf, r...]
    unnamed x24 -> x4, local copies, waits for them, and re-layouts: 8.61 us -> 2.71 us
    pallas_call x1, Pallas kernels: 85.8 us -> 91.3 us  [back_call(): pl.pallas_call(back_kernel, out_shape=(sds((T, D), BF), sds((T, D), BF),...]
where the time goes in v8:
time: 288 us
  Pallas kernels  278 us (97%)
  local copies, waits for them, and re-layouts  7.08 us (2%)
    pallas_call x1, Pallas kernels, front_call(): pl.pallas_call(front_kernel, out_shape=(sds((T, 128), F32), rowf, rowf, r...  183 us
    pallas_call x1, Pallas kernels, back_call(): pl.pallas_call(back_kernel, out_shape=(sds((T, D), BF), sds((T, D), BF),...  91.3 us

profile of v8, /device:TPU:0, one launch (start us, length us, event | category | flops | bytes accessed | tf_op | source)
XLA Modules:
  0.0 287.8 jit_solution(8549085360481294653)
XLA Ops:
  0.7 0.7 slice_bitcast_fusion
  1.4 0.7 stack.40
  2.2 0.1 tile.10
  2.3 0.6 fusion.small_ref
  2.9 182.8 %front.1 = (f32[128,128]{1,0:T(8,128)}, f32[128,1024]{1,0:T(8,128)}, f32[128,1024]{1,0:T(8,128)}, f32[128,1024]{1,0:T(8,128)}, bf16[128,1024]{1,0:T(8,128)(2,1)}...) custom-call(bf16[128,1024]{1,0:T(8,128)(2,1)} %x_ref.1, ...), custom_call_target="tpu_custom_call" | custom-call | flops 16999999488 | bytes 41943040 | tf_op jit(solution)/shard_map/front/pallas_call | solution.py:793
  185.7 1.2 slice.35
  187.5 0.0 copy-start
  187.6 91.3 %back.1 = (bf16[128,1024]{1,0:T(8,128)(2,1)}, bf16[128,1024]{1,0:T(8,128)(2,1)}, f32[32,1024]{1,0:T(8,128)}, f32[32,1024]{1,0:T(8,128)}, f32[32,1024]{1,0:T(8,12...) custom-call(f32[128,1024]{1,0:T(8,128)} %get-tuple-element.58.dh_ref, ...), custom_call_target="tpu_custom_call" | custom-call | flops 4000000000 | bytes 20971520 | tf_op jit(solution)/shard_map/back/pallas_call | solution.py:1065
  278.8 0.0 copy-done
  278.8 0.6 multiply_add_fusion
  279.4 4.0 %finish.1 = (bf16[128,1024]{1,0:T(8,128)(2,1)}, bf16[128,1024]{1,0:T(8,128)(2,1)}, f32[32,1024]{1,0:T(8,128)}, f32[32,1024]{1,0:T(8,128)}, f32[32,1024]{1,0:T(8,...) custom-call(bf16[128,1024]{1,0:T(8,128)(2,1)} %get-tuple-element.74., ...), custom_call_target="tpu_custom_call" | custom-call | tf_op jit(solution)/shard_map/finish/pallas_call | solution.py:1134
  283.5 1.4 copy.40
  284.8 1.4 copy.41
  286.2 1.6 slice_reduce_fusion
  (3 shorter events, 0.0 us)
Async XLA Ops:
  187.5 91.3 %copy-start = (f32[2]{0:T(128)S(1)}, f32[2]{0:T(128)}, u32[]{:S(2)}) copy-start(f32[2]{0:T(128)} %param.39) | copy-start | bytes 28

commit v9 on v8

--- a/solution.py
+++ b/solution.py
@@ -1092,9 +1092,9 @@
 
 
 def finish_kernel(
-    lo_hbm, ig_hbm, gq_hbm, gk_hbm, gv_hbm, go_hbm, sm_hbm, gup_hbm, gdn0_hbm, gdn12_hbm,
-    lo_out, ig_out, q_out, k_out, v_out, o_out, up_out, dn_out, eu_out, ed_out, r_out, m_out, n_out,
-    sm_ref, gup_ref, turned, sems,
+    lo_hbm, ig_hbm, gq_hbm, gk_hbm, gv_hbm, go_hbm, sm_hbm, gup_hbm, gdn0_hbm, gdn12_hbm, count_ref, load_ref,
+    lo_out, ig_out, q_out, k_out, v_out, o_out, up_out, dn_out, eu_out, ed_out, r_out, m_out, n0_out, n1_out, n2_out, n3_out, cnt_out, load_out,
+    sm_ref, gup_ref, sems,
 ):
     pairs = (
         (gup_hbm, gup_ref), (sm_hbm, sm_ref), (lo_hbm, lo_out), (ig_hbm, ig_out), (gq_hbm, q_out), (gk_hbm, k_out),
@@ -1107,7 +1107,12 @@
     copies[1].wait()
     S, _, WR, F = gup_ref.shape
     FR = F // 2
-    at = (lax.axis_index("dp") * S + lax.axis_index("shard")) % (128 // WR) * WR
+    slot = (lax.axis_index("dp") * S + lax.axis_index("shard")) % (128 // WR)
+    tokens = lo_out.shape[0] * 2 * S
+    zeros = count_ref[0, 0].astype(jnp.int32)
+    for i, n in enumerate((zeros, tokens - zeros)):
+        cnt_out[i] = n
+        load_out[i] = 0.9 * load_ref[i] + 0.1 * n.astype(F32) * 2 / tokens
     for s in range(S):
         for c in range(2):
             cols = slice((c * S + s) * FR, (c * S + s + 1) * FR)
@@ -1115,19 +1120,22 @@
             up_out[:, cols] = gup_ref[s, 0, :, part].astype(F32)
             for e in range(2):
                 eu_out[e, :, cols] = gup_ref[s, 1 + e, :, part].astype(F32)
-    turned[...] = jnp.concatenate([sm_ref[...], jnp.zeros((120, 128), F32)], axis=0).T
-    mine = turned[pl.ds(pl.multiple_of(at, WR), WR), :]
-    r_out[...] = mine[:, 4:6]
-    m_out[...] = mine[:, 6:8]
-    n_out[...] = mine[:, 0:4]
+    mine = sm_ref[:, 0:WR]
+    for j in range(1, 128 // WR):
+        mine = jnp.where(slot == j, sm_ref[:, j * WR : (j + 1) * WR], mine)
+    for i, out in enumerate((n0_out, n1_out, n2_out, n3_out)):
+        out[...] = mine[i, :]
+    r_out[...] = mine[4:6, :]
+    m_out[...] = mine[6:8, :]
     for c in copies[2:]:
         c.wait()
 
 
-def finish_call(lo, ig, gwq, gwk, gwv, gwo, smalls, gup, gdn0, gdn12):
+def finish_call(lo, ig, gwq, gwk, gwv, gwo, smalls, gup, gdn0, gdn12, count, load):
     T, D = lo.shape
     S, _, WR, F = gup.shape
     FF = S * F
+    sm = pl.BlockSpec(memory_space=pltpu.SMEM)
     vm = pl.BlockSpec(memory_space=pltpu.VMEM)
     sds = jax.ShapeDtypeStruct
     sq = sds((WR, D), F32)
@@ -1135,16 +1143,17 @@
         finish_kernel,
         out_shape=(
             sds((T, D), BF), sds((T, D), BF), sq, sq, sq, sq, sds((WR, FF), F32), sds(gdn0.shape, F32),
-            sds((2, WR, FF), F32), sds(gdn12.shape, F32), sds((WR, 2), F32), sds((WR, 2), F32), sds((WR, 4), F32),
+            sds((2, WR, FF), F32), sds(gdn12.shape, F32), sds((2, WR), F32), sds((2, WR), F32),
+            *[sds((WR,), F32)] * 4, sds((2,), jnp.int32), sds((2,), F32),
         ),
-        in_specs=[pl.BlockSpec(memory_space=pl.ANY)] * 10,
-        out_specs=(vm,) * 13,
+        in_specs=[pl.BlockSpec(memory_space=pl.ANY)] * 10 + [sm, sm],
+        out_specs=(vm,) * 16 + (sm, sm),
         scratch_shapes=[
-            pltpu.VMEM(smalls.shape, F32), pltpu.VMEM(gup.shape, BF), pltpu.VMEM((128, 128), F32), pltpu.SemaphoreType.DMA((10,)),
+            pltpu.VMEM(smalls.shape, F32), pltpu.VMEM(gup.shape, BF), pltpu.SemaphoreType.DMA((10,)),
         ],
         compiler_params=pltpu.CompilerParams(vmem_limit_bytes=66000000),
         name="finish",
-    )(lo, ig, gwq, gwk, gwv, gwo, smalls, gup, gdn0, gdn12)
+    )(lo, ig, gwq, gwk, gwv, gwo, smalls, gup, gdn0, gdn12, count, load)
 
 
 def body_plain(
@@ -1319,7 +1328,6 @@
     FR = w_down.shape[0]
     F = FR * C
     E = expert_up.shape[0]
-    ndev = C * S
     dev = lax.axis_index(BOTH)
     small = jnp.stack(
         [ln1_gain, ln1_bias, ln2_gain, ln2_bias, w_router[:, 0], w_router[:, 1], w_mix[:, 0], w_mix[:, 1]]
@@ -1338,15 +1346,11 @@
         dh2, y_parts, sc, small, stat, u1, u2, x1, dys, q, k, v, p, o,
         expert_ids.reshape(1, T), slot_ids.reshape(1, T), wa.reshape(4, D, D), gup, S,
     )
-    lo, ig, gq, gk, gv, go, gu, gd, geu, ged, gr, gm, gn = finish_call(
-        layer_out, input_grad, gwq, gwk, gwv, gwo, smalls, gup, gdn0, gdn12
+    lo, ig, gq, gk, gv, go, gu, gd, geu, ged, gr, gm, n0, n1, n2, n3, counts, load_new = finish_call(
+        layer_out, input_grad, gwq, gwk, gwv, gwo, smalls, gup, gdn0, gdn12, count, load_avg
     )
-    tokens0 = count[0, 0].astype(jnp.int32)
-    counts = jnp.stack([tokens0, T * ndev - tokens0])
-    load_new = 0.9 * load_avg + 0.1 * counts.astype(F32) * E / (T * ndev)
     return (
-        lo, ig, gn[:, 0], gn[:, 1], gq, gk, gv, go, gn[:, 2], gn[:, 3],
-        gu, gd, gr, gm, geu, ged, counts, load_new,
+        lo, ig, n0, n1, gq, gk, gv, go, n2, n3, gu, gd, gr.T, gm.T, geu, ged, counts, load_new,
     )
 
 

time: 288 us -> 282 us (0.979)
  local copies, waits for them, and re-layouts: 7.08 us -> 1.56 us
where the time goes in v9:
time: 282 us
  Pallas kernels  279 us (99%)
    pallas_call x1, Pallas kernels, front_call(): pl.pallas_call(front_kernel, out_shape=(sds((T, 128), F32), rowf, rowf, r...  183 us
    pallas_call x1, Pallas kernels, back_call(): pl.pallas_call(back_kernel, out_shape=(sds((T, D), BF), sds((T, D), BF),...  91.4 us

profile of v9, /device:TPU:0, one launch (start us, length us, event | category | flops | bytes accessed | tf_op | source)
XLA Modules:
  0.0 282.1 jit_solution(15280392817445767847)
XLA Ops:
  0.7 0.7 slice_bitcast_fusion
  1.4 0.7 stack.31
  2.2 0.1 tile.10
  2.3 0.6 fusion.small_ref
  2.9 182.9 %front.1 = (f32[128,128]{1,0:T(8,128)}, f32[128,1024]{1,0:T(8,128)}, f32[128,1024]{1,0:T(8,128)}, f32[128,1024]{1,0:T(8,128)}, bf16[128,1024]{1,0:T(8,128)(2,1)}...) custom-call(bf16[128,1024]{1,0:T(8,128)(2,1)} %x_ref.1, ...), custom_call_target="tpu_custom_call" | custom-call | flops 16999999488 | bytes 41943040 | tf_op jit(solution)/shard_map/front/pallas_call | solution.py:793
  185.7 91.4 %back.1 = (bf16[128,1024]{1,0:T(8,128)(2,1)}, bf16[128,1024]{1,0:T(8,128)(2,1)}, f32[32,1024]{1,0:T(8,128)}, f32[32,1024]{1,0:T(8,128)}, f32[32,1024]{1,0:T(8,12...) custom-call(f32[128,1024]{1,0:T(8,128)} %get-tuple-element.63.dh_ref, ...), custom_call_target="tpu_custom_call" | custom-call | flops 4000000000 | bytes 20971520 | tf_op jit(solution)/shard_map/back/pallas_call | solution.py:1065
  277.1 4.8 %finish.1 = (bf16[128,1024]{1,0:T(8,128)(2,1)}, bf16[128,1024]{1,0:T(8,128)(2,1)}, f32[32,1024]{1,0:T(8,128)}, f32[32,1024]{1,0:T(8,128)}, f32[32,1024]{1,0:T(8,...) custom-call(bf16[128,1024]{1,0:T(8,128)(2,1)} %get-tuple-element.79., ...), custom_call_target="tpu_custom_call" | custom-call | tf_op jit(solution)/shard_map/finish/pallas_call | solution.py:1142
  (3 shorter events, 0.0 us)

commit v10 on v9

--- a/solution.py
+++ b/solution.py
@@ -492,9 +492,9 @@
 
     pass_on(0)
     wg.b(2)
+    dyg.start()
     wg.c(1)
     wg.b(3)
-    dyg.start()
     pass_on(1)
     wg.c(2)
     pass_on(2)

time: 282 us -> 276 us (0.979)
  Pallas kernels: 279 us -> 272 us
    pallas_call x1, Pallas kernels: 91.4 us -> 86.2 us  [back_call(): pl.pallas_call(back_kernel, out_shape=(sds((T, D), BF), sds((T, D), BF),...]
where the time goes in v10:
time: 276 us; the launch traced here: 275 us
  Pallas kernels  272 us (99%)
    pallas_call x1, Pallas kernels, front_call(): pl.pallas_call(front_kernel, out_shape=(sds((T, 128), F32), rowf, rowf, r...  181 us
    pallas_call x1, Pallas kernels, back_call(): pl.pallas_call(back_kernel, out_shape=(sds((T, D), BF), sds((T, D), BF),...  86.2 us

profile of v10, /device:TPU:0, one launch (start us, length us, event | category | flops | bytes accessed | tf_op | source)
XLA Modules:
  0.0 275.4 jit_solution(13456166270169966734)
XLA Ops:
  0.7 0.7 slice_bitcast_fusion
  1.4 0.7 stack.31
  2.2 0.1 tile.10
  2.3 0.6 fusion.small_ref
  2.9 181.4 %front.1 = (f32[128,128]{1,0:T(8,128)}, f32[128,1024]{1,0:T(8,128)}, f32[128,1024]{1,0:T(8,128)}, f32[128,1024]{1,0:T(8,128)}, bf16[128,1024]{1,0:T(8,128)(2,1)}...) custom-call(bf16[128,1024]{1,0:T(8,128)(2,1)} %x_ref.1, ...), custom_call_target="tpu_custom_call" | custom-call | flops 16999999488 | bytes 41943040 | tf_op jit(solution)/shard_map/front/pallas_call | solution.py:793
  184.3 86.2 %back.1 = (bf16[128,1024]{1,0:T(8,128)(2,1)}, bf16[128,1024]{1,0:T(8,128)(2,1)}, f32[32,1024]{1,0:T(8,128)}, f32[32,1024]{1,0:T(8,128)}, f32[32,1024]{1,0:T(8,12...) custom-call(f32[128,1024]{1,0:T(8,128)} %get-tuple-element.63.dh_ref, ...), custom_call_target="tpu_custom_call" | custom-call | flops 4000000000 | bytes 20971520 | tf_op jit(solution)/shard_map/back/pallas_call | solution.py:1065
  270.4 4.8 %finish.1 = (bf16[128,1024]{1,0:T(8,128)(2,1)}, bf16[128,1024]{1,0:T(8,128)(2,1)}, f32[32,1024]{1,0:T(8,128)}, f32[32,1024]{1,0:T(8,128)}, f32[32,1024]{1,0:T(8,...) custom-call(bf16[128,1024]{1,0:T(8,128)(2,1)} %get-tuple-element.79., ...), custom_call_target="tpu_custom_call" | custom-call | tf_op jit(solution)/shard_map/finish/pallas_call | solution.py:1142
  (3 shorter events, 0.0 us)
